TPU v7x, 128 devices: a whole 4x4x4 slice. The times are simulated.
128 devices in a mesh: slave: 16 (over y, z), master: 8 (over x, core).
Axes of the slice: x: 4, y: 4, z: 4, core: 2. Of those that a mesh axis runs over, the one named last changes fastest.
Arguments:
- slave_basis: bfloat16 [256, 128, 128], P('slave'), may hold values from -1.5 to 1.5
- master_basis: bfloat16 [512, 128, 128], P(('slave', 'master')), may hold values from -1.5 to 1.5
- slave_gap: float32 [256, 128], P('slave'), may hold values from -6 to 6
- master_disp: float32 [512, 128], P(('slave', 'master')), may hold values from -6 to 6
- pressure: float32 [256, 128], P('slave'), may hold values from -6 to 6
- active: int32 [256, 128], P('slave'), may hold values 0 or 1
- need_owner: int32 [16384, 1], P(('slave', 'master')), may hold values from 0 to 127; in each aligned block of 128 rows (0 to 127, 128 to 255, ...) at most 2 rows name the same one
- need_slot: int32 [16384], P(('slave', 'master')), may hold values from 0 to 3
- pair_need: int32 [65536], P(('slave', 'master')), may hold values from 0 to 127
- pair_slave: int32 [65536], P(('slave', 'master')), may hold values from 0 to 15
- pair_segs: int32 [65536], P(('slave', 'master')), may hold values from 1 to 8
- pair_weight: float32 [65536, 128], P(('slave', 'master')), may hold values from 0.05 to 0.5
Outputs:
- pressure_out: float32 [256, 128], P('slave')
- disp_out: float32 [512, 128], P(('slave', 'master'))
- tile_out: bfloat16 [65536, 128, 128], P(('slave', 'master'))
Inputs may be any that keep to these rules, and one draw needn't show every extreme that they name: `need_owner`: among the 128 requests of one device no owner is named more than 2 times, a bound that some block reaches.
All inputs are finite; a program needn't handle non-finite values. No bound on the sum of `active` on one device may be relied on, other than what follows from the above.
Results may differ from a plain program's by a relative error of at most 0.0049.
Values may be sent and summed in bfloat16 or wider, within the bound.
A program may use at most 128 MiB of HBM per device.

v0:
```python
import jax
import jax.numpy as jnp
from jax import lax
from jax.sharding import PartitionSpec as P

GAUSS = 16
ITERS = 2


def blockwise(function, arrays):
    shaped = tuple((a.reshape((-1, 128) + a.shape[1:]) for a in arrays))
    result = lax.map(function, shaped)
    return result.reshape((-1,) + result.shape[2:])


def build_tiles(slave_basis, received, slave_index, need_index, weights):
    left = slave_basis[slave_index]
    scaled = (received[need_index].astype(jnp.float32) * weights[:, None, :]).astype(jnp.bfloat16)
    tile = jnp.einsum("pnq,pmq->pnm", left, scaled, preferred_element_type=jnp.float32)
    return tile.astype(jnp.bfloat16)


def on_device(
    slave_basis,
    master_basis,
    slave_gap,
    master_disp,
    pressure,
    active,
    need_owner,
    need_slot,
    pair_need,
    pair_slave,
    pair_segs,
    pair_weight,
):
    high = lax.Precision.HIGHEST
    peers = lax.axis_size(("slave", "master"))
    need_dev = need_slot.shape[0]
    cap = 2 * need_dev // peers
    nodes = slave_basis.shape[1]
    qpts = slave_basis.shape[2]
    owner = need_owner[:, 0]
    match = (owner[:, None] == jnp.arange(peers, dtype=jnp.int32)[None, :]).astype(jnp.int32)
    earlier = jnp.cumsum(match, axis=0) - match
    rank = jnp.sum(earlier * match, axis=1)
    position = owner * cap + rank
    request = jnp.zeros((peers * cap,), jnp.int32).at[position].set(need_slot)
    filled = jnp.zeros((peers * cap,), jnp.int32).at[position].set(1)
    wanted, present = (
        lax.all_to_all(
            request.reshape(peers, cap),
            ("slave", "master"),
            split_axis=0,
            concat_axis=0,
            tiled=True,
        ),
        lax.all_to_all(
            filled.reshape(peers, cap), ("slave", "master"), split_axis=0, concat_axis=0, tiled=True
        ),
    )
    wanted = wanted.reshape(-1)
    present = present.reshape(-1)
    outgoing = master_basis[wanted].reshape(peers, cap, nodes, qpts)
    incoming = lax.all_to_all(
        outgoing, ("slave", "master"), split_axis=0, concat_axis=0, tiled=True
    )
    received = incoming.reshape(peers * cap, nodes, qpts)[position]
    limit = GAUSS * pair_segs
    weights = jnp.where(
        jnp.arange(qpts, dtype=jnp.int32)[None, :] < limit[:, None],
        pair_weight,
        jnp.zeros_like(pair_weight),
    )
    slave_count = slave_basis.shape[0]
    slave_onehot = (
        pair_slave[None, :] == jnp.arange(slave_count, dtype=jnp.int32)[:, None]
    ).astype(jnp.float32)
    need_onehot = (pair_need[None, :] == jnp.arange(need_dev, dtype=jnp.int32)[:, None]).astype(
        jnp.float32
    )
    owner_onehot = (
        (wanted[None, :] == jnp.arange(master_basis.shape[0], dtype=jnp.int32)[:, None])
        & (present[None, :] == 1)
    ).astype(jnp.float32)
    slave_weight = jnp.dot(slave_onehot, weights, precision=high)
    slave_float = slave_basis.astype(jnp.float32)
    master_float = master_basis.astype(jnp.float32)
    squares = jnp.square(slave_float)
    lump_part = jnp.einsum("snq,sq->sn", squares, slave_weight, precision=high)

    def make_tiles(items):
        return build_tiles(slave_basis, received, items[0], items[1], items[2])

    stored = blockwise(make_tiles, (pair_slave, pair_need, weights))
    lam = pressure
    disp = master_disp
    flags = active == 1
    root_lump = None
    for update in range(ITERS):
        own_proj = jnp.einsum("mnq,mn->mq", master_float, disp, precision=high)
        outgoing_proj = own_proj[wanted].reshape(peers, cap, qpts)
        returned = lax.all_to_all(
            outgoing_proj, ("slave", "master"), split_axis=0, concat_axis=0, tiled=True
        )
        need_proj = returned.reshape(peers * cap, qpts)[position]
        pair_terms = weights * need_proj[pair_need]
        slave_terms = jnp.dot(slave_onehot, pair_terms, precision=high)
        partial_coupled = jnp.einsum("snq,sq->sn", slave_float, slave_terms, precision=high)
        if update == 0:
            lump_total, coupled = lax.psum((lump_part, partial_coupled), "master")
            root_lump = jnp.sqrt(1.0 + lump_total)
        else:
            coupled = lax.psum(partial_coupled, "master")
        gap = slave_gap - coupled / root_lump
        lam = jnp.where(flags, lam - 1.0 * gap, jnp.zeros_like(lam))
        slave_proj = jnp.einsum("snq,sn->sq", slave_float, lam, precision=high)
        need_load = jnp.dot(need_onehot, weights * slave_proj[pair_slave], precision=high)
        outbound = jnp.zeros((peers * cap, qpts), jnp.float32).at[position].set(need_load)
        inbound = lax.all_to_all(
            outbound.reshape(peers, cap, qpts),
            ("slave", "master"),
            split_axis=0,
            concat_axis=0,
            tiled=True,
        )
        own_load = jnp.dot(owner_onehot, inbound.reshape(peers * cap, qpts), precision=high)
        force = jnp.einsum("mnq,mq->mn", master_float, own_load, precision=high)
        disp = disp - 0.05 * force
    return (lam, disp, stored)


def solution(mesh):
    return jax.shard_map(
        on_device,
        mesh=mesh,
        in_specs=(
            P("slave", None, None),
            P(("slave", "master"), None, None),
            P("slave", None),
            P(("slave", "master"), None),
            P("slave", None),
            P("slave", None),
            P(("slave", "master"), None),
            P(("slave", "master")),
            P(("slave", "master")),
            P(("slave", "master")),
            P(("slave", "master")),
            P(("slave", "master"), None),
        ),
        out_specs=(
            P("slave", None),
            P(("slave", "master"), None),
            P(("slave", "master"), None, None),
        ),
        check_vma=False,
    )
```

profile of v0, /device:TPU:1, one launch (start us, length us, event | category | flops | bytes accessed | tf_op | source)
XLA Modules:
  0.0 331.9 jit_solution(11572906067537918175)
XLA Ops:
  0.7 0.8 fusion.24
  1.7 0.8 select_reduce_fusion
  2.5 0.7 fusion.38
  3.2 1.1 scatter_custom_fusion
  4.3 0.8 all_to_all.27
  5.1 11.5 %all-to-all-start = ((s32[128,1,2]{2,1,0:T(1,128)}), s32[128,1,2]{2,1,0:T(1,128)S(1)}, u32[]{:S(2)}, u32[]{:S(2)}) async-start(s32[128,1,2]{2,1,0:T(1,128)} %bitcast.13), calls=%async_computation | async-start | bytes 131072 | tf_op jit(solution)/shard_map/all_to_all | solution.py:51
  16.6 0.7 compare_select_fusion.4
  17.3 0.7 broadcast_multiply_fusion
  17.9 0.7 compare_select_fusion.3
  18.6 1.1 fusion.17
  19.7 0.9 fusion.25
  20.6 0.9 fusion.43
  21.5 2.8 fusion.6
  24.3 1.7 all-to-all-done
  26.0 0.5 broadcast.180
  26.5 0.8 reduce.7
  27.5 1.3 gather_fusion.2
  28.9 8.1 %all-to-all-start.1 = ((f32[128,2,128]{2,1,0:T(2,128)}), f32[128,2,128]{2,1,0:T(2,128)S(1)}, u32[]{:S(2)}, u32[]{:S(2)}) async-start(f32[128,2,128]{2,1,0:T(2,128)} %bitcast.15), calls=%async_computation.1 | async-start | bytes 262144 | tf_op jit(solution)/shard_map/all_to_all | solution.py:103
  36.9 1.0 scatter_custom_fusion.1
  37.9 0.8 all_to_all.30
  38.7 8.2 %all-to-all-done.1 = f32[128,2,128]{2,1,0:T(2,128)S(1)} async-done(((f32[128,2,128]{2,1,0:T(2,128)}), f32[128,2,128]{2,1,0:T(2,128)S(1)}, u32[]{:S(2)}, u32[]{:S(2)}) %all-to-all-start.1) | async-done | bytes 131104 | tf_op jit(solution)/shard_map/all_to_all | solution.py:103
  46.9 4.2 %all-to-all-start.2 = ((s32[128,1,2]{2,1,0:T(1,128)}), s32[128,1,2]{2,1,0:T(1,128)S(1)}, u32[]{:S(2)}, u32[]{:S(2)}) async-start(s32[128,1,2]{2,1,0:T(1,128)} %bitcast.25), calls=%async_computation.2 | async-start | bytes 131072 | tf_op jit(solution)/shard_map/all_to_all | solution.py:58
  51.2 0.6 gather_fusion.3
  51.8 1.0 gather_fusion.4
  53.1 0.9 fusion.44
  54.0 22.8 %all-reduce = (f32[16,128]{1,0:T(8,128)S(1)}, f32[16,128]{1,0:T(8,128)S(1)}) all-reduce(f32[16,128]{1,0:T(8,128)S(1)} %bitcast.138, f32[16,128]{1,0:T(8,128)S(1)} %bitcast.148), channel_id=1, replica_groups=mesh['slave'=16,'master'=8] {'master'}, use_global_device_ids=true, to_apply=%region_3.4 | all-reduce | flops 4096 | bytes 32768 | tf_op jit(solution)/shard_map/psum | solution.py:111
  76.9 0.5 fusion.45
  77.4 1.0 gather_fusion.5
  78.4 0.3 fusion.13
  78.7 1.5 scatter_custom_fusion.2
  80.2 10.4 %all-to-all-start.3 = ((f32[128,2,128]{2,1,0:T(2,128)}), f32[128,2,128]{2,1,0:T(2,128)S(1)}, u32[]{:S(2)}, u32[]{:S(2)}) async-start(f32[128,2,128]{2,1,0:T(2,128)} %bitcast.30), calls=%async_computation.3 | async-start | bytes 262144 | tf_op jit(solution)/shard_map/all_to_all | solution.py:120
  91.1 9.5 %all-to-all-done.3 = f32[128,2,128]{2,1,0:T(2,128)S(1)} async-done(((f32[128,2,128]{2,1,0:T(2,128)}), f32[128,2,128]{2,1,0:T(2,128)S(1)}, u32[]{:S(2)}, u32[]{:S(2)}) %all-to-all-start.3) | async-done | bytes 131104 | tf_op jit(solution)/shard_map/all_to_all | solution.py:120
  100.7 0.3 fusion.46
  101.3 0.7 gather_fusion.6
  102.0 14.1 %all_to_all.43 = f32[128,2,128]{2,1,0:T(2,128)S(1)} all-to-all(f32[128,2,128]{2,1,0:T(2,128)S(1)} %bitcast.132), channel_id=1, replica_groups=mesh['slave'=16,'master'=8] {'slave','master'}, dimensions={0} | all-to-all | bytes 262144 | tf_op jit(solution)/shard_map/all_to_all | solution.py:103
  116.1 0.6 gather_fusion.7
  116.8 1.0 gather_fusion.8
  118.0 0.9 fusion.48
  118.9 12.8 %psum.23 = f32[16,128]{1,0:T(8,128)S(1)} all-reduce(f32[16,128]{1,0:T(8,128)S(1)} %bitcast.139), channel_id=1, replica_groups=mesh['slave'=16,'master'=8] {'master'}, use_global_device_ids=true, to_apply=%region_7.8 | all-reduce | flops 2048 | bytes 16384 | tf_op jit(solution)/shard_map/psum | solution.py:114
  131.8 0.5 fusion.49
  132.3 1.0 gather_fusion.9
  133.4 0.3 fusion.9
  133.7 1.5 scatter_custom_fusion.3
  135.2 4.9 %all-to-all-start.5 = ((f32[128,2,128]{2,1,0:T(2,128)}), f32[128,2,128]{2,1,0:T(2,128)S(1)}, u32[]{:S(2)}, u32[]{:S(2)}) async-start(f32[128,2,128]{2,1,0:T(2,128)} %bitcast.50), calls=%async_computation.5 | async-start | bytes 262144 | tf_op jit(solution)/shard_map/all_to_all | solution.py:120
  140.1 8.3 %gather_fusion.10 = bf16[256,128,128]{2,1,0:T(8,128)(2,1)} fusion(bf16[4,128,128]{2,1,0:T(8,128)(2,1)S(1)} %copy-done, s32[1024]{0:T(1024)S(1)} %pad_clamp_fusion.5), kind=kCustom, calls=%fused_computation.10 | custom fusion | bytes 16778240 | tf_op jit(solution)/shard_map/gather | solution.py:64
  148.4 1.8 all-to-all-done.5
  150.2 8.7 %all-to-all-start.6 = ((bf16[128,2,128,128]{3,2,1,0:T(8,128)(2,1)}), bf16[128,2,128,128]{3,2,1,0:T(8,128)(2,1)}, u32[]{:S(2)}, u32[]{:S(2)}) async-start(bf16[128,2,128,128]{3,2,1,0:T(8,128)(2,1)} %bitcast.125), calls=%async_computation.6 | async-start | bytes 16777216 | tf_op jit(solution)/shard_map/all_to_all | solution.py:65
  159.1 0.3 fusion.50
  159.4 0.6 multiply_subtract_fusion
  160.0 98.3 %all-to-all-done.6 = bf16[128,2,128,128]{3,2,1,0:T(8,128)(2,1)} async-done(((bf16[128,2,128,128]{3,2,1,0:T(8,128)(2,1)}), bf16[128,2,128,128]{3,2,1,0:T(8,128)(2,1)}, u32[]{:S(2)}, u32[]{:S(2)}) %all-to-all-start.6) | async-done | bytes 8388640 | tf_op jit(solution)/shard_map/all_to_all | solution.py:65
  258.3 6.4 %gather_fusion.11 = bf16[128,128,128]{2,1,0:T(8,128)(2,1)} fusion(bf16[256,128,128]{2,1,0:T(8,128)(2,1)} %bitcast.59, s32[1024]{0:T(1024)S(1)} %pad_clamp_fusion.4), kind=kCustom, calls=%fused_computation.11 | custom fusion | bytes 8389120 | tf_op jit(solution)/shard_map/gather | solution.py:68
  264.7 67.2 %while.10 = (s32[]{:T(128)}, bf16[4,128,128,128]{3,2,1,0:T(8,128)(2,1)}, s32[4,128]{1,0:T(4,128)S(1)}, bf16[16,128,128]{2,1,0:T(8,128)(2,1)S(1)}, s32[4,128]{1,0...) while((s32[]{:T(128)}, bf16[4,128,128,128]{3,2,1,0:T(8,128)(2,1)}, ...), condition=%wide.region_10.11_spmd, body=%wide.region_9.10_spmd.sunk | while | flops 545262336 | bytes 29569628 | solution.py:12
  264.8 3.0 gather_fusion
  267.8 5.2 %gather_fusion.1 = bf16[128,128,128]{2,1,0:T(8,128)(2,1)} fusion(bf16[128,128,128]{2,1,0:T(8,128)(2,1)} %get-tuple-element.129, s32[1024]{0:T(1024)S(1)} %pad_clamp_fusion.9), kind=kCustom, calls=%fused_computation.1.clone.1 | custom fusion | bytes 8389120 | tf_op jit(solution)/shard_map/while/body/eval_jaxpr/gather | solution.py:18
  273.0 8.5 %bitcast_dynamic-update-slice_fusion.2 = bf16[4,128,128,128]{3,2,1,0:T(8,128)(2,1)} fusion(bf16[4,128,128,128]{3,2,1,0:T(8,128)(2,1)} %get-tuple-element.117, s32[]{:T(128)} %get-tuple-element.116, bf16[128,128,128]{2,1,0:T(8,128)(2,1)} %gather_fusion, bf16[128,128,128]{2,1,0:T(8,128)(2,1)} %gather_fusion.1, ...), kind=kOutput, calls=%fused_computation.18.clone.1 | convolution fusion | flops 545259520 | bytes 12648960 | tf_op jit(solution)/shard_map/while/body/eval_jaxpr/pnq,pmq->pnm/dot_general | solution.py:19
  281.6 3.0 gather_fusion
  284.6 5.2 %gather_fusion.1 = bf16[128,128,128]{2,1,0:T(8,128)(2,1)} fusion(bf16[128,128,128]{2,1,0:T(8,128)(2,1)} %get-tuple-element.129, s32[1024]{0:T(1024)S(1)} %pad_clamp_fusion.9), kind=kCustom, calls=%fused_computation.1.clone.1 | custom fusion | bytes 8389120 | tf_op jit(solution)/shard_map/while/body/eval_jaxpr/gather | solution.py:18
  289.8 8.5 %bitcast_dynamic-update-slice_fusion.2 = bf16[4,128,128,128]{3,2,1,0:T(8,128)(2,1)} fusion(bf16[4,128,128,128]{3,2,1,0:T(8,128)(2,1)} %get-tuple-element.117, s32[]{:T(128)} %get-tuple-element.116, bf16[128,128,128]{2,1,0:T(8,128)(2,1)} %gather_fusion, bf16[128,128,128]{2,1,0:T(8,128)(2,1)} %gather_fusion.1, ...), kind=kOutput, calls=%fused_computation.18.clone.1 | convolution fusion | flops 545259520 | bytes 12648960 | tf_op jit(solution)/shard_map/while/body/eval_jaxpr/pnq,pmq->pnm/dot_general | solution.py:19
  298.3 3.0 gather_fusion
  301.4 5.2 %gather_fusion.1 = bf16[128,128,128]{2,1,0:T(8,128)(2,1)} fusion(bf16[128,128,128]{2,1,0:T(8,128)(2,1)} %get-tuple-element.129, s32[1024]{0:T(1024)S(1)} %pad_clamp_fusion.9), kind=kCustom, calls=%fused_computation.1.clone.1 | custom fusion | bytes 8389120 | tf_op jit(solution)/shard_map/while/body/eval_jaxpr/gather | solution.py:18
  306.6 8.5 %bitcast_dynamic-update-slice_fusion.2 = bf16[4,128,128,128]{3,2,1,0:T(8,128)(2,1)} fusion(bf16[4,128,128,128]{3,2,1,0:T(8,128)(2,1)} %get-tuple-element.117, s32[]{:T(128)} %get-tuple-element.116, bf16[128,128,128]{2,1,0:T(8,128)(2,1)} %gather_fusion, bf16[128,128,128]{2,1,0:T(8,128)(2,1)} %gather_fusion.1, ...), kind=kOutput, calls=%fused_computation.18.clone.1 | convolution fusion | flops 545259520 | bytes 12648960 | tf_op jit(solution)/shard_map/while/body/eval_jaxpr/pnq,pmq->pnm/dot_general | solution.py:19
  315.1 3.0 gather_fusion
  318.1 5.2 %gather_fusion.1 = bf16[128,128,128]{2,1,0:T(8,128)(2,1)} fusion(bf16[128,128,128]{2,1,0:T(8,128)(2,1)} %get-tuple-element.129, s32[1024]{0:T(1024)S(1)} %pad_clamp_fusion.9), kind=kCustom, calls=%fused_computation.1.clone.1 | custom fusion | bytes 8389120 | tf_op jit(solution)/shard_map/while/body/eval_jaxpr/gather | solution.py:18
  323.4 8.5 %bitcast_dynamic-update-slice_fusion.2 = bf16[4,128,128,128]{3,2,1,0:T(8,128)(2,1)} fusion(bf16[4,128,128,128]{3,2,1,0:T(8,128)(2,1)} %get-tuple-element.117, s32[]{:T(128)} %get-tuple-element.116, bf16[128,128,128]{2,1,0:T(8,128)(2,1)} %gather_fusion, bf16[128,128,128]{2,1,0:T(8,128)(2,1)} %gather_fusion.1, ...), kind=kOutput, calls=%fused_computation.18.clone.1 | convolution fusion | flops 545259520 | bytes 12648960 | tf_op jit(solution)/shard_map/while/body/eval_jaxpr/pnq,pmq->pnm/dot_general | solution.py:19
  (55 shorter events, 2.0 us)
Async XLA Ops:
  0.6 20.0 %copy-start = (bf16[4,128,128]{2,1,0:T(8,128)(2,1)S(1)}, bf16[4,128,128]{2,1,0:T(8,128)(2,1)}, u32[]{:S(2)}) copy-start(bf16[4,128,128]{2,1,0:T(8,128)(2,1)} %param.15) | copy-start | bytes 393220
  0.6 52.2 %copy-start.2 = (s32[512]{0:T(512)S(1)}, s32[512]{0:T(512)}, u32[]{:S(2)}) copy-start(s32[512]{0:T(512)} %param.23) | copy-start | bytes 6148
  0.7 52.4 %copy-start.1 = (bf16[16,128,128]{2,1,0:T(8,128)(2,1)S(1)}, bf16[16,128,128]{2,1,0:T(8,128)(2,1)}, u32[]{:S(2)}) copy-start(bf16[16,128,128]{2,1,0:T(8,128)(2,1)} %param.14) | copy-start | bytes 1572868
  0.7 76.2 %copy-start.5 = (f32[16,128]{1,0:T(8,128)S(1)}, f32[16,128]{1,0:T(8,128)}, u32[]{:S(2)}) copy-start(f32[16,128]{1,0:T(8,128)} %param.16) | copy-start | bytes 24580
  0.7 76.2 %copy-start.7 = (f32[16,128]{1,0:T(8,128)S(1)}, f32[16,128]{1,0:T(8,128)}, u32[]{:S(2)}) copy-start(f32[16,128]{1,0:T(8,128)} %param.18) | copy-start | bytes 24580
  0.7 76.1 %copy-start.8 = (s32[16,128]{1,0:T(8,128)S(1)}, s32[16,128]{1,0:T(8,128)}, u32[]{:S(2)}) copy-start(s32[16,128]{1,0:T(8,128)} %param.19) | copy-start | bytes 24580
  5.1 20.9 %all-to-all-start = ((s32[128,1,2]{2,1,0:T(1,128)}), s32[128,1,2]{2,1,0:T(1,128)S(1)}, u32[]{:S(2)}, u32[]{:S(2)}) async-start(s32[128,1,2]{2,1,0:T(1,128)} %bitcast.13), calls=%async_computation | async-start | bytes 131072 | tf_op jit(solution)/shard_map/all_to_all | solution.py:51
  27.5 50.9 %copy-start.3 = (s32[512]{0:T(512)S(1)}, s32[512]{0:T(512)}, u32[]{:S(2)}) copy-start(s32[512]{0:T(512)} %param.22) | copy-start | bytes 6148
  28.9 18.0 %all-to-all-start.1 = ((f32[128,2,128]{2,1,0:T(2,128)}), f32[128,2,128]{2,1,0:T(2,128)S(1)}, u32[]{:S(2)}, u32[]{:S(2)}) async-start(f32[128,2,128]{2,1,0:T(2,128)} %bitcast.15), calls=%async_computation.1 | async-start | bytes 262144 | tf_op jit(solution)/shard_map/all_to_all | solution.py:103
  46.9 33.3 %all-to-all-start.2 = ((s32[128,1,2]{2,1,0:T(1,128)}), s32[128,1,2]{2,1,0:T(1,128)S(1)}, u32[]{:S(2)}, u32[]{:S(2)}) async-start(s32[128,1,2]{2,1,0:T(1,128)} %bitcast.25), calls=%async_computation.2 | async-start | bytes 131072 | tf_op jit(solution)/shard_map/all_to_all | solution.py:58
  51.1 49.9 %copy-start.6 = (f32[4,128]{1,0:T(4,128)S(1)}, f32[4,128]{1,0:T(4,128)}, u32[]{:S(2)}) copy-start(f32[4,128]{1,0:T(4,128)} %param.17) | copy-start | bytes 6148
  80.2 20.4 %all-to-all-start.3 = ((f32[128,2,128]{2,1,0:T(2,128)}), f32[128,2,128]{2,1,0:T(2,128)S(1)}, u32[]{:S(2)}, u32[]{:S(2)}) async-start(f32[128,2,128]{2,1,0:T(2,128)} %bitcast.30), calls=%async_computation.3 | async-start | bytes 262144 | tf_op jit(solution)/shard_map/all_to_all | solution.py:120
  131.8 16.6 %copy-start.4 = (f32[16,128]{1,0:T(8,128)}, f32[16,128]{1,0:T(8,128)S(1)}, u32[]{:S(2)}) copy-start(f32[16,128]{1,0:T(8,128)S(1)} %subtract_select_fusion) | copy-start | bytes 24580
  135.2 15.0 %all-to-all-start.5 = ((f32[128,2,128]{2,1,0:T(2,128)}), f32[128,2,128]{2,1,0:T(2,128)S(1)}, u32[]{:S(2)}, u32[]{:S(2)}) async-start(f32[128,2,128]{2,1,0:T(2,128)} %bitcast.50), calls=%async_computation.5 | async-start | bytes 262144 | tf_op jit(solution)/shard_map/all_to_all | solution.py:120
  150.2 108.1 %all-to-all-start.6 = ((bf16[128,2,128,128]{3,2,1,0:T(8,128)(2,1)}), bf16[128,2,128,128]{3,2,1,0:T(8,128)(2,1)}, u32[]{:S(2)}, u32[]{:S(2)}) async-start(bf16[128,2,128,128]{3,2,1,0:T(8,128)(2,1)} %bitcast.125), calls=%async_computation.6 | async-start | bytes 16777216 | tf_op jit(solution)/shard_map/all_to_all | solution.py:65
where the time goes:
time: 337 us; the launch traced here: 332 us
  waiting for transfers between devices  119 us (35%)
  local copies, waits for them, and re-layouts  62.9 us (19%)
  blocking collectives  49.8 us (15%)
  starting transfers between devices  47.8 us (14%)
  matrix products  43.6 us (13%)
  other arithmetic  7.37 us (2%)
    all_to_all x1, waiting for transfers between devices, on_device(): lax.all_to_all(outgoing, ('slave', 'master'), split_axis=0, concat_axis=0...  98.3 us
    dot_general x4, matrix products, build_tiles(): jnp.einsum('pnq,pmq->pnm', left, scaled, preferred_element_type=jnp.float32)  34 us
    psum x1, blocking collectives, on_device(): lump_total, coupled = lax.psum((lump_part, partial_coupled), 'master')  22.8 us
    gather x4, local copies, waits for them, and re-layouts, build_tiles(): received[need_index].astype(jnp.float32) * weights[:, None, :]  21 us
    all_to_all x2, starting transfers between devices, on_device(): lax.all_to_all(outbound.reshape(peers, cap, qpts), ('slave', 'master'), s...  15.3 us
    all_to_all x1, blocking collectives, on_device(): lax.all_to_all(outgoing_proj, ('slave', 'master'), split_axis=0, concat_a...  14.1 us
    psum x1, blocking collectives, on_device(): coupled = lax.psum(partial_coupled, 'master')  12.8 us
    gather x4, local copies, waits for them, and re-layouts, build_tiles(): left = slave_basis[slave_index]  12 us
  transfers between devices with their start and end apart: 6, of which 5 were waited for; matrix products, arithmetic and copies ran while one was open for 7% of the time, Pallas kernels for 0%

commit v1 on v0

v1 whole, which is shorter than its diff:
```python
import functools

import jax
import jax.numpy as jnp
from jax import lax
from jax.experimental import pallas as pl
from jax.experimental.pallas import tpu as pltpu
from jax.sharding import PartitionSpec as P

GAUSS = 16
ITERS = 2
GROUP = 32


def tile_kernel(group, sidx_ref, nidx_ref, slave_ref, recv_ref, w_ref, out_ref):
    base = pl.program_id(0) * group

    def body(g, carry):
        s = sidx_ref[base + g]
        r = nidx_ref[base + g]
        left = slave_ref[s]
        w = w_ref[pl.ds(g, 1), :]
        right = (recv_ref[r].astype(jnp.float32) * w).astype(jnp.bfloat16)
        tile = lax.dot_general(
            left, right, (((1,), (1,)), ((), ())), preferred_element_type=jnp.float32
        )
        out_ref[g] = tile.astype(out_ref.dtype)
        return carry

    lax.fori_loop(0, group, body, 0)


def build_tiles(slave_basis, received, pair_slave, pair_need, weights):
    pairs = weights.shape[0]
    nodes, qpts = slave_basis.shape[1], slave_basis.shape[2]
    group = GROUP
    grid_spec = pltpu.PrefetchScalarGridSpec(
        num_scalar_prefetch=2,
        grid=(pairs // group,),
        in_specs=[
            pl.BlockSpec(slave_basis.shape, lambda i, s, n: (0, 0, 0)),
            pl.BlockSpec(received.shape, lambda i, s, n: (0, 0, 0)),
            pl.BlockSpec((group, qpts), lambda i, s, n: (i, 0)),
        ],
        out_specs=pl.BlockSpec((group, nodes, nodes), lambda i, s, n: (i, 0, 0)),
    )
    return pl.pallas_call(
        functools.partial(tile_kernel, group),
        grid_spec=grid_spec,
        out_shape=jax.ShapeDtypeStruct((pairs, nodes, nodes), jnp.bfloat16),
        compiler_params=pltpu.CompilerParams(vmem_limit_bytes=48 * 1024 * 1024),
    )(pair_slave, pair_need, slave_basis, received, weights)


def on_device(
    slave_basis,
    master_basis,
    slave_gap,
    master_disp,
    pressure,
    active,
    need_owner,
    need_slot,
    pair_need,
    pair_slave,
    pair_segs,
    pair_weight,
):
    high = lax.Precision.HIGHEST
    everyone = ("slave", "master")
    mb_dev = master_basis.shape[0]
    need_dev = need_slot.shape[0]
    qpts = slave_basis.shape[2]
    request = need_owner[:, 0] * mb_dev + need_slot
    every_basis = lax.all_gather(master_basis, everyone, axis=0, tiled=True)
    mblocks = every_basis.shape[0]
    received = every_basis[request]
    limit = GAUSS * pair_segs
    weights = jnp.where(
        jnp.arange(qpts, dtype=jnp.int32)[None, :] < limit[:, None],
        pair_weight,
        jnp.zeros_like(pair_weight),
    )
    slave_count = slave_basis.shape[0]
    slave_onehot = (
        pair_slave[None, :] == jnp.arange(slave_count, dtype=jnp.int32)[:, None]
    ).astype(jnp.float32)
    need_onehot = (pair_need[None, :] == jnp.arange(need_dev, dtype=jnp.int32)[:, None]).astype(
        jnp.float32
    )
    block_onehot = (request[None, :] == jnp.arange(mblocks, dtype=jnp.int32)[:, None]).astype(
        jnp.float32
    )
    slave_weight = jnp.dot(slave_onehot, weights, precision=high)
    slave_float = slave_basis.astype(jnp.float32)
    master_float = master_basis.astype(jnp.float32)
    squares = jnp.square(slave_float)
    lump_part = jnp.einsum("snq,sq->sn", squares, slave_weight, precision=high)

    stored = build_tiles(slave_basis, received, pair_slave, pair_need, weights)
    lam = pressure
    disp = master_disp
    flags = active == 1
    root_lump = None
    for update in range(ITERS):
        own_proj = jnp.einsum("mnq,mn->mq", master_float, disp, precision=high)
        every_proj = lax.all_gather(own_proj, everyone, axis=0, tiled=True)
        need_proj = every_proj[request]
        pair_terms = weights * need_proj[pair_need]
        slave_terms = jnp.dot(slave_onehot, pair_terms, precision=high)
        partial_coupled = jnp.einsum("snq,sq->sn", slave_float, slave_terms, precision=high)
        if update == 0:
            lump_total, coupled = lax.psum((lump_part, partial_coupled), "master")
            root_lump = jnp.sqrt(1.0 + lump_total)
        else:
            coupled = lax.psum(partial_coupled, "master")
        gap = slave_gap - coupled / root_lump
        lam = jnp.where(flags, lam - 1.0 * gap, jnp.zeros_like(lam))
        slave_proj = jnp.einsum("snq,sn->sq", slave_float, lam, precision=high)
        need_load = jnp.dot(need_onehot, weights * slave_proj[pair_slave], precision=high)
        block_load = jnp.dot(block_onehot, need_load, precision=high)
        own_load = lax.psum_scatter(block_load, everyone, scatter_dimension=0, tiled=True)
        force = jnp.einsum("mnq,mq->mn", master_float, own_load, precision=high)
        disp = disp - 0.05 * force
    return (lam, disp, stored)


def solution(mesh):
    return jax.shard_map(
        on_device,
        mesh=mesh,
        in_specs=(
            P("slave", None, None),
            P(("slave", "master"), None, None),
            P("slave", None),
            P(("slave", "master"), None),
            P("slave", None),
            P("slave", None),
            P(("slave", "master"), None),
            P(("slave", "master")),
            P(("slave", "master")),
            P(("slave", "master")),
            P(("slave", "master")),
            P(("slave", "master"), None),
        ),
        out_specs=(
            P("slave", None),
            P(("slave", "master"), None),
            P(("slave", "master"), None, None),
        ),
        check_vma=False,
    )
```

time: 337 us -> 601 us (1.78)
  waiting for transfers between devices: 119 us -> 363 us
  Pallas kernels: 0 us -> 83 us
  blocking collectives: 49.8 us -> 107 us
  starting transfers between devices: 47.8 us -> 0.12 us
  local copies, waits for them, and re-layouts: 62.9 us -> 17.9 us
  matrix products: 43.6 us -> 11.1 us
  between operations: 0.98 us -> 13.9 us
    unnamed x0 -> x5, waiting for transfers between devices: none -> 283 us
    all_to_all x6 -> x0, waiting for transfers between devices: 119 us -> none  [the longest x1 98.3 us: on_device(): lax.all_to_all(outgoing, ('slave', 'master'), split_axis=0, concat_axis=0...]
    pallas_call x0 -> x1, Pallas kernels: none -> 83 us  [build_tiles(): pl.pallas_call(functools.partial(tile_kernel, group), grid_spec=grid_spec...]
    all_gather x0 -> x1, waiting for transfers between devices: none -> 79.4 us  [on_device(): every_basis = lax.all_gather(master_basis, everyone, axis=0, tiled=True)]
    all_gather x0 -> x2, blocking collectives: none -> 72.7 us  [on_device(): every_proj = lax.all_gather(own_proj, everyone, axis=0, tiled=True)]
    all_to_all x6 -> x0, starting transfers between devices: 47.8 us -> none  [the longest x2 15.3 us: on_device(): lax.all_to_all(outbound.reshape(peers, cap, qpts), ('slave', 'master'), s...]
    gather x14 -> x3, local copies, waits for them, and re-layouts: 51.1 us -> 10.2 us  [the longest x1 8.86 us: on_device(): received = every_basis[request]]
    dot_general x6 -> x2, matrix products: 34.4 us -> 1.93 us  [on_device(): block_load = jnp.dot(block_onehot, need_load, precision=high)]
  transfers between devices with their start and end apart: 6 -> 3, of which waited for: 5 -> 3; matrix products, arithmetic and copies ran while one was open for 7% -> 0% of each run, Pallas kernels for 0% -> 0%
where the time goes in v1:
time: 601 us
  waiting for transfers between devices  363 us (60%)
  blocking collectives  107 us (18%)
  Pallas kernels  83 us (14%)
  local copies, waits for them, and re-layouts  17.9 us (3%)
  between operations  13.9 us (2%)
  matrix products  11.1 us (2%)
    unnamed x5, waiting for transfers between devices  283 us
    pallas_call x1, Pallas kernels, build_tiles(): pl.pallas_call(functools.partial(tile_kernel, group), grid_spec=grid_spec...  83 us
    all_gather x1, waiting for transfers between devices, on_device(): every_basis = lax.all_gather(master_basis, everyone, axis=0, tiled=True)  79.4 us
    all_gather x2, blocking collectives, on_device(): every_proj = lax.all_gather(own_proj, everyone, axis=0, tiled=True)  72.7 us
    psum x1, blocking collectives, on_device(): lump_total, coupled = lax.psum((lump_part, partial_coupled), 'master')  22.4 us
    psum x1, blocking collectives, on_device(): coupled = lax.psum(partial_coupled, 'master')  12.1 us
  transfers between devices with their start and end apart: 3, of which 3 were waited for; matrix products, arithmetic and copies ran while one was open for 0% of the time, Pallas kernels for 0%

profile of v1, /device:TPU:1, one launch (start us, length us, event | category | flops | bytes accessed | tf_op | source)
XLA Modules:
  0.0 600.5 jit_solution(13837256573782815036)
XLA Ops:
  7.2 0.0 copy-start.1
  7.2 0.0 copy-start.7
  7.2 0.0 copy-start.10
  7.2 0.0 copy-start.9
  7.2 0.0 all-reduce.6.cloned.1.call-start
  7.3 0.7 broadcast_multiply_fusion
  8.0 0.7 compare_select_fusion.1
  8.7 0.7 compare_select_fusion
  9.4 0.7 compare_select_fusion.2
  10.0 1.1 fusion.13.w_ref
  11.1 0.0 copy-start.3
  11.2 0.9 fusion.18
  12.0 1.1 fusion.22
  13.2 38.8 %all-gather = f32[128,4,128]{2,1,0:T(4,128)S(1)} all-gather(f32[1,4,128]{2,1,0:T(4,128)S(1)} %bitcast.83), channel_id=1, replica_groups=mesh['slave'=16,'master'=8] {'slave','master'}, dimensions={0}, use_global_device_ids=true | all-gather | bytes 264192 | tf_op jit(solution)/shard_map/all_gather | solution.py:107
  52.0 0.6 gather_fusion
  52.6 0.0 copy-start.4
  52.6 0.0 copy-start.8
  52.6 1.0 gather_fusion.1
  53.7 0.9 fusion.11
  54.6 0.0 copy-done.1
  54.6 1.7 fusion
  56.3 0.9 fusion.23
  57.2 22.4 %all-reduce.2 = (f32[16,128]{1,0:T(8,128)S(1)}, f32[16,128]{1,0:T(8,128)S(1)}) all-reduce(f32[16,128]{1,0:T(8,128)S(1)} %bitcast.79, f32[16,128]{1,0:T(8,128)S(1)} %bitcast.91), channel_id=1, replica_groups=mesh['slave'=16,'master'=8] {'master'}, use_global_device_ids=true, to_apply=%region_0.1 | all-reduce | flops 4096 | bytes 32768 | tf_op jit(solution)/shard_map/psum | solution.py:113
  79.6 0.0 copy-done.7
  79.6 0.0 copy-done.10
  79.6 0.0 copy-done.9
  79.7 0.5 fusion.24
  80.2 1.0 gather_fusion.2
  81.2 0.0 copy-done.3
  81.2 0.3 fusion.7
  81.5 1.0 fusion.10
  82.5 0.0 all-reduce.6.cloned.1.call-update
  82.5 0.0 all-reduce.8.cloned.1.call-start
  82.6 142.1 %all-reduce.6.cloned.1.call-done = f32[512,128]{1,0:T(8,128)} async-done(((f32[512,128]{1,0:T(8,128)}), f32[512,128]{1,0:T(8,128)}) %all-reduce.6.cloned.1.call-update) | async-done | bytes 262160
  224.7 0.7 constant_dynamic-slice_fusion.1
  225.4 0.0 copy-done.4
  225.4 0.3 fusion.25
  225.7 0.0 copy-done.8
  225.7 0.2 fusion.26
  225.9 33.9 %all-gather.1 = f32[128,4,128]{2,1,0:T(4,128)S(1)} all-gather(f32[1,4,128]{2,1,0:T(4,128)S(1)} %bitcast.84), channel_id=1, replica_groups=mesh['slave'=16,'master'=8] {'slave','master'}, dimensions={0}, use_global_device_ids=true | all-gather | bytes 264192 | tf_op jit(solution)/shard_map/all_gather | solution.py:107
  259.8 0.6 gather_fusion.3
  260.5 1.0 gather_fusion.4
  261.5 0.0 copy-done.2
  261.5 0.2 fusion.5
  261.8 0.9 fusion.27
  262.7 12.1 %psum.23 = f32[16,128]{1,0:T(8,128)S(1)} all-reduce(f32[16,128]{1,0:T(8,128)S(1)} %bitcast.80), channel_id=1, replica_groups=mesh['slave'=16,'master'=8] {'master'}, use_global_device_ids=true, to_apply=%region_3.4 | all-reduce | flops 2048 | bytes 16384 | tf_op jit(solution)/shard_map/psum | solution.py:116
  274.8 0.0 copy-start.6
  274.8 0.5 fusion.28
  275.4 1.0 gather_fusion.5
  276.4 0.3 fusion.3
  276.7 1.0 fusion.9
  277.7 0.0 all-reduce.8.cloned.1.call-update
  277.7 0.0 all-gather.4.cloned.1.call-start
  277.7 0.7 all-gather.4.cloned.1.call-update
  278.4 140.5 %all-reduce.8.cloned.1.call-done = f32[512,128]{1,0:T(8,128)} async-done(((f32[512,128]{1,0:T(8,128)}), f32[512,128]{1,0:T(8,128)}) %all-reduce.8.cloned.1.call-update) | async-done | bytes 262160
  419.0 0.7 constant_dynamic-slice_fusion
  419.6 0.0 copy-done.5
  419.7 0.3 fusion.29
  419.9 0.6 multiply_subtract_fusion
  420.6 79.4 %all-gather.4.cloned.1.call-done = bf16[512,128,128]{2,1,0:T(8,128)(2,1)} async-done(((bf16[4,128,128]{2,1,0:T(8,128)(2,1)}), bf16[512,128,128]{2,1,0:T(8,128)(2,1)}) %all-gather.4.cloned.1.call-update) | async-done | bytes 16777232 | tf_op jit(solution)/shard_map/all_gather | solution.py:75
  499.9 8.9 %gather_fusion.6 = bf16[128,128,128]{2,1,0:T(8,128)(2,1)} fusion(bf16[512,128,128]{2,1,0:T(8,128)(2,1)} %all-gather.4.cloned.1.call-done, s32[1024]{0:T(1024)S(1)} %pad_clamp_fusion.2), kind=kCustom, calls=%fused_computation.6 | custom fusion | bytes 8389120 | tf_op jit(solution)/shard_map/gather | solution.py:77
  508.8 0.0 copy-done.6
  508.8 2.2 copy-done
  511.0 83.0 %shard_map.139 = bf16[512,128,128]{2,1,0:T(8,128)(2,1)} custom-call(s32[512]{0:T(512)S(1)} %copy-done.2, s32[512]{0:T(512)S(1)} %copy-done.3, bf16[16,128,128]{2,1,0:T(8,128)(2,1)S(1)} %copy-done.1, bf16[128,128,128]{2,1,0:T(8,128)(2,1)S(1)} %copy-done, f32[512,128]{1,0:T(8,128)S(1)} %fusion.13.w_ref), custom_call_target="tpu_custom_call" | custom-call | tf_op jit(solution)/shard_map/pallas_call | solution.py:47
  (9 shorter events, 0.1 us)
Async XLA Ops:
  7.2 47.4 %copy-start.1 = (bf16[16,128,128]{2,1,0:T(8,128)(2,1)S(1)}, bf16[16,128,128]{2,1,0:T(8,128)(2,1)}, u32[]{:S(2)}) copy-start(bf16[16,128,128]{2,1,0:T(8,128)(2,1)} %slave_ref.1) | copy-start | bytes 1572868
  7.2 72.5 %copy-start.7 = (f32[16,128]{1,0:T(8,128)S(1)}, f32[16,128]{1,0:T(8,128)}, u32[]{:S(2)}) copy-start(f32[16,128]{1,0:T(8,128)} %param.14) | copy-start | bytes 24580
  7.2 72.5 %copy-start.10 = (s32[16,128]{1,0:T(8,128)S(1)}, s32[16,128]{1,0:T(8,128)}, u32[]{:S(2)}) copy-start(s32[16,128]{1,0:T(8,128)} %param.17) | copy-start | bytes 24580
  7.2 72.4 %copy-start.9 = (f32[16,128]{1,0:T(8,128)S(1)}, f32[16,128]{1,0:T(8,128)}, u32[]{:S(2)}) copy-start(f32[16,128]{1,0:T(8,128)} %param.16) | copy-start | bytes 24580
  7.2 217.5 %all-reduce.6.cloned.1.call-start = ((), (), s32[]{:S(2)}) async-start(), calls=%async_computation.1 | async-start | bytes 524288
  11.1 70.1 %copy-start.3 = (s32[512]{0:T(512)S(1)}, s32[512]{0:T(512)}, u32[]{:S(2)}) copy-start(s32[512]{0:T(512)} %nidx_ref.1) | copy-start | bytes 6148
  52.6 172.8 %copy-start.4 = (bf16[4,128,128]{2,1,0:T(8,128)(2,1)S(1)}, bf16[4,128,128]{2,1,0:T(8,128)(2,1)}, u32[]{:S(2)}) copy-start(bf16[4,128,128]{2,1,0:T(8,128)(2,1)} %param.13) | copy-start | bytes 393220
  52.6 173.1 %copy-start.8 = (f32[4,128]{1,0:T(4,128)S(1)}, f32[4,128]{1,0:T(4,128)}, u32[]{:S(2)}) copy-start(f32[4,128]{1,0:T(4,128)} %param.15) | copy-start | bytes 6148
  56.3 205.2 %copy-start.2 = (s32[512]{0:T(512)S(1)}, s32[512]{0:T(512)}, u32[]{:S(2)}) copy-start(s32[512]{0:T(512)} %sidx_ref.1) | copy-start | bytes 6148
  82.5 336.4 %all-reduce.8.cloned.1.call-start = ((), (), s32[]{:S(2)}) async-start(), calls=%async_computation.2 | async-start | bytes 524288
  259.8 159.8 %copy-start.5 = (bf16[4,128,128]{2,1,0:T(8,128)(2,1)S(1)}, bf16[4,128,128]{2,1,0:T(8,128)(2,1)}, u32[]{:S(2)}) copy-start(bf16[4,128,128]{2,1,0:T(8,128)(2,1)} %param.13) | copy-start | bytes 393220
  274.8 234.0 %copy-start.6 = (f32[16,128]{1,0:T(8,128)}, f32[16,128]{1,0:T(8,128)S(1)}, u32[]{:S(2)}) copy-start(f32[16,128]{1,0:T(8,128)S(1)} %subtract_select_fusion) | copy-start | bytes 24580
  277.7 222.2 %all-gather.4.cloned.1.call-start = ((), (), s32[]{:S(2)}) async-start(), calls=%async_computation | async-start | bytes 16908288 | tf_op jit(solution)/shard_map/all_gather | solution.py:75
  508.8 2.2 copy-start
Sparse Core Ops, SparseCore 0:
  82.7 142.0 all-reduce.5
  277.8 141.1 all-reduce.7
  422.1 77.7 all-gather.3

commit v2 on v1

v2 whole, which is shorter than its diff:
```python
import functools

import jax
import jax.numpy as jnp
from jax import lax
from jax.experimental import pallas as pl
from jax.experimental.pallas import tpu as pltpu
from jax.sharding import PartitionSpec as P

GAUSS = 16
ITERS = 2
GROUP = 64


def tile_kernel(group, sidx_ref, nidx_ref, mreq_ref, slave_ref, basis_hbm, w_ref, out_ref, recv, sems):
    need = recv.shape[0]

    @pl.when(pl.program_id(0) == 0)
    def _():
        for r in range(need):
            pltpu.make_async_copy(basis_hbm.at[mreq_ref[r]], recv.at[r], sems.at[r]).start()
        for r in range(need):
            pltpu.make_async_copy(basis_hbm.at[0], recv.at[r], sems.at[r]).wait()

    base = pl.program_id(0) * group
    for g in range(group):
        s = sidx_ref[base + g]
        r = nidx_ref[base + g]
        left = slave_ref[s]
        w = w_ref[pl.ds(g, 1), :]
        right = (recv[r].astype(jnp.float32) * w).astype(jnp.bfloat16)
        tile = lax.dot_general(
            left, right, (((1,), (1,)), ((), ())), preferred_element_type=jnp.float32
        )
        out_ref[g] = tile.astype(out_ref.dtype)


def build_tiles(slave_basis, every_basis, request, pair_slave, pair_need, weights):
    pairs = weights.shape[0]
    nodes, qpts = slave_basis.shape[1], slave_basis.shape[2]
    need = request.shape[0]
    group = GROUP
    grid_spec = pltpu.PrefetchScalarGridSpec(
        num_scalar_prefetch=3,
        grid=(pairs // group,),
        in_specs=[
            pl.BlockSpec(slave_basis.shape, lambda i, s, n, m: (0, 0, 0)),
            pl.BlockSpec(memory_space=pl.ANY),
            pl.BlockSpec((group, qpts), lambda i, s, n, m: (i, 0)),
        ],
        out_specs=pl.BlockSpec((group, nodes, nodes), lambda i, s, n, m: (i, 0, 0)),
        scratch_shapes=[
            pltpu.VMEM((need, nodes, qpts), jnp.bfloat16),
            pltpu.SemaphoreType.DMA((need,)),
        ],
    )
    return pl.pallas_call(
        functools.partial(tile_kernel, group),
        grid_spec=grid_spec,
        out_shape=jax.ShapeDtypeStruct((pairs, nodes, nodes), jnp.bfloat16),
        compiler_params=pltpu.CompilerParams(
            vmem_limit_bytes=48 * 1024 * 1024, dimension_semantics=("arbitrary",)
        ),
    )(pair_slave, pair_need, request, slave_basis, every_basis, weights)


def master_sum(x):
    count = lax.axis_size("master")
    spread = jnp.broadcast_to(x[None], (count,) + x.shape)
    got = lax.all_to_all(spread, "master", split_axis=0, concat_axis=0, tiled=True)
    return jnp.sum(got, axis=0)


def on_device(
    slave_basis,
    master_basis,
    slave_gap,
    master_disp,
    pressure,
    active,
    need_owner,
    need_slot,
    pair_need,
    pair_slave,
    pair_segs,
    pair_weight,
):
    high = lax.Precision.HIGHEST
    everyone = ("slave", "master")
    peers = lax.axis_size(everyone)
    mb_dev = master_basis.shape[0]
    need_dev = need_slot.shape[0]
    cap = 2 * need_dev // peers
    qpts = slave_basis.shape[2]
    owner = need_owner[:, 0]
    request = owner * mb_dev + need_slot
    every_basis = lax.all_gather(master_basis, everyone, axis=0, tiled=True)

    match = (owner[:, None] == jnp.arange(peers, dtype=jnp.int32)[None, :]).astype(jnp.int32)
    earlier = jnp.cumsum(match, axis=0) - match
    rank = jnp.sum(earlier * match, axis=1)
    position = owner * cap + rank
    slots = jnp.zeros((peers * cap,), jnp.int32).at[position].set(need_slot)
    filled = jnp.zeros((peers * cap,), jnp.int32).at[position].set(1)
    asked = lax.all_to_all(
        jnp.stack([slots, filled]).reshape(2, peers, cap),
        everyone,
        split_axis=1,
        concat_axis=1,
        tiled=True,
    )
    wanted = asked[0].reshape(-1)
    present = asked[1].reshape(-1)

    limit = GAUSS * pair_segs
    weights = jnp.where(
        jnp.arange(qpts, dtype=jnp.int32)[None, :] < limit[:, None],
        pair_weight,
        jnp.zeros_like(pair_weight),
    )
    slave_count = slave_basis.shape[0]
    slave_onehot = (
        pair_slave[None, :] == jnp.arange(slave_count, dtype=jnp.int32)[:, None]
    ).astype(jnp.float32)
    need_onehot = (pair_need[None, :] == jnp.arange(need_dev, dtype=jnp.int32)[:, None]).astype(
        jnp.float32
    )
    owner_onehot = (
        (wanted[None, :] == jnp.arange(mb_dev, dtype=jnp.int32)[:, None]) & (present[None, :] == 1)
    ).astype(jnp.float32)
    slave_weight = jnp.dot(slave_onehot, weights, precision=high)
    slave_float = slave_basis.astype(jnp.float32)
    master_float = master_basis.astype(jnp.float32)
    squares = jnp.square(slave_float)
    lump_part = jnp.einsum("snq,sq->sn", squares, slave_weight, precision=high)

    stored = build_tiles(slave_basis, every_basis, request, pair_slave, pair_need, weights)
    lam = pressure
    disp = master_disp
    flags = active == 1
    root_lump = None
    for update in range(ITERS):
        own_proj = jnp.einsum("mnq,mn->mq", master_float, disp, precision=high)
        outgoing_proj = own_proj[wanted].reshape(peers, cap, qpts)
        returned = lax.all_to_all(outgoing_proj, everyone, split_axis=0, concat_axis=0, tiled=True)
        need_proj = returned.reshape(peers * cap, qpts)[position]
        pair_terms = weights * need_proj[pair_need]
        slave_terms = jnp.dot(slave_onehot, pair_terms, precision=high)
        partial_coupled = jnp.einsum("snq,sq->sn", slave_float, slave_terms, precision=high)
        if update == 0:
            both = master_sum(jnp.stack([lump_part, partial_coupled]))
            root_lump = jnp.sqrt(1.0 + both[0])
            coupled = both[1]
        else:
            coupled = master_sum(partial_coupled)
        gap = slave_gap - coupled / root_lump
        lam = jnp.where(flags, lam - 1.0 * gap, jnp.zeros_like(lam))
        slave_proj = jnp.einsum("snq,sn->sq", slave_float, lam, precision=high)
        need_load = jnp.dot(need_onehot, weights * slave_proj[pair_slave], precision=high)
        outbound = jnp.zeros((peers * cap, qpts), jnp.float32).at[position].set(need_load)
        inbound = lax.all_to_all(
            outbound.reshape(peers, cap, qpts), everyone, split_axis=0, concat_axis=0, tiled=True
        )
        own_load = jnp.dot(owner_onehot, inbound.reshape(peers * cap, qpts), precision=high)
        force = jnp.einsum("mnq,mq->mn", master_float, own_load, precision=high)
        disp = disp - 0.05 * force
    return (lam, disp, stored)


def solution(mesh):
    return jax.shard_map(
        on_device,
        mesh=mesh,
        in_specs=(
            P("slave", None, None),
            P(("slave", "master"), None, None),
            P("slave", None),
            P(("slave", "master"), None),
            P("slave", None),
            P("slave", None),
            P(("slave", "master"), None),
            P(("slave", "master")),
            P(("slave", "master")),
            P(("slave", "master")),
            P(("slave", "master")),
            P(("slave", "master"), None),
        ),
        out_specs=(
            P("slave", None),
            P(("slave", "master"), None),
            P(("slave", "master"), None, None),
        ),
        check_vma=False,
    )
```

time: 601 us -> 164 us (0.27)
  waiting for transfers between devices: 363 us -> 39 us
  blocking collectives: 107 us -> 22.5 us
  Pallas kernels: 83 us -> 18 us
  starting transfers between devices: 0.12 us -> 30.7 us
    unnamed x5 -> x1, waiting for transfers between devices: 283 us -> 0.68 us
    all_gather x1, waiting for transfers between devices: 79.4 us -> 0.01 us  [on_device(): every_basis = lax.all_gather(master_basis, everyone, axis=0, tiled=True)]
    all_gather x2 -> x0, blocking collectives: 72.7 us -> none  [on_device(): every_proj = lax.all_gather(own_proj, everyone, axis=0, tiled=True)]
    pallas_call x1, Pallas kernels: 83 us -> 18 us  [build_tiles(): pl.pallas_call(functools.partial(tile_kernel, group), grid_spec=grid_spec...]
    all_to_all x0 -> x5, waiting for transfers between devices: none -> 38.3 us  [the longest x2 20.7 us: on_device(): lax.all_to_all(outbound.reshape(peers, cap, qpts), everyone, split_axis=0...]
    psum x2 -> x0, blocking collectives: 34.5 us -> none  [the longest x1 22.4 us: on_device(): lump_total, coupled = lax.psum((lump_part, partial_coupled), 'master')]
    all_to_all x0 -> x5, starting transfers between devices: none -> 30.6 us  [the longest x1 11.5 us: on_device(): lax.all_to_all(jnp.stack([slots, filled]).reshape(2, peers, cap), everyon...]
    all_to_all x0 -> x2, blocking collectives: none -> 22.5 us  [the longest x1 14.6 us: on_device(): lax.all_to_all(outgoing_proj, everyone, split_axis=0, concat_axis=0, tile...]
  transfers between devices with their start and end apart: 3 -> 6, of which waited for: 3 -> 5; matrix products, arithmetic and copies ran while one was open for 0% -> 23% of each run, Pallas kernels for 0% -> 0%
where the time goes in v2:
time: 164 us; the launch traced here: 163 us
  waiting for transfers between devices  39 us (24%)
  starting transfers between devices  30.7 us (19%)
  blocking collectives  22.5 us (14%)
  Pallas kernels  18 us (11%)
  matrix products  15 us (9%)
  local copies, waits for them, and re-layouts  14.9 us (9%)
  between operations  14.4 us (9%)
  other arithmetic  7.99 us (5%)
    all_to_all x2, waiting for transfers between devices, on_device(): lax.all_to_all(outbound.reshape(peers, cap, qpts), everyone, split_axis=0...  20.7 us
    pallas_call x1, Pallas kernels, build_tiles(): pl.pallas_call(functools.partial(tile_kernel, group), grid_spec=grid_spec...  18 us
    all_to_all x1, blocking collectives, on_device(): lax.all_to_all(outgoing_proj, everyone, split_axis=0, concat_axis=0, tile...  14.6 us
    all_to_all x1, starting transfers between devices, on_device(): lax.all_to_all(jnp.stack([slots, filled]).reshape(2, peers, cap), everyon...  11.5 us
    all_to_all x1, waiting for transfers between devices, on_device(): lax.all_to_all(outgoing_proj, everyone, split_axis=0, concat_axis=0, tile...  9.95 us
    all_to_all x2, starting transfers between devices, on_device(): lax.all_to_all(outbound.reshape(peers, cap, qpts), everyone, split_axis=0...  8.76 us
    all_to_all x1, blocking collectives, master_sum(): lax.all_to_all(spread, 'master', split_axis=0, concat_axis=0, tiled=True)  7.91 us
    all_to_all x1, starting transfers between devices, on_device(): lax.all_to_all(outgoing_proj, everyone, split_axis=0, concat_axis=0, tile...  6.64 us
  transfers between devices with their start and end apart: 6, of which 5 were waited for; matrix products, arithmetic and copies ran while one was open for 23% of the time, Pallas kernels for 0%

profile of v2, /device:TPU:1, one launch (start us, length us, event | category | flops | bytes accessed | tf_op | source)
XLA Modules:
  0.0 162.5 jit_solution(4390012738808657465)
XLA Ops:
  7.2 0.0 all-gather.2.cloned.1.call-start
  7.3 0.7 all-gather.2.cloned.1.call-update
  8.0 0.7 fusion.18
  8.7 0.2 reduce_window_sum.11
  8.9 0.8 select_reduce_fusion
  9.7 0.7 fusion.38
  10.4 1.0 scatter_custom_fusion.1
  11.4 0.1 stack.20
  11.5 1.1 scatter_custom_fusion
  12.6 0.1 stack.19
  12.8 0.8 copy.18
  13.6 11.5 %all-to-all-start = ((s32[2,128,2]{2,0,1:T(2,128)}), s32[2,128,2]{2,0,1:T(2,128)S(1)}, u32[]{:S(2)}, u32[]{:S(2)}) async-start(s32[2,128,2]{2,0,1:T(2,128)} %copy.18), calls=%async_computation | async-start | bytes 262144 | tf_op jit(solution)/shard_map/all_to_all | solution.py:105
  25.1 0.7 broadcast_multiply_fusion
  25.7 1.1 fusion.44
  26.9 1.1 fusion.11.w_ref
  28.0 0.9 fusion.19
  28.8 2.8 %fusion = f32[16,1,128]{2,1,0:T(1,128)S(1)} fusion(f32[16,128,1]{1,2,0:T(1,128)S(1)} %bitcast.123, bf16[16,128,128]{2,1,0:T(8,128)(2,1)} %slave_ref.1), kind=kOutput, calls=%fused_computation.12 | convolution fusion | flops 3670016 | bytes 540672 | tf_op jit(solution)/shard_map/snq,sq->sn/dot_general | solution.py:135
  31.6 0.7 compare_select_fusion.2
  32.3 3.1 %all-to-all-done = s32[2,128,2]{2,0,1:T(2,128)S(1)} async-done(((s32[2,128,2]{2,0,1:T(2,128)}), s32[2,128,2]{2,0,1:T(2,128)S(1)}, u32[]{:S(2)}, u32[]{:S(2)}) %all-to-all-start) | async-done | bytes 2080 | tf_op jit(solution)/shard_map/all_to_all | solution.py:105
  35.4 0.2 fusion.43
  35.6 0.1 reshape_squeeze.3
  35.8 1.3 gather_fusion
  37.1 6.6 %all-to-all-start.1 = ((f32[128,2,128]{2,1,0:T(2,128)}), f32[128,2,128]{2,1,0:T(2,128)S(1)}, u32[]{:S(2)}, u32[]{:S(2)}) async-start(f32[128,2,128]{2,1,0:T(2,128)} %bitcast.13), calls=%async_computation.1 | async-start | bytes 262144 | tf_op jit(solution)/shard_map/all_to_all | solution.py:145
  43.8 10.0 %all-to-all-done.1 = f32[128,2,128]{2,1,0:T(2,128)S(1)} async-done(((f32[128,2,128]{2,1,0:T(2,128)}), f32[128,2,128]{2,1,0:T(2,128)S(1)}, u32[]{:S(2)}, u32[]{:S(2)}) %all-to-all-start.1) | async-done | bytes 131104 | tf_op jit(solution)/shard_map/all_to_all | solution.py:145
  53.8 0.6 gather_fusion.1
  54.4 1.0 gather_fusion.2
  55.5 0.9 fusion.9
  56.4 2.0 %fusion.45 = f32[16,1,128]{2,1,0:T(1,128)S(1)} fusion(f32[16,128,1]{1,2,0:T(1,128)S(1)} %bitcast.112, bf16[16,128,128]{2,1,0:T(8,128)(2,1)} %slave_ref.1), kind=kOutput, calls=%fused_computation.82 | convolution fusion | flops 3145728 | bytes 540672 | tf_op jit(solution)/shard_map/snq,sq->sn/dot_general | solution.py:149
  58.4 0.7 broadcast_in_dim.15
  59.0 3.8 %all-to-all-start.2 = ((f32[8,2,16,128]{3,2,1,0:T(8,128)}), f32[8,2,16,128]{3,2,1,0:T(8,128)S(1)}, u32[]{:S(2)}, u32[]{:S(2)}) async-start(f32[8,2,16,128]{3,2,1,0:T(8,128)} %broadcast_in_dim.15), calls=%async_computation.2 | async-start | bytes 262144 | tf_op jit(solution)/shard_map/all_to_all | solution.py:70
  62.8 0.7 compare_select_fusion.1
  63.5 4.6 %all-to-all-done.2 = f32[8,2,16,128]{3,2,1,0:T(8,128)S(1)} async-done(((f32[8,2,16,128]{3,2,1,0:T(8,128)}), f32[8,2,16,128]{3,2,1,0:T(8,128)S(1)}, u32[]{:S(2)}, u32[]{:S(2)}) %all-to-all-start.2) | async-done | bytes 131104 | tf_op jit(solution)/shard_map/all_to_all | solution.py:70
  68.1 0.7 fusion.28
  68.8 1.6 fusion.46
  70.4 1.0 gather_fusion.3
  71.4 1.0 fusion.7
  72.4 1.5 scatter_custom_fusion.2
  73.9 4.4 %all-to-all-start.3 = ((f32[128,2,128]{2,1,0:T(2,128)}), f32[128,2,128]{2,1,0:T(2,128)S(1)}, u32[]{:S(2)}, u32[]{:S(2)}) async-start(f32[128,2,128]{2,1,0:T(2,128)} %bitcast.26), calls=%async_computation.3 | async-start | bytes 262144 | tf_op jit(solution)/shard_map/all_to_all | solution.py:161
  78.3 0.1 eq.85
  78.4 0.2 compare_reduce_fusion
  78.7 0.1 eq.91
  78.8 10.6 %all-to-all-done.3 = f32[128,2,128]{2,1,0:T(2,128)S(1)} async-done(((f32[128,2,128]{2,1,0:T(2,128)}), f32[128,2,128]{2,1,0:T(2,128)S(1)}, u32[]{:S(2)}, u32[]{:S(2)}) %all-to-all-start.3) | async-done | bytes 131104 | tf_op jit(solution)/shard_map/all_to_all | solution.py:161
  89.4 0.2 fusion.32
  89.6 1.2 fusion.47
  90.8 0.7 multiply_subtract_fusion.1
  91.5 1.1 fusion.48
  92.6 0.7 gather_fusion.4
  93.4 14.6 %all_to_all.35 = f32[128,2,128]{2,1,0:T(2,128)S(1)} all-to-all(f32[128,2,128]{2,1,0:T(2,128)S(1)} %bitcast.109), channel_id=1, replica_groups=mesh['slave'=16,'master'=8] {'slave','master'}, dimensions={0} | all-to-all | bytes 262144 | tf_op jit(solution)/shard_map/all_to_all | solution.py:145
  108.0 0.6 gather_fusion.5
  108.6 1.0 gather_fusion.6
  109.7 0.2 fusion.5
  109.9 0.9 fusion.49
  110.8 7.9 %all_to_all.36 = f32[8,16,128]{2,1,0:T(8,128)S(1)} all-to-all(f32[8,16,128]{2,1,0:T(8,128)S(1)} %broadcast_in_dim.17), channel_id=1, replica_groups=mesh['slave'=16,'master'=8] {'master'}, dimensions={0} | all-to-all | bytes 131072 | tf_op jit(solution)/shard_map/all_to_all | solution.py:70
  118.8 0.0 copy-start.4
  118.8 0.5 fusion.50
  119.3 1.0 gather_fusion.7
  120.4 0.3 fusion.3
  120.7 1.5 scatter_custom_fusion.3
  122.2 4.4 %all-to-all-start.6 = ((f32[128,2,128]{2,1,0:T(2,128)}), f32[128,2,128]{2,1,0:T(2,128)S(1)}, u32[]{:S(2)}, u32[]{:S(2)}) async-start(f32[128,2,128]{2,1,0:T(2,128)} %bitcast.46), calls=%async_computation.6 | async-start | bytes 262144 | tf_op jit(solution)/shard_map/all_to_all | solution.py:161
  126.6 10.1 %all-to-all-done.6 = f32[128,2,128]{2,1,0:T(2,128)S(1)} async-done(((f32[128,2,128]{2,1,0:T(2,128)}), f32[128,2,128]{2,1,0:T(2,128)S(1)}, u32[]{:S(2)}, u32[]{:S(2)}) %all-to-all-start.6) | async-done | bytes 131104 | tf_op jit(solution)/shard_map/all_to_all | solution.py:161
  136.6 0.2 fusion.30
  136.8 0.3 fusion.51
  137.1 0.6 multiply_subtract_fusion
  137.7 18.0 %shard_map.139 = bf16[512,128,128]{2,1,0:T(8,128)(2,1)} custom-call(s32[512]{0:T(512)S(1)} %copy-done.1, s32[512]{0:T(512)S(1)} %copy-done.2, s32[128]{0:T(128)S(1)} %multiply_add_fusion.mreq_ref, bf16[16,128,128]{2,1,0:T(8,128)(2,1)S(1)} %copy-done, bf16[512,128,128]{2,1,0:T(8,128)(2,1)} %all-gather.2.cloned.1.call-done.basis_hbm, f32[512,128]{1,0:T(8,128)S(1)} %fusion.11.w_ref), custom_call_target="tpu_custom_call" | custom-call | tf_op jit(solution)/shard_map/pallas_call | solution.py:57
  (29 shorter events, 0.2 us)
Async XLA Ops:
  7.2 129.6 %copy-start.3 = (bf16[4,128,128]{2,1,0:T(8,128)(2,1)S(1)}, bf16[4,128,128]{2,1,0:T(8,128)(2,1)}, u32[]{:S(2)}) copy-start(bf16[4,128,128]{2,1,0:T(8,128)(2,1)} %param.13) | copy-start | bytes 393220
  7.2 119.3 %copy-start.6 = (s32[128,1]{0,1:T(1,128)S(1)}, s32[128,1]{0,1:T(1,128)}, u32[]{:S(2)}) copy-start(s32[128,1]{0,1:T(1,128)} %param.18) | copy-start | bytes 1540
  7.2 119.3 %copy-start.7 = (s32[128]{0:T(128)S(1)}, s32[128]{0:T(128)}, u32[]{:S(2)}) copy-start(s32[128]{0:T(128)} %param.19) | copy-start | bytes 1540
  7.2 102.5 %copy-start.1 = (s32[512]{0:T(512)S(1)}, s32[512]{0:T(512)}, u32[]{:S(2)}) copy-start(s32[512]{0:T(512)} %sidx_ref.1) | copy-start | bytes 6148
  7.2 102.7 %copy-start = (bf16[16,128,128]{2,1,0:T(8,128)(2,1)S(1)}, bf16[16,128,128]{2,1,0:T(8,128)(2,1)}, u32[]{:S(2)}) copy-start(bf16[16,128,128]{2,1,0:T(8,128)(2,1)} %slave_ref.1) | copy-start | bytes 1572868
  7.2 113.1 %copy-start.2 = (s32[512]{0:T(512)S(1)}, s32[512]{0:T(512)}, u32[]{:S(2)}) copy-start(s32[512]{0:T(512)} %nidx_ref.1) | copy-start | bytes 6148
  7.2 111.5 %copy-start.5 = (f32[16,128]{1,0:T(8,128)S(1)}, f32[16,128]{1,0:T(8,128)}, u32[]{:S(2)}) copy-start(f32[16,128]{1,0:T(8,128)} %param.14) | copy-start | bytes 24580
  7.2 130.5 %all-gather.2.cloned.1.call-start = ((), (), s32[]{:S(2)}) async-start(), calls=%async_computation.7 | async-start | bytes 16908288 | tf_op jit(solution)/shard_map/all_gather | solution.py:97
  13.6 21.9 %all-to-all-start = ((s32[2,128,2]{2,0,1:T(2,128)}), s32[2,128,2]{2,0,1:T(2,128)S(1)}, u32[]{:S(2)}, u32[]{:S(2)}) async-start(s32[2,128,2]{2,0,1:T(2,128)} %copy.18), calls=%async_computation | async-start | bytes 262144 | tf_op jit(solution)/shard_map/all_to_all | solution.py:105
  37.1 16.6 %all-to-all-start.1 = ((f32[128,2,128]{2,1,0:T(2,128)}), f32[128,2,128]{2,1,0:T(2,128)S(1)}, u32[]{:S(2)}, u32[]{:S(2)}) async-start(f32[128,2,128]{2,1,0:T(2,128)} %bitcast.13), calls=%async_computation.1 | async-start | bytes 262144 | tf_op jit(solution)/shard_map/all_to_all | solution.py:145
  59.0 9.0 %all-to-all-start.2 = ((f32[8,2,16,128]{3,2,1,0:T(8,128)}), f32[8,2,16,128]{3,2,1,0:T(8,128)S(1)}, u32[]{:S(2)}, u32[]{:S(2)}) async-start(f32[8,2,16,128]{3,2,1,0:T(8,128)} %broadcast_in_dim.15), calls=%async_computation.2 | async-start | bytes 262144 | tf_op jit(solution)/shard_map/all_to_all | solution.py:70
  73.9 15.6 %all-to-all-start.3 = ((f32[128,2,128]{2,1,0:T(2,128)}), f32[128,2,128]{2,1,0:T(2,128)S(1)}, u32[]{:S(2)}, u32[]{:S(2)}) async-start(f32[128,2,128]{2,1,0:T(2,128)} %bitcast.26), calls=%async_computation.3 | async-start | bytes 262144 | tf_op jit(solution)/shard_map/all_to_all | solution.py:161
  118.8 36.9 %copy-start.4 = (f32[16,128]{1,0:T(8,128)}, f32[16,128]{1,0:T(8,128)S(1)}, u32[]{:S(2)}) copy-start(f32[16,128]{1,0:T(8,128)S(1)} %subtract_select_fusion) | copy-start | bytes 24580
  122.2 14.5 %all-to-all-start.6 = ((f32[128,2,128]{2,1,0:T(2,128)}), f32[128,2,128]{2,1,0:T(2,128)S(1)}, u32[]{:S(2)}, u32[]{:S(2)}) async-start(f32[128,2,128]{2,1,0:T(2,128)} %bitcast.46), calls=%async_computation.6 | async-start | bytes 262144 | tf_op jit(solution)/shard_map/all_to_all | solution.py:161
Sparse Core Ops, SparseCore 0:
  11.2 85.5 all-gather.1

commit v3 on v2

--- a/solution.py
+++ b/solution.py
@@ -54,6 +54,11 @@
             pltpu.SemaphoreType.DMA((need,)),
         ],
     )
+    cost = pl.CostEstimate(
+        flops=2 * pairs * nodes * nodes * qpts,
+        bytes_accessed=pairs * nodes * nodes * 2 + need * nodes * qpts * 2 + pairs * qpts * 4,
+        transcendentals=0,
+    )
     return pl.pallas_call(
         functools.partial(tile_kernel, group),
         grid_spec=grid_spec,
@@ -61,6 +66,7 @@
         compiler_params=pltpu.CompilerParams(
             vmem_limit_bytes=48 * 1024 * 1024, dimension_semantics=("arbitrary",)
         ),
+        cost_estimate=cost,
     )(pair_slave, pair_need, request, slave_basis, every_basis, weights)
 
 
@@ -90,27 +96,10 @@
     peers = lax.axis_size(everyone)
     mb_dev = master_basis.shape[0]
     need_dev = need_slot.shape[0]
-    cap = 2 * need_dev // peers
     qpts = slave_basis.shape[2]
     owner = need_owner[:, 0]
     request = owner * mb_dev + need_slot
     every_basis = lax.all_gather(master_basis, everyone, axis=0, tiled=True)
-
-    match = (owner[:, None] == jnp.arange(peers, dtype=jnp.int32)[None, :]).astype(jnp.int32)
-    earlier = jnp.cumsum(match, axis=0) - match
-    rank = jnp.sum(earlier * match, axis=1)
-    position = owner * cap + rank
-    slots = jnp.zeros((peers * cap,), jnp.int32).at[position].set(need_slot)
-    filled = jnp.zeros((peers * cap,), jnp.int32).at[position].set(1)
-    asked = lax.all_to_all(
-        jnp.stack([slots, filled]).reshape(2, peers, cap),
-        everyone,
-        split_axis=1,
-        concat_axis=1,
-        tiled=True,
-    )
-    wanted = asked[0].reshape(-1)
-    present = asked[1].reshape(-1)
 
     limit = GAUSS * pair_segs
     weights = jnp.where(
@@ -125,9 +114,10 @@
     need_onehot = (pair_need[None, :] == jnp.arange(need_dev, dtype=jnp.int32)[:, None]).astype(
         jnp.float32
     )
-    owner_onehot = (
-        (wanted[None, :] == jnp.arange(mb_dev, dtype=jnp.int32)[:, None]) & (present[None, :] == 1)
-    ).astype(jnp.float32)
+    mblocks = peers * mb_dev
+    block_onehot = (request[None, :] == jnp.arange(mblocks, dtype=jnp.int32)[:, None]).astype(
+        jnp.float32
+    )
     slave_weight = jnp.dot(slave_onehot, weights, precision=high)
     slave_float = slave_basis.astype(jnp.float32)
     master_float = master_basis.astype(jnp.float32)
@@ -141,9 +131,9 @@
     root_lump = None
     for update in range(ITERS):
         own_proj = jnp.einsum("mnq,mn->mq", master_float, disp, precision=high)
-        outgoing_proj = own_proj[wanted].reshape(peers, cap, qpts)
+        outgoing_proj = jnp.broadcast_to(own_proj[None], (peers,) + own_proj.shape)
         returned = lax.all_to_all(outgoing_proj, everyone, split_axis=0, concat_axis=0, tiled=True)
-        need_proj = returned.reshape(peers * cap, qpts)[position]
+        need_proj = returned.reshape(mblocks, qpts)[request]
         pair_terms = weights * need_proj[pair_need]
         slave_terms = jnp.dot(slave_onehot, pair_terms, precision=high)
         partial_coupled = jnp.einsum("snq,sq->sn", slave_float, slave_terms, precision=high)
@@ -157,11 +147,11 @@
         lam = jnp.where(flags, lam - 1.0 * gap, jnp.zeros_like(lam))
         slave_proj = jnp.einsum("snq,sn->sq", slave_float, lam, precision=high)
         need_load = jnp.dot(need_onehot, weights * slave_proj[pair_slave], precision=high)
-        outbound = jnp.zeros((peers * cap, qpts), jnp.float32).at[position].set(need_load)
+        outbound = jnp.dot(block_onehot, need_load, precision=high)
         inbound = lax.all_to_all(
-            outbound.reshape(peers, cap, qpts), everyone, split_axis=0, concat_axis=0, tiled=True
+            outbound.reshape(peers, mb_dev, qpts), everyone, split_axis=0, concat_axis=0, tiled=True
         )
-        own_load = jnp.dot(owner_onehot, inbound.reshape(peers * cap, qpts), precision=high)
+        own_load = jnp.sum(inbound, axis=0)
         force = jnp.einsum("mnq,mq->mn", master_float, own_load, precision=high)
         disp = disp - 0.05 * force
     return (lam, disp, stored)

time: 164 us -> 145 us (0.88)
  blocking collectives: 22.5 us -> 57 us
  waiting for transfers between devices: 39 us -> 9.42 us
  starting transfers between devices: 30.7 us -> 15.6 us
  local copies, waits for them, and re-layouts: 14.9 us -> 6.97 us
  matrix products: 15 us -> 17 us
  other arithmetic: 7.99 us -> 6.24 us
    all_to_all x0 -> x2, blocking collectives: none -> 30.4 us  [on_device(): lax.all_to_all(outbound.reshape(peers, mb_dev, qpts), everyone, split_axi...]
    all_to_all x3 -> x0, waiting for transfers between devices: 23.8 us -> none  [the longest x2 20.7 us: on_device(): lax.all_to_all(outbound.reshape(peers, cap, qpts), everyone, split_axis=0...]
    all_to_all x3 -> x0, starting transfers between devices: 20.2 us -> none  [the longest x1 11.5 us: on_device(): lax.all_to_all(jnp.stack([slots, filled]).reshape(2, peers, cap), everyon...]
    all_to_all x1, waiting for transfers between devices: 9.95 us -> 4.16 us  [on_device(): lax.all_to_all(outgoing_proj, everyone, split_axis=0, concat_axis=0, tile...]
    scatter x4 -> x0, local copies, waits for them, and re-layouts: 5.05 us -> none  [the longest x2 2.97 us: on_device(): jnp.zeros((peers * cap, qpts), jnp.float32).at[position].set(need_load)]
    all_to_all x1, starting transfers between devices: 6.64 us -> 11.5 us  [on_device(): lax.all_to_all(outgoing_proj, everyone, split_axis=0, concat_axis=0, tile...]
    all_to_all x1, blocking collectives: 14.6 us -> 18.2 us  [on_device(): lax.all_to_all(outgoing_proj, everyone, split_axis=0, concat_axis=0, tile...]
    gather x4 -> x2, local copies, waits for them, and re-layouts: 3.38 us -> 1.29 us  [on_device(): need_proj = returned.reshape(mblocks, qpts)[request]]
  transfers between devices with their start and end apart: 6 -> 3, of which waited for: 5 -> 2; matrix products, arithmetic and copies ran while one was open for 23% -> 21% of each run, Pallas kernels for 0% -> 0%
where the time goes in v3:
time: 145 us; the launch traced here: 144 us
  blocking collectives  57 us (39%)
  Pallas kernels  17.9 us (12%)
  matrix products  17 us (12%)
  starting transfers between devices  15.6 us (11%)
  between operations  14.3 us (10%)
  waiting for transfers between devices  9.42 us (6%)
  local copies, waits for them, and re-layouts  6.97 us (5%)
  other arithmetic  6.24 us (4%)
    all_to_all x2, blocking collectives, on_device(): lax.all_to_all(outbound.reshape(peers, mb_dev, qpts), everyone, split_axi...  30.4 us
    all_to_all x1, blocking collectives, on_device(): lax.all_to_all(outgoing_proj, everyone, split_axis=0, concat_axis=0, tile...  18.2 us
    pallas_call x1, Pallas kernels, build_tiles(): pl.pallas_call(functools.partial(tile_kernel, group), grid_spec=grid_spec...  17.9 us
    all_to_all x1, starting transfers between devices, on_device(): lax.all_to_all(outgoing_proj, everyone, split_axis=0, concat_axis=0, tile...  11.5 us
    all_to_all x1, blocking collectives, master_sum(): lax.all_to_all(spread, 'master', split_axis=0, concat_axis=0, tiled=True)  8.36 us
    all_to_all x1, waiting for transfers between devices, master_sum(): lax.all_to_all(spread, 'master', split_axis=0, concat_axis=0, tiled=True)  4.57 us
    all_to_all x1, waiting for transfers between devices, on_device(): lax.all_to_all(outgoing_proj, everyone, split_axis=0, concat_axis=0, tile...  4.16 us
    all_to_all x1, starting transfers between devices, master_sum(): lax.all_to_all(spread, 'master', split_axis=0, concat_axis=0, tiled=True)  4.03 us
  transfers between devices with their start and end apart: 3, of which 2 were waited for; matrix products, arithmetic and copies ran while one was open for 21% of the time, Pallas kernels for 0%

profile of v3, /device:TPU:1, one launch (start us, length us, event | category | flops | bytes accessed | tf_op | source)
XLA Modules:
  0.0 144.4 jit_solution(13389733791480531437)
XLA Ops:
  7.2 0.0 copy-start.3
  7.2 0.0 copy-start.2
  7.2 0.0 copy-start.1
  7.2 0.0 copy-start
  7.2 0.0 copy-start.5
  7.2 0.0 all-gather.2.cloned.1.call-start
  7.3 0.7 all-gather.2.cloned.1.call-update
  8.0 1.1 fusion.28
  9.1 0.8 broadcast_in_dim.17
  9.8 11.5 %all-to-all-start = ((f32[128,4,128]{2,1,0:T(4,128)}), f32[128,4,128]{2,1,0:T(4,128)S(1)}, u32[]{:S(2)}, u32[]{:S(2)}) async-start(f32[128,4,128]{2,1,0:T(4,128)} %broadcast_in_dim.17), calls=%async_computation | async-start | bytes 524288 | tf_op jit(solution)/shard_map/all_to_all | solution.py:135
  21.3 0.7 compare_select_fusion.2
  22.0 0.7 broadcast_multiply_fusion
  22.7 0.7 compare_select_fusion.1
  23.4 1.1 fusion.13.w_ref
  24.5 0.9 fusion.18
  25.4 2.8 %fusion = f32[16,1,128]{2,1,0:T(1,128)S(1)} fusion(f32[16,128,1]{1,2,0:T(1,128)S(1)} %bitcast.110, bf16[16,128,128]{2,1,0:T(8,128)(2,1)} %slave_ref.1), kind=kOutput, calls=%fused_computation.6 | convolution fusion | flops 3670016 | bytes 540672 | tf_op jit(solution)/shard_map/snq,sq->sn/dot_general | solution.py:125
  28.2 4.2 %all-to-all-done = f32[128,4,128]{2,1,0:T(4,128)S(1)} async-done(((f32[128,4,128]{2,1,0:T(4,128)}), f32[128,4,128]{2,1,0:T(4,128)S(1)}, u32[]{:S(2)}, u32[]{:S(2)}) %all-to-all-start) | async-done | bytes 262176 | tf_op jit(solution)/shard_map/all_to_all | solution.py:135
  32.3 0.6 gather_fusion
  33.0 1.0 gather_fusion.1
  34.0 0.9 fusion.11
  34.9 1.9 %fusion.29 = f32[16,1,128]{2,1,0:T(1,128)S(1)} fusion(f32[16,128,1]{1,2,0:T(1,128)S(1)} %bitcast.97, bf16[16,128,128]{2,1,0:T(8,128)(2,1)} %slave_ref.1), kind=kOutput, calls=%fused_computation.54 | convolution fusion | flops 3145728 | bytes 540672 | tf_op jit(solution)/shard_map/snq,sq->sn/dot_general | solution.py:139
  36.9 0.7 broadcast_in_dim.20
  37.6 4.0 %all-to-all-start.1 = ((f32[8,2,16,128]{3,2,1,0:T(8,128)}), f32[8,2,16,128]{3,2,1,0:T(8,128)S(1)}, u32[]{:S(2)}, u32[]{:S(2)}) async-start(f32[8,2,16,128]{3,2,1,0:T(8,128)} %broadcast_in_dim.20), calls=%async_computation.1 | async-start | bytes 262144 | tf_op jit(solution)/shard_map/all_to_all | solution.py:76
  41.6 0.7 compare_select_fusion
  42.3 4.6 %all-to-all-done.1 = f32[8,2,16,128]{3,2,1,0:T(8,128)S(1)} async-done(((f32[8,2,16,128]{3,2,1,0:T(8,128)}), f32[8,2,16,128]{3,2,1,0:T(8,128)S(1)}, u32[]{:S(2)}, u32[]{:S(2)}) %all-to-all-start.1) | async-done | bytes 131104 | tf_op jit(solution)/shard_map/all_to_all | solution.py:76
  46.9 0.7 fusion.27
  47.6 1.6 %fusion.30 = f32[16,1,128]{2,1,0:T(1,128)S(1)} fusion(f32[16,128,1]{1,2,0:T(1,128)S(1)} %bitcast.96, bf16[16,128,128]{2,1,0:T(8,128)(2,1)} %slave_ref.1), kind=kOutput, calls=%fused_computation.55 | convolution fusion | flops 3145728 | bytes 540672 | tf_op jit(solution)/shard_map/snq,sn->sq/dot_general | solution.py:148
  49.2 1.0 gather_fusion.2
  50.2 1.0 fusion.7
  51.2 0.3 fusion.10
  51.5 15.5 %all_to_all.30 = f32[128,4,128]{2,1,0:T(4,128)S(1)} all-to-all(f32[128,4,128]{2,1,0:T(4,128)S(1)} %bitcast.94), channel_id=1, replica_groups=mesh['slave'=16,'master'=8] {'slave','master'}, dimensions={0} | all-to-all | bytes 524288 | tf_op jit(solution)/shard_map/all_to_all | solution.py:151
  67.0 0.1 reduce_sum.37
  67.2 1.3 fusion.31
  68.4 0.7 multiply_subtract_fusion.1
  69.1 1.1 fusion.32
  70.3 18.2 %all_to_all.31 = f32[128,4,128]{2,1,0:T(4,128)S(1)} all-to-all(f32[128,4,128]{2,1,0:T(4,128)S(1)} %broadcast_in_dim.22), channel_id=1, replica_groups=mesh['slave'=16,'master'=8] {'slave','master'}, dimensions={0} | all-to-all | bytes 524288 | tf_op jit(solution)/shard_map/all_to_all | solution.py:135
  88.5 0.6 gather_fusion.3
  89.2 1.0 gather_fusion.4
  90.2 0.9 fusion.5
  91.1 1.9 %fusion.33 = f32[16,1,128]{2,1,0:T(1,128)S(1)} fusion(f32[16,128,1]{1,2,0:T(1,128)S(1)} %bitcast.98, bf16[16,128,128]{2,1,0:T(8,128)(2,1)} %slave_ref.1), kind=kOutput, calls=%fused_computation.58 | convolution fusion | flops 3145728 | bytes 540672 | tf_op jit(solution)/shard_map/snq,sq->sn/dot_general | solution.py:139
  93.1 8.4 %all_to_all.32 = f32[8,16,128]{2,1,0:T(8,128)S(1)} all-to-all(f32[8,16,128]{2,1,0:T(8,128)S(1)} %broadcast_in_dim.23), channel_id=1, replica_groups=mesh['slave'=16,'master'=8] {'master'}, dimensions={0} | all-to-all | bytes 131072 | tf_op jit(solution)/shard_map/all_to_all | solution.py:76
  101.5 0.0 copy-done.5
  101.5 0.0 copy-start.4
  101.5 0.0 copy-done
  101.5 0.5 fusion.34
  102.0 1.0 gather_fusion.5
  103.1 0.0 copy-done.2
  103.1 0.3 fusion.3
  103.4 0.3 fusion.9
  103.7 14.9 %all_to_all.33 = f32[128,4,128]{2,1,0:T(4,128)S(1)} all-to-all(f32[128,4,128]{2,1,0:T(4,128)S(1)} %bitcast.95), channel_id=1, replica_groups=mesh['slave'=16,'master'=8] {'slave','master'}, dimensions={0} | all-to-all | bytes 524288 | tf_op jit(solution)/shard_map/all_to_all | solution.py:151
  118.5 0.1 reduce_sum.39
  118.7 0.0 copy-done.3
  118.7 0.3 fusion.35
  119.0 0.6 multiply_subtract_fusion
  119.6 0.0 all-gather.2.cloned.1.call-done.basis_hbm
  119.6 0.0 copy-done.1
  119.6 17.9 %shard_map.139 = bf16[512,128,128]{2,1,0:T(8,128)(2,1)} custom-call(s32[512]{0:T(512)S(1)} %copy-done.1, s32[512]{0:T(512)S(1)} %copy-done.2, s32[128]{0:T(128)S(1)} %get-tuple-element.6.mreq_ref, bf16[16,128,128]{2,1,0:T(8,128)(2,1)S(1)} %copy-done, bf16[512,128,128]{2,1,0:T(8,128)(2,1)} %all-gather.2.cloned.1.call-done.basis_hbm, f32[512,128]{1,0:T(8,128)S(1)} %fusion.13.w_ref), custom_call_target="tpu_custom_call" | custom-call | flops 2147483648 | bytes 21233664 | tf_op jit(solution)/shard_map/pallas_call | solution.py:62
  137.5 0.0 copy-done.4
  (9 shorter events, 0.1 us)
Async XLA Ops:
  7.2 111.5 %copy-start.3 = (bf16[4,128,128]{2,1,0:T(8,128)(2,1)S(1)}, bf16[4,128,128]{2,1,0:T(8,128)(2,1)}, u32[]{:S(2)}) copy-start(bf16[4,128,128]{2,1,0:T(8,128)(2,1)} %param.13) | copy-start | bytes 393220
  7.2 95.9 %copy-start.2 = (s32[512]{0:T(512)S(1)}, s32[512]{0:T(512)}, u32[]{:S(2)}) copy-start(s32[512]{0:T(512)} %nidx_ref.1) | copy-start | bytes 6148
  7.2 112.4 %copy-start.1 = (s32[512]{0:T(512)S(1)}, s32[512]{0:T(512)}, u32[]{:S(2)}) copy-start(s32[512]{0:T(512)} %sidx_ref.1) | copy-start | bytes 6148
  7.2 94.3 %copy-start = (bf16[16,128,128]{2,1,0:T(8,128)(2,1)S(1)}, bf16[16,128,128]{2,1,0:T(8,128)(2,1)}, u32[]{:S(2)}) copy-start(bf16[16,128,128]{2,1,0:T(8,128)(2,1)} %slave_ref.1) | copy-start | bytes 1572868
  7.2 94.2 %copy-start.5 = (f32[16,128]{1,0:T(8,128)S(1)}, f32[16,128]{1,0:T(8,128)}, u32[]{:S(2)}) copy-start(f32[16,128]{1,0:T(8,128)} %param.14) | copy-start | bytes 24580
  7.2 112.4 %all-gather.2.cloned.1.call-start = ((), (), s32[]{:S(2)}) async-start(), calls=%async_computation.6 | async-start | bytes 16908288 | tf_op jit(solution)/shard_map/all_gather | solution.py:102
  9.8 22.5 %all-to-all-start = ((f32[128,4,128]{2,1,0:T(4,128)}), f32[128,4,128]{2,1,0:T(4,128)S(1)}, u32[]{:S(2)}, u32[]{:S(2)}) async-start(f32[128,4,128]{2,1,0:T(4,128)} %broadcast_in_dim.17), calls=%async_computation | async-start | bytes 524288 | tf_op jit(solution)/shard_map/all_to_all | solution.py:135
  37.6 9.3 %all-to-all-start.1 = ((f32[8,2,16,128]{3,2,1,0:T(8,128)}), f32[8,2,16,128]{3,2,1,0:T(8,128)S(1)}, u32[]{:S(2)}, u32[]{:S(2)}) async-start(f32[8,2,16,128]{3,2,1,0:T(8,128)} %broadcast_in_dim.20), calls=%async_computation.1 | async-start | bytes 262144 | tf_op jit(solution)/shard_map/all_to_all | solution.py:76
  101.5 36.1 %copy-start.4 = (f32[16,128]{1,0:T(8,128)}, f32[16,128]{1,0:T(8,128)S(1)}, u32[]{:S(2)}) copy-start(f32[16,128]{1,0:T(8,128)S(1)} %subtract_select_fusion) | copy-start | bytes 24580
Sparse Core Ops, SparseCore 0:
  11.2 86.9 all-gather.1

commit v4 on v3

--- a/solution.py
+++ b/solution.py
@@ -70,10 +70,78 @@
     )(pair_slave, pair_need, request, slave_basis, every_basis, weights)
 
 
+def exchange_kernel(axes, sizes, spread, x_ref, o_ref, landed, send_sems, recv_sems):
+    n = 1
+    for s in sizes:
+        n *= s
+    me = 0
+    for a, s in zip(axes, sizes):
+        me = me * s + lax.axis_index(a)
+
+    def device_of(t):
+        coords = {}
+        for a, s in zip(reversed(axes), reversed(sizes)):
+            coords[a] = t % s
+            t = t // s
+        return tuple(coords[a] if a in coords else lax.axis_index(a) for a in ("slave", "master"))
+
+    def source(t):
+        return x_ref if spread else x_ref.at[t]
+
+    def start(k, carry):
+        t = lax.rem(me + k, n)
+        pltpu.make_async_remote_copy(
+            src_ref=source(t), dst_ref=landed.at[me], send_sem=send_sems.at[t],
+            recv_sem=recv_sems.at[me], device_id=device_of(t),
+            device_id_type=pl.DeviceIdType.MESH,
+        ).start()
+        return carry
+
+    lax.fori_loop(1, n, start, 0)
+    own = x_ref[...] if spread else x_ref[me]
+    o_ref[me] = own
+
+    def finish(k, carry):
+        t = lax.rem(me + k, n)
+        f = lax.rem(me + n - k, n)
+        pltpu.make_async_remote_copy(
+            src_ref=source(t), dst_ref=landed.at[me], send_sem=send_sems.at[t],
+            recv_sem=recv_sems.at[me], device_id=device_of(t),
+            device_id_type=pl.DeviceIdType.MESH,
+        ).wait_send()
+        pltpu.make_async_remote_copy(
+            src_ref=source(f), dst_ref=landed.at[f], send_sem=send_sems.at[f],
+            recv_sem=recv_sems.at[f], device_id=device_of(f),
+            device_id_type=pl.DeviceIdType.MESH,
+        ).wait_recv()
+        o_ref[f] = landed[f]
+        return carry
+
+    lax.fori_loop(1, n, finish, 0)
+
+
+def exchange(x, axes, sizes, spread):
+    n = 1
+    for s in sizes:
+        n *= s
+    piece = x.shape if spread else x.shape[1:]
+    return pl.pallas_call(
+        functools.partial(exchange_kernel, axes, sizes, spread),
+        out_shape=jax.ShapeDtypeStruct((n,) + piece, x.dtype),
+        in_specs=[pl.BlockSpec(memory_space=pltpu.VMEM)],
+        out_specs=pl.BlockSpec(memory_space=pltpu.VMEM),
+        scratch_shapes=[
+            pltpu.VMEM((n,) + piece, x.dtype),
+            pltpu.SemaphoreType.DMA((n,)),
+            pltpu.SemaphoreType.DMA((n,)),
+        ],
+        compiler_params=pltpu.CompilerParams(has_side_effects=True),
+    )(x)
+
+
 def master_sum(x):
     count = lax.axis_size("master")
-    spread = jnp.broadcast_to(x[None], (count,) + x.shape)
-    got = lax.all_to_all(spread, "master", split_axis=0, concat_axis=0, tiled=True)
+    got = exchange(x, ("master",), (count,), True)
     return jnp.sum(got, axis=0)
 
 
@@ -94,6 +162,7 @@
     high = lax.Precision.HIGHEST
     everyone = ("slave", "master")
     peers = lax.axis_size(everyone)
+    sizes = (lax.axis_size("slave"), lax.axis_size("master"))
     mb_dev = master_basis.shape[0]
     need_dev = need_slot.shape[0]
     qpts = slave_basis.shape[2]
@@ -131,8 +200,7 @@
     root_lump = None
     for update in range(ITERS):
         own_proj = jnp.einsum("mnq,mn->mq", master_float, disp, precision=high)
-        outgoing_proj = jnp.broadcast_to(own_proj[None], (peers,) + own_proj.shape)
-        returned = lax.all_to_all(outgoing_proj, everyone, split_axis=0, concat_axis=0, tiled=True)
+        returned = exchange(own_proj, everyone, sizes, True)
         need_proj = returned.reshape(mblocks, qpts)[request]
         pair_terms = weights * need_proj[pair_need]
         slave_terms = jnp.dot(slave_onehot, pair_terms, precision=high)
@@ -148,9 +216,7 @@
         slave_proj = jnp.einsum("snq,sn->sq", slave_float, lam, precision=high)
         need_load = jnp.dot(need_onehot, weights * slave_proj[pair_slave], precision=high)
         outbound = jnp.dot(block_onehot, need_load, precision=high)
-        inbound = lax.all_to_all(
-            outbound.reshape(peers, mb_dev, qpts), everyone, split_axis=0, concat_axis=0, tiled=True
-        )
+        inbound = exchange(outbound.reshape(peers, mb_dev, qpts), everyone, sizes, False)
         own_load = jnp.sum(inbound, axis=0)
         force = jnp.einsum("mnq,mq->mn", master_float, own_load, precision=high)
         disp = disp - 0.05 * force

time: 145 us -> 188 us (1.30)
  Pallas kernels: 17.9 us -> 133 us
  blocking collectives: 57 us -> 0 us
  starting transfers between devices: 15.6 us -> 0.04 us
  waiting for transfers between devices: 9.42 us -> 0.68 us
  other arithmetic: 6.24 us -> 11.2 us
  matrix products: 17 us -> 21.2 us
    pallas_call x0 -> x6, Pallas kernels: none -> 114 us  [exchange(): pl.pallas_call(functools.partial(exchange_kernel, axes, sizes, spread), o...]
    all_to_all x4 -> x0, blocking collectives: 57 us -> none  [the longest x2 30.4 us: on_device(): lax.all_to_all(outbound.reshape(peers, mb_dev, qpts), everyone, split_axi...]
    all_to_all x2 -> x0, starting transfers between devices: 15.5 us -> none  [the longest x1 11.5 us: on_device(): lax.all_to_all(outgoing_proj, everyone, split_axis=0, concat_axis=0, tile...]
    all_to_all x2 -> x0, waiting for transfers between devices: 8.73 us -> none  [the longest x1 4.57 us: master_sum(): lax.all_to_all(spread, 'master', split_axis=0, concat_axis=0, tiled=True)]
    reduce_sum x2, other arithmetic: 0.29 us -> 2.19 us  [on_device(): own_load = jnp.sum(inbound, axis=0)]
    gather x2, local copies, waits for them, and re-layouts: 1.29 us -> 3.19 us  [on_device(): need_proj = returned.reshape(mblocks, qpts)[request]]
  transfers between devices with their start and end apart: 3 -> 1, of which waited for: 2 -> 0; matrix products, arithmetic and copies ran while one was open for 21% -> 21% of each run, Pallas kernels for 0% -> 61%
where the time goes in v4:
time: 188 us; the launch traced here: 187 us
  Pallas kernels  133 us (71%)
  matrix products  21.2 us (11%)
  between operations  14.2 us (8%)
  other arithmetic  11.2 us (6%)
  local copies, waits for them, and re-layouts  7.35 us (4%)
    pallas_call x6, Pallas kernels, exchange(): pl.pallas_call(functools.partial(exchange_kernel, axes, sizes, spread), o...  114 us
    pallas_call x1, Pallas kernels, build_tiles(): pl.pallas_call(functools.partial(tile_kernel, group), grid_spec=grid_spec...  18.1 us
    dot_general x2, matrix products, on_device(): jnp.einsum('snq,sq->sn', slave_float, slave_terms, precision=high)  4.51 us
  transfers between devices with their start and end apart: 1, of which 0 were waited for; matrix products, arithmetic and copies ran while one was open for 21% of the time, Pallas kernels for 61%

profile of v4, /device:TPU:1, one launch (start us, length us, event | category | flops | bytes accessed | tf_op | source)
XLA Modules:
  0.0 187.3 jit_solution(4198384955039232115)
XLA Ops:
  7.2 0.0 copy-start.3
  7.2 0.0 copy-start.2
  7.2 0.0 copy-start.1
  7.2 0.0 copy-start
  7.2 0.0 all-gather.2.cloned.1.call-start
  7.3 0.7 all-gather.2.cloned.1.call-update
  7.9 1.7 fusion.28
  9.6 26.2 %shard_map.139 = f32[128,4,128]{2,1,0:T(4,128)} custom-call(f32[4,128]{1,0:T(4,128)} %bitcast.105), custom_call_target="tpu_custom_call" | custom-call | tf_op jit(solution)/shard_map/pallas_call | solution.py:128
  35.9 0.7 compare_select_fusion.2
  36.5 1.6 gather_fusion
  38.1 0.7 compare_select_fusion.1
  38.8 1.0 gather_fusion.1
  39.9 0.7 broadcast_multiply_fusion
  40.6 1.1 fusion.13.w_ref
  41.6 0.9 fusion.18
  42.5 0.9 fusion.11
  43.4 1.9 %fusion.29 = f32[16,1,128]{2,1,0:T(1,128)S(1)} fusion(f32[16,128,1]{1,2,0:T(1,128)S(1)} %bitcast.97, bf16[16,128,128]{2,1,0:T(8,128)(2,1)} %slave_ref.1), kind=kOutput, calls=%fused_computation.54 | convolution fusion | flops 3145728 | bytes 540672 | tf_op jit(solution)/shard_map/snq,sq->sn/dot_general | solution.py:207
  45.4 2.8 %fusion = f32[16,1,128]{2,1,0:T(1,128)S(1)} fusion(f32[16,128,1]{1,2,0:T(1,128)S(1)} %bitcast.110, bf16[16,128,128]{2,1,0:T(8,128)(2,1)} %slave_ref.1), kind=kOutput, calls=%fused_computation.6 | convolution fusion | flops 3670016 | bytes 540672 | tf_op jit(solution)/shard_map/snq,sq->sn/dot_general | solution.py:194
  48.2 0.6 pad_maximum_fusion.x_ref
  48.8 11.6 %shard_map.140 = f32[8,2,16,128]{3,2,1,0:T(8,128)} custom-call(f32[2,16,128]{2,1,0:T(8,128)} %pad_maximum_fusion.x_ref), custom_call_target="tpu_custom_call" | custom-call | tf_op jit(solution)/shard_map/pallas_call | solution.py:128
  60.4 0.9 reduce_sum.36
  61.3 0.7 compare_select_fusion
  62.0 0.7 fusion.27
  62.8 1.6 fusion.30
  64.3 1.0 gather_fusion.2
  65.4 1.0 fusion.7
  66.4 1.0 fusion.10
  67.3 23.2 %shard_map.141 = f32[128,4,128]{2,1,0:T(4,128)} custom-call(f32[128,4,128]{2,1,0:T(4,128)} %bitcast.94), custom_call_target="tpu_custom_call" | custom-call | tf_op jit(solution)/shard_map/pallas_call | solution.py:128
  90.5 1.1 reduce_sum.37
  91.6 1.2 fusion.31
  92.8 0.7 multiply_subtract_fusion.1
  93.5 1.7 fusion.32
  95.2 20.4 %shard_map.142 = f32[128,4,128]{2,1,0:T(4,128)} custom-call(f32[4,128]{1,0:T(4,128)} %bitcast.106), custom_call_target="tpu_custom_call" | custom-call | tf_op jit(solution)/shard_map/pallas_call | solution.py:128
  115.6 1.6 gather_fusion.3
  117.2 1.0 gather_fusion.4
  118.2 0.9 fusion.5
  119.1 2.6 %fusion.33 = f32[16,1,128]{2,1,0:T(1,128)} fusion(f32[16,128,1]{1,2,0:T(1,128)S(1)} %bitcast.98, bf16[16,128,128]{2,1,0:T(8,128)(2,1)} %slave_ref.1), kind=kOutput, calls=%fused_computation.58 | convolution fusion | flops 3145728 | bytes 540672 | tf_op jit(solution)/shard_map/snq,sq->sn/dot_general | solution.py:207
  121.7 10.3 %shard_map.143 = f32[8,16,128]{2,1,0:T(8,128)} custom-call(f32[16,128]{1,0:T(8,128)} %bitcast.99), custom_call_target="tpu_custom_call" | custom-call | tf_op jit(solution)/shard_map/pallas_call | solution.py:128
  132.0 0.9 reduce_sum.38
  132.9 0.7 subtract_select_fusion
  133.6 0.0 copy-start.4
  133.6 1.6 fusion.34
  135.1 1.0 gather_fusion.5
  136.2 0.0 copy-done.2
  136.2 0.3 fusion.3
  136.5 1.0 fusion.9
  137.5 22.8 %shard_map.144 = f32[128,4,128]{2,1,0:T(4,128)} custom-call(f32[128,4,128]{2,1,0:T(4,128)} %bitcast.95), custom_call_target="tpu_custom_call" | custom-call | tf_op jit(solution)/shard_map/pallas_call | solution.py:128
  160.3 1.1 reduce_sum.39
  161.4 0.0 copy-done.3
  161.4 0.3 fusion.35
  161.7 0.6 multiply_subtract_fusion
  162.3 0.0 all-gather.2.cloned.1.call-done.basis_hbm
  162.3 0.0 copy-done.1
  162.3 0.0 copy-done
  162.3 18.1 %shard_map.145 = bf16[512,128,128]{2,1,0:T(8,128)(2,1)} custom-call(s32[512]{0:T(512)S(1)} %copy-done.1, s32[512]{0:T(512)S(1)} %copy-done.2, s32[128]{0:T(128)S(1)} %get-tuple-element.6.mreq_ref, bf16[16,128,128]{2,1,0:T(8,128)(2,1)S(1)} %copy-done, bf16[512,128,128]{2,1,0:T(8,128)(2,1)} %all-gather.2.cloned.1.call-done.basis_hbm, f32[512,128]{1,0:T(8,128)S(1)} %fusion.13.w_ref), custom_call_target="tpu_custom_call" | custom-call | flops 2147483648 | bytes 21233664 | tf_op jit(solution)/shard_map/pallas_call | solution.py:62
  180.4 0.0 copy-done.4
  (3 shorter events, 0.0 us)
Async XLA Ops:
  7.2 154.2 %copy-start.3 = (bf16[4,128,128]{2,1,0:T(8,128)(2,1)S(1)}, bf16[4,128,128]{2,1,0:T(8,128)(2,1)}, u32[]{:S(2)}) copy-start(bf16[4,128,128]{2,1,0:T(8,128)(2,1)} %param.13) | copy-start | bytes 393220
  7.2 129.0 %copy-start.2 = (s32[512]{0:T(512)S(1)}, s32[512]{0:T(512)}, u32[]{:S(2)}) copy-start(s32[512]{0:T(512)} %nidx_ref.1) | copy-start | bytes 6148
  7.2 155.1 %copy-start.1 = (s32[512]{0:T(512)S(1)}, s32[512]{0:T(512)}, u32[]{:S(2)}) copy-start(s32[512]{0:T(512)} %sidx_ref.1) | copy-start | bytes 6148
  7.2 155.1 %copy-start = (bf16[16,128,128]{2,1,0:T(8,128)(2,1)S(1)}, bf16[16,128,128]{2,1,0:T(8,128)(2,1)}, u32[]{:S(2)}) copy-start(bf16[16,128,128]{2,1,0:T(8,128)(2,1)} %slave_ref.1) | copy-start | bytes 1572868
  7.2 155.1 %all-gather.2.cloned.1.call-start = ((), (), s32[]{:S(2)}) async-start(), calls=%async_computation | async-start | bytes 16908288 | tf_op jit(solution)/shard_map/all_gather | solution.py:171
  133.6 46.8 %copy-start.4 = (f32[16,128]{1,0:T(8,128)}, f32[16,128]{1,0:T(8,128)S(1)}, u32[]{:S(2)}) copy-start(f32[16,128]{1,0:T(8,128)S(1)} %subtract_select_fusion) | copy-start | bytes 24580
Sparse Core Ops, SparseCore 0:
  11.2 86.9 all-gather.1

commit v5 on v3

--- a/solution.py
+++ b/solution.py
@@ -151,6 +151,8 @@
         inbound = lax.all_to_all(
             outbound.reshape(peers, mb_dev, qpts), everyone, split_axis=0, concat_axis=0, tiled=True
         )
+        if update == ITERS - 1:
+            stored, inbound = lax.optimization_barrier((stored, inbound))
         own_load = jnp.sum(inbound, axis=0)
         force = jnp.einsum("mnq,mq->mn", master_float, own_load, precision=high)
         disp = disp - 0.05 * force

time: 145 us -> 135 us (0.931)
  blocking collectives: 57 us -> 42.1 us
  starting transfers between devices: 15.6 us -> 19.7 us
    all_to_all x2 -> x1, blocking collectives: 30.4 us -> 15.5 us  [on_device(): lax.all_to_all(outbound.reshape(peers, mb_dev, qpts), everyone, split_axi...]
    all_to_all x0 -> x1, starting transfers between devices: none -> 4.19 us  [on_device(): lax.all_to_all(outbound.reshape(peers, mb_dev, qpts), everyone, split_axi...]
  transfers between devices with their start and end apart: 3 -> 4, of which waited for: 2 -> 2; matrix products, arithmetic and copies ran while one was open for 21% -> 22% of each run, Pallas kernels for 0% -> 13%
where the time goes in v5:
time: 135 us; the launch traced here: 134 us
  blocking collectives  42.1 us (31%)
  starting transfers between devices  19.7 us (15%)
  Pallas kernels  17.9 us (13%)
  matrix products  17.7 us (13%)
  between operations  14.3 us (11%)
  waiting for transfers between devices  9.44 us (7%)
  local copies, waits for them, and re-layouts  6.97 us (5%)
  other arithmetic  6.24 us (5%)
    all_to_all x1, blocking collectives, on_device(): lax.all_to_all(outgoing_proj, everyone, split_axis=0, concat_axis=0, tile...  18.2 us
    pallas_call x1, Pallas kernels, build_tiles(): pl.pallas_call(functools.partial(tile_kernel, group), grid_spec=grid_spec...  17.9 us
    all_to_all x1, blocking collectives, on_device(): lax.all_to_all(outbound.reshape(peers, mb_dev, qpts), everyone, split_axi...  15.5 us
    all_to_all x1, starting transfers between devices, on_device(): lax.all_to_all(outgoing_proj, everyone, split_axis=0, concat_axis=0, tile...  11.5 us
    all_to_all x1, blocking collectives, master_sum(): lax.all_to_all(spread, 'master', split_axis=0, concat_axis=0, tiled=True)  8.36 us
    all_to_all x1, waiting for transfers between devices, master_sum(): lax.all_to_all(spread, 'master', split_axis=0, concat_axis=0, tiled=True)  4.57 us
    all_to_all x1, starting transfers between devices, on_device(): lax.all_to_all(outbound.reshape(peers, mb_dev, qpts), everyone, split_axi...  4.19 us
    all_to_all x1, waiting for transfers between devices, on_device(): lax.all_to_all(outgoing_proj, everyone, split_axis=0, concat_axis=0, tile...  4.16 us
  transfers between devices with their start and end apart: 4, of which 2 were waited for; matrix products, arithmetic and copies ran while one was open for 22% of the time, Pallas kernels for 13%

profile of v5, /device:TPU:1, one launch (start us, length us, event | category | flops | bytes accessed | tf_op | source)
XLA Modules:
  0.0 134.4 jit_solution(9017829607546793271)
XLA Ops:
  7.2 0.0 copy-start.2
  7.2 0.0 copy-start.1
  7.2 0.0 copy-start
  7.2 0.0 copy-start.5
  7.2 0.0 all-gather.2.cloned.1.call-start
  7.3 0.7 all-gather.2.cloned.1.call-update
  7.9 1.1 fusion.28
  9.1 0.8 broadcast_in_dim.17
  9.8 11.5 %all-to-all-start = ((f32[128,4,128]{2,1,0:T(4,128)}), f32[128,4,128]{2,1,0:T(4,128)S(1)}, u32[]{:S(2)}, u32[]{:S(2)}) async-start(f32[128,4,128]{2,1,0:T(4,128)} %broadcast_in_dim.17), calls=%async_computation | async-start | bytes 524288 | tf_op jit(solution)/shard_map/all_to_all | solution.py:135
  21.3 0.7 compare_select_fusion.1
  22.0 0.7 compare_select_fusion.2
  22.7 0.7 broadcast_multiply_fusion
  23.4 1.1 fusion.13.w_ref
  24.5 0.9 fusion.18
  25.4 2.8 %fusion = f32[16,1,128]{2,1,0:T(1,128)S(1)} fusion(f32[16,128,1]{1,2,0:T(1,128)S(1)} %bitcast.109, bf16[16,128,128]{2,1,0:T(8,128)(2,1)} %slave_ref.1), kind=kOutput, calls=%fused_computation.6 | convolution fusion | flops 3670016 | bytes 540672 | tf_op jit(solution)/shard_map/snq,sq->sn/dot_general | solution.py:125
  28.2 4.2 %all-to-all-done = f32[128,4,128]{2,1,0:T(4,128)S(1)} async-done(((f32[128,4,128]{2,1,0:T(4,128)}), f32[128,4,128]{2,1,0:T(4,128)S(1)}, u32[]{:S(2)}, u32[]{:S(2)}) %all-to-all-start) | async-done | bytes 262176 | tf_op jit(solution)/shard_map/all_to_all | solution.py:135
  32.3 0.6 gather_fusion
  33.0 1.0 gather_fusion.1
  34.0 0.9 fusion.11
  34.9 1.9 %fusion.29 = f32[16,1,128]{2,1,0:T(1,128)S(1)} fusion(f32[16,128,1]{1,2,0:T(1,128)S(1)} %bitcast.96, bf16[16,128,128]{2,1,0:T(8,128)(2,1)} %slave_ref.1), kind=kOutput, calls=%fused_computation.54 | convolution fusion | flops 3145728 | bytes 540672 | tf_op jit(solution)/shard_map/snq,sq->sn/dot_general | solution.py:139
  36.9 0.7 broadcast_in_dim.20
  37.6 4.0 %all-to-all-start.1 = ((f32[8,2,16,128]{3,2,1,0:T(8,128)}), f32[8,2,16,128]{3,2,1,0:T(8,128)S(1)}, u32[]{:S(2)}, u32[]{:S(2)}) async-start(f32[8,2,16,128]{3,2,1,0:T(8,128)} %broadcast_in_dim.20), calls=%async_computation.1 | async-start | bytes 262144 | tf_op jit(solution)/shard_map/all_to_all | solution.py:76
  41.6 0.7 compare_select_fusion
  42.3 4.6 %all-to-all-done.1 = f32[8,2,16,128]{3,2,1,0:T(8,128)S(1)} async-done(((f32[8,2,16,128]{3,2,1,0:T(8,128)}), f32[8,2,16,128]{3,2,1,0:T(8,128)S(1)}, u32[]{:S(2)}, u32[]{:S(2)}) %all-to-all-start.1) | async-done | bytes 131104 | tf_op jit(solution)/shard_map/all_to_all | solution.py:76
  46.9 0.7 fusion.27
  47.6 1.6 %fusion.30 = f32[16,1,128]{2,1,0:T(1,128)S(1)} fusion(f32[16,128,1]{1,2,0:T(1,128)S(1)} %bitcast.95, bf16[16,128,128]{2,1,0:T(8,128)(2,1)} %slave_ref.1), kind=kOutput, calls=%fused_computation.55 | convolution fusion | flops 3145728 | bytes 540672 | tf_op jit(solution)/shard_map/snq,sn->sq/dot_general | solution.py:148
  49.2 1.0 gather_fusion.2
  50.2 1.0 fusion.7
  51.2 0.3 fusion.10
  51.5 15.5 %all_to_all.30 = f32[128,4,128]{2,1,0:T(4,128)S(1)} all-to-all(f32[128,4,128]{2,1,0:T(4,128)S(1)} %bitcast.94), channel_id=1, replica_groups=mesh['slave'=16,'master'=8] {'slave','master'}, dimensions={0} | all-to-all | bytes 524288 | tf_op jit(solution)/shard_map/all_to_all | solution.py:151
  67.0 0.1 reduce_sum.37
  67.2 1.3 fusion.31
  68.4 0.7 multiply_subtract_fusion.1
  69.1 1.1 fusion.32
  70.3 18.2 %all_to_all.31 = f32[128,4,128]{2,1,0:T(4,128)S(1)} all-to-all(f32[128,4,128]{2,1,0:T(4,128)S(1)} %broadcast_in_dim.22), channel_id=1, replica_groups=mesh['slave'=16,'master'=8] {'slave','master'}, dimensions={0} | all-to-all | bytes 524288 | tf_op jit(solution)/shard_map/all_to_all | solution.py:135
  88.5 0.6 gather_fusion.3
  89.2 1.0 gather_fusion.4
  90.2 0.9 fusion.5
  91.1 1.9 %fusion.33 = f32[16,1,128]{2,1,0:T(1,128)S(1)} fusion(f32[16,128,1]{1,2,0:T(1,128)S(1)} %bitcast.97, bf16[16,128,128]{2,1,0:T(8,128)(2,1)} %slave_ref.1), kind=kOutput, calls=%fused_computation.58 | convolution fusion | flops 3145728 | bytes 540672 | tf_op jit(solution)/shard_map/snq,sq->sn/dot_general | solution.py:139
  93.1 8.4 %all_to_all.32 = f32[8,16,128]{2,1,0:T(8,128)S(1)} all-to-all(f32[8,16,128]{2,1,0:T(8,128)S(1)} %broadcast_in_dim.23), channel_id=1, replica_groups=mesh['slave'=16,'master'=8] {'master'}, dimensions={0} | all-to-all | bytes 131072 | tf_op jit(solution)/shard_map/all_to_all | solution.py:76
  101.4 0.0 copy-done.5
  101.5 0.0 copy-start.4
  101.5 0.0 copy-done
  101.5 0.5 fusion.34
  102.0 1.0 gather_fusion.5
  103.1 0.0 copy-done.2
  103.1 0.3 fusion.3
  103.4 1.0 fusion.9
  104.3 4.2 %all-to-all-start.5 = ((f32[128,4,128]{2,1,0:T(4,128)}), f32[128,4,128]{2,1,0:T(4,128)S(1)}, u32[]{:S(2)}, u32[]{:S(2)}) async-start(f32[128,4,128]{2,1,0:T(4,128)} %bitcast.40), calls=%async_computation.5 | async-start | bytes 524288 | tf_op jit(solution)/shard_map/all_to_all | solution.py:151
  108.5 0.0 copy-start.3
  108.6 0.0 all-gather.2.cloned.1.call-done.basis_hbm
  108.6 0.0 copy-done.1
  108.6 17.9 %shard_map.139 = bf16[512,128,128]{2,1,0:T(8,128)(2,1)} custom-call(s32[512]{0:T(512)S(1)} %copy-done.1, s32[512]{0:T(512)S(1)} %copy-done.2, s32[128]{0:T(128)S(1)} %get-tuple-element.10.mreq_ref, bf16[16,128,128]{2,1,0:T(8,128)(2,1)S(1)} %copy-done, bf16[512,128,128]{2,1,0:T(8,128)(2,1)} %all-gather.2.cloned.1.call-done.basis_hbm, f32[512,128]{1,0:T(8,128)S(1)} %fusion.13.w_ref), custom_call_target="tpu_custom_call" | custom-call | flops 2147483648 | bytes 21233664 | tf_op jit(solution)/shard_map/pallas_call | solution.py:62
  126.5 0.0 copy-done.4
  126.5 0.0 all-to-all-done.5
  126.6 0.1 reduce_sum.39
  126.7 0.0 copy-done.3
  126.7 0.3 fusion.35
  127.0 0.6 multiply_subtract_fusion
  (9 shorter events, 0.1 us)
Async XLA Ops:
  7.2 95.9 %copy-start.2 = (s32[512]{0:T(512)S(1)}, s32[512]{0:T(512)}, u32[]{:S(2)}) copy-start(s32[512]{0:T(512)} %nidx_ref.1) | copy-start | bytes 6148
  7.2 101.4 %copy-start.1 = (s32[512]{0:T(512)S(1)}, s32[512]{0:T(512)}, u32[]{:S(2)}) copy-start(s32[512]{0:T(512)} %sidx_ref.1) | copy-start | bytes 6148
  7.2 94.3 %copy-start = (bf16[16,128,128]{2,1,0:T(8,128)(2,1)S(1)}, bf16[16,128,128]{2,1,0:T(8,128)(2,1)}, u32[]{:S(2)}) copy-start(bf16[16,128,128]{2,1,0:T(8,128)(2,1)} %slave_ref.1) | copy-start | bytes 1572868
  7.2 94.2 %copy-start.5 = (f32[16,128]{1,0:T(8,128)S(1)}, f32[16,128]{1,0:T(8,128)}, u32[]{:S(2)}) copy-start(f32[16,128]{1,0:T(8,128)} %param.14) | copy-start | bytes 24580
  7.2 101.4 %all-gather.2.cloned.1.call-start = ((), (), s32[]{:S(2)}) async-start(), calls=%async_computation.6 | async-start | bytes 16908288 | tf_op jit(solution)/shard_map/all_gather | solution.py:102
  9.8 22.5 %all-to-all-start = ((f32[128,4,128]{2,1,0:T(4,128)}), f32[128,4,128]{2,1,0:T(4,128)S(1)}, u32[]{:S(2)}, u32[]{:S(2)}) async-start(f32[128,4,128]{2,1,0:T(4,128)} %broadcast_in_dim.17), calls=%async_computation | async-start | bytes 524288 | tf_op jit(solution)/shard_map/all_to_all | solution.py:135
  37.6 9.3 %all-to-all-start.1 = ((f32[8,2,16,128]{3,2,1,0:T(8,128)}), f32[8,2,16,128]{3,2,1,0:T(8,128)S(1)}, u32[]{:S(2)}, u32[]{:S(2)}) async-start(f32[8,2,16,128]{3,2,1,0:T(8,128)} %broadcast_in_dim.20), calls=%async_computation.1 | async-start | bytes 262144 | tf_op jit(solution)/shard_map/all_to_all | solution.py:76
  101.5 25.1 %copy-start.4 = (f32[16,128]{1,0:T(8,128)}, f32[16,128]{1,0:T(8,128)S(1)}, u32[]{:S(2)}) copy-start(f32[16,128]{1,0:T(8,128)S(1)} %subtract_select_fusion) | copy-start | bytes 24580
  104.3 22.2 %all-to-all-start.5 = ((f32[128,4,128]{2,1,0:T(4,128)}), f32[128,4,128]{2,1,0:T(4,128)S(1)}, u32[]{:S(2)}, u32[]{:S(2)}) async-start(f32[128,4,128]{2,1,0:T(4,128)} %bitcast.40), calls=%async_computation.5 | async-start | bytes 524288 | tf_op jit(solution)/shard_map/all_to_all | solution.py:151
  108.5 18.2 %copy-start.3 = (bf16[4,128,128]{2,1,0:T(8,128)(2,1)S(1)}, bf16[4,128,128]{2,1,0:T(8,128)(2,1)}, u32[]{:S(2)}) copy-start(bf16[4,128,128]{2,1,0:T(8,128)(2,1)} %param.13) | copy-start | bytes 393220
Sparse Core Ops, SparseCore 0:
  11.2 87.0 all-gather.1

commit v6 on v5

--- a/solution.py
+++ b/solution.py
@@ -12,7 +12,8 @@
 GROUP = 64
 
 
-def tile_kernel(group, sidx_ref, nidx_ref, mreq_ref, slave_ref, basis_hbm, w_ref, out_ref, recv, sems):
+def tile_kernel(group, first, sidx_ref, nidx_ref, mreq_ref, slave_ref, basis_hbm, w_ref, *rest):
+    out_ref, recv, sems = rest[-3:]
     need = recv.shape[0]
 
     @pl.when(pl.program_id(0) == 0)
@@ -22,7 +23,7 @@
         for r in range(need):
             pltpu.make_async_copy(basis_hbm.at[0], recv.at[r], sems.at[r]).wait()
 
-    base = pl.program_id(0) * group
+    base = (pl.program_id(0) + first) * group
     for g in range(group):
         s = sidx_ref[base + g]
         r = nidx_ref[base + g]
@@ -35,46 +36,58 @@
         out_ref[g] = tile.astype(out_ref.dtype)
 
 
-def build_tiles(slave_basis, every_basis, request, pair_slave, pair_need, weights):
+def build_tiles(slave_basis, every_basis, request, pair_slave, pair_need, weights, part, into=None):
     pairs = weights.shape[0]
     nodes, qpts = slave_basis.shape[1], slave_basis.shape[2]
     need = request.shape[0]
     group = GROUP
+    steps = pairs // group // 2
+    first = part * steps
+    extra = [] if into is None else [pl.BlockSpec(memory_space=pl.ANY)]
     grid_spec = pltpu.PrefetchScalarGridSpec(
         num_scalar_prefetch=3,
-        grid=(pairs // group,),
+        grid=(steps,),
         in_specs=[
             pl.BlockSpec(slave_basis.shape, lambda i, s, n, m: (0, 0, 0)),
             pl.BlockSpec(memory_space=pl.ANY),
-            pl.BlockSpec((group, qpts), lambda i, s, n, m: (i, 0)),
-        ],
-        out_specs=pl.BlockSpec((group, nodes, nodes), lambda i, s, n, m: (i, 0, 0)),
+            pl.BlockSpec((group, qpts), lambda i, s, n, m: (i + first, 0)),
+        ]
+        + extra,
+        out_specs=pl.BlockSpec((group, nodes, nodes), lambda i, s, n, m: (i + first, 0, 0)),
         scratch_shapes=[
             pltpu.VMEM((need, nodes, qpts), jnp.bfloat16),
             pltpu.SemaphoreType.DMA((need,)),
         ],
     )
     cost = pl.CostEstimate(
-        flops=2 * pairs * nodes * nodes * qpts,
-        bytes_accessed=pairs * nodes * nodes * 2 + need * nodes * qpts * 2 + pairs * qpts * 4,
+        flops=pairs * nodes * nodes * qpts,
+        bytes_accessed=pairs * nodes * nodes + need * nodes * qpts * 2 + pairs * qpts * 2,
         transcendentals=0,
     )
+    operands = [pair_slave, pair_need, request, slave_basis, every_basis, weights]
+    aliases = {}
+    if into is not None:
+        aliases = {len(operands): 0}
+        operands.append(into)
     return pl.pallas_call(
-        functools.partial(tile_kernel, group),
+        functools.partial(tile_kernel, group, first),
         grid_spec=grid_spec,
         out_shape=jax.ShapeDtypeStruct((pairs, nodes, nodes), jnp.bfloat16),
         compiler_params=pltpu.CompilerParams(
             vmem_limit_bytes=48 * 1024 * 1024, dimension_semantics=("arbitrary",)
         ),
         cost_estimate=cost,
-    )(pair_slave, pair_need, request, slave_basis, every_basis, weights)
-
-
-def master_sum(x):
+        input_output_aliases=aliases,
+    )(*operands)
+
+
+def master_sum(x, tied=None):
     count = lax.axis_size("master")
     spread = jnp.broadcast_to(x[None], (count,) + x.shape)
     got = lax.all_to_all(spread, "master", split_axis=0, concat_axis=0, tiled=True)
-    return jnp.sum(got, axis=0)
+    if tied is not None:
+        tied, got = lax.optimization_barrier((tied, got))
+    return jnp.sum(got, axis=0), tied
 
 
 def on_device(
@@ -124,7 +137,7 @@
     squares = jnp.square(slave_float)
     lump_part = jnp.einsum("snq,sq->sn", squares, slave_weight, precision=high)
 
-    stored = build_tiles(slave_basis, every_basis, request, pair_slave, pair_need, weights)
+    tile_args = (slave_basis, every_basis, request, pair_slave, pair_need, weights)
     lam = pressure
     disp = master_disp
     flags = active == 1
@@ -138,11 +151,11 @@
         slave_terms = jnp.dot(slave_onehot, pair_terms, precision=high)
         partial_coupled = jnp.einsum("snq,sq->sn", slave_float, slave_terms, precision=high)
         if update == 0:
-            both = master_sum(jnp.stack([lump_part, partial_coupled]))
+            both, _ = master_sum(jnp.stack([lump_part, partial_coupled]))
             root_lump = jnp.sqrt(1.0 + both[0])
             coupled = both[1]
         else:
-            coupled = master_sum(partial_coupled)
+            coupled, stored = master_sum(partial_coupled, build_tiles(*tile_args, 0))
         gap = slave_gap - coupled / root_lump
         lam = jnp.where(flags, lam - 1.0 * gap, jnp.zeros_like(lam))
         slave_proj = jnp.einsum("snq,sn->sq", slave_float, lam, precision=high)
@@ -152,6 +165,7 @@
             outbound.reshape(peers, mb_dev, qpts), everyone, split_axis=0, concat_axis=0, tiled=True
         )
         if update == ITERS - 1:
+            stored = build_tiles(*tile_args, 1, stored)
             stored, inbound = lax.optimization_barrier((stored, inbound))
         own_load = jnp.sum(inbound, axis=0)
         force = jnp.einsum("mnq,mq->mn", master_float, own_load, precision=high)

time: 135 us -> 141 us (1.044)
  blocking collectives: 42.1 us -> 33.7 us
  starting transfers between devices: 19.7 us -> 27.3 us
  Pallas kernels: 17.9 us -> 23.1 us
    all_to_all x1 -> x0, blocking collectives: 8.36 us -> none  [master_sum(): lax.all_to_all(spread, 'master', split_axis=0, concat_axis=0, tiled=True)]
    pallas_call x1 -> x2, Pallas kernels: 17.9 us -> 23.1 us  [build_tiles(): pl.pallas_call(functools.partial(tile_kernel, group, first), grid_spec=gr...]
    all_to_all x1 -> x2, starting transfers between devices: 4.03 us -> 8.42 us  [master_sum(): lax.all_to_all(spread, 'master', split_axis=0, concat_axis=0, tiled=True)]
    all_to_all x1, starting transfers between devices: 4.19 us -> 7.35 us  [on_device(): lax.all_to_all(outbound.reshape(peers, mb_dev, qpts), everyone, split_axi...]
    all_to_all x1 -> x2, waiting for transfers between devices: 4.57 us -> 4.58 us  [master_sum(): lax.all_to_all(spread, 'master', split_axis=0, concat_axis=0, tiled=True)]
  transfers between devices with their start and end apart: 4 -> 5, of which waited for: 2 -> 2; matrix products, arithmetic and copies ran while one was open for 22% -> 20% of each run, Pallas kernels for 13% -> 17%
where the time goes in v6:
time: 141 us; the launch traced here: 139 us
  blocking collectives  33.7 us (24%)
  starting transfers between devices  27.3 us (19%)
  Pallas kernels  23.1 us (16%)
  matrix products  17.7 us (13%)
  between operations  14.3 us (10%)
  waiting for transfers between devices  9.47 us (7%)
  local copies, waits for them, and re-layouts  7.61 us (5%)
  other arithmetic  6.24 us (4%)
    pallas_call x2, Pallas kernels, build_tiles(): pl.pallas_call(functools.partial(tile_kernel, group, first), grid_spec=gr...  23.1 us
    all_to_all x1, blocking collectives, on_device(): lax.all_to_all(outgoing_proj, everyone, split_axis=0, concat_axis=0, tile...  18.2 us
    all_to_all x1, blocking collectives, on_device(): lax.all_to_all(outbound.reshape(peers, mb_dev, qpts), everyone, split_axi...  15.5 us
    all_to_all x1, starting transfers between devices, on_device(): lax.all_to_all(outgoing_proj, everyone, split_axis=0, concat_axis=0, tile...  11.5 us
    all_to_all x2, starting transfers between devices, master_sum(): lax.all_to_all(spread, 'master', split_axis=0, concat_axis=0, tiled=True)  8.42 us
    all_to_all x1, starting transfers between devices, on_device(): lax.all_to_all(outbound.reshape(peers, mb_dev, qpts), everyone, split_axi...  7.35 us
    all_to_all x2, waiting for transfers between devices, master_sum(): lax.all_to_all(spread, 'master', split_axis=0, concat_axis=0, tiled=True)  4.58 us
    all_to_all x1, waiting for transfers between devices, on_device(): lax.all_to_all(outgoing_proj, everyone, split_axis=0, concat_axis=0, tile...  4.16 us
  transfers between devices with their start and end apart: 5, of which 2 were waited for; matrix products, arithmetic and copies ran while one was open for 20% of the time, Pallas kernels for 17%

profile of v6, /device:TPU:1, one launch (start us, length us, event | category | flops | bytes accessed | tf_op | source)
XLA Modules:
  0.0 139.5 jit_solution(18144938982556434832)
XLA Ops:
  7.2 0.0 copy-start.2
  7.2 0.0 copy-start.1
  7.2 0.0 copy-start
  7.2 0.0 all-gather.2.cloned.1.call-start
  7.2 0.7 all-gather.2.cloned.1.call-update
  7.9 1.1 fusion.28
  9.0 0.8 broadcast_in_dim.17
  9.8 11.5 %all-to-all-start = ((f32[128,4,128]{2,1,0:T(4,128)}), f32[128,4,128]{2,1,0:T(4,128)S(1)}, u32[]{:S(2)}, u32[]{:S(2)}) async-start(f32[128,4,128]{2,1,0:T(4,128)} %broadcast_in_dim.17), calls=%async_computation | async-start | bytes 524288 | tf_op jit(solution)/shard_map/all_to_all | solution.py:148
  21.3 0.7 compare_select_fusion.1
  22.0 0.7 compare_select_fusion.2
  22.7 0.7 broadcast_multiply_fusion
  23.3 1.1 fusion.13.w_ref
  24.4 0.9 fusion.18
  25.3 2.8 %fusion = f32[16,1,128]{2,1,0:T(1,128)S(1)} fusion(f32[16,128,1]{1,2,0:T(1,128)S(1)} %bitcast.109, bf16[16,128,128]{2,1,0:T(8,128)(2,1)} %slave_ref.3), kind=kOutput, calls=%fused_computation.6 | convolution fusion | flops 3670016 | bytes 540672 | tf_op jit(solution)/shard_map/snq,sq->sn/dot_general | solution.py:138
  28.1 4.2 %all-to-all-done = f32[128,4,128]{2,1,0:T(4,128)S(1)} async-done(((f32[128,4,128]{2,1,0:T(4,128)}), f32[128,4,128]{2,1,0:T(4,128)S(1)}, u32[]{:S(2)}, u32[]{:S(2)}) %all-to-all-start) | async-done | bytes 262176 | tf_op jit(solution)/shard_map/all_to_all | solution.py:148
  32.3 0.6 gather_fusion
  33.0 1.0 gather_fusion.1
  34.0 0.9 fusion.11
  34.9 1.9 %fusion.29 = f32[16,1,128]{2,1,0:T(1,128)S(1)} fusion(f32[16,128,1]{1,2,0:T(1,128)S(1)} %bitcast.96, bf16[16,128,128]{2,1,0:T(8,128)(2,1)} %slave_ref.3), kind=kOutput, calls=%fused_computation.54 | convolution fusion | flops 3145728 | bytes 540672 | tf_op jit(solution)/shard_map/snq,sq->sn/dot_general | solution.py:152
  36.9 0.7 broadcast_in_dim.20
  37.6 4.0 %all-to-all-start.1 = ((f32[8,2,16,128]{3,2,1,0:T(8,128)}), f32[8,2,16,128]{3,2,1,0:T(8,128)S(1)}, u32[]{:S(2)}, u32[]{:S(2)}) async-start(f32[8,2,16,128]{3,2,1,0:T(8,128)} %broadcast_in_dim.20), calls=%async_computation.1 | async-start | bytes 262144 | tf_op jit(solution)/shard_map/all_to_all | solution.py:87
  41.6 0.7 compare_select_fusion
  42.3 4.6 %all-to-all-done.1 = f32[8,2,16,128]{3,2,1,0:T(8,128)S(1)} async-done(((f32[8,2,16,128]{3,2,1,0:T(8,128)}), f32[8,2,16,128]{3,2,1,0:T(8,128)S(1)}, u32[]{:S(2)}, u32[]{:S(2)}) %all-to-all-start.1) | async-done | bytes 131104 | tf_op jit(solution)/shard_map/all_to_all | solution.py:87
  46.9 0.7 fusion.27
  47.6 1.6 %fusion.30 = f32[16,1,128]{2,1,0:T(1,128)S(1)} fusion(f32[16,128,1]{1,2,0:T(1,128)S(1)} %bitcast.95, bf16[16,128,128]{2,1,0:T(8,128)(2,1)} %slave_ref.3), kind=kOutput, calls=%fused_computation.55 | convolution fusion | flops 3145728 | bytes 540672 | tf_op jit(solution)/shard_map/snq,sn->sq/dot_general | solution.py:161
  49.2 1.0 gather_fusion.2
  50.2 1.0 fusion.7
  51.2 0.3 fusion.10
  51.5 15.5 %all_to_all.30 = f32[128,4,128]{2,1,0:T(4,128)S(1)} all-to-all(f32[128,4,128]{2,1,0:T(4,128)S(1)} %bitcast.94), channel_id=1, replica_groups=mesh['slave'=16,'master'=8] {'slave','master'}, dimensions={0} | all-to-all | bytes 524288 | tf_op jit(solution)/shard_map/all_to_all | solution.py:164
  67.0 0.1 reduce_sum.37
  67.1 1.3 fusion.31
  68.4 0.7 multiply_subtract_fusion.1
  69.1 1.1 fusion.32
  70.3 18.2 %all_to_all.31 = f32[128,4,128]{2,1,0:T(4,128)S(1)} all-to-all(f32[128,4,128]{2,1,0:T(4,128)S(1)} %broadcast_in_dim.22), channel_id=1, replica_groups=mesh['slave'=16,'master'=8] {'slave','master'}, dimensions={0} | all-to-all | bytes 524288 | tf_op jit(solution)/shard_map/all_to_all | solution.py:148
  88.5 0.6 gather_fusion.3
  89.1 1.0 gather_fusion.4
  90.2 0.9 fusion.5
  91.1 1.9 %fusion.33 = f32[16,1,128]{2,1,0:T(1,128)S(1)} fusion(f32[16,128,1]{1,2,0:T(1,128)S(1)} %bitcast.97, bf16[16,128,128]{2,1,0:T(8,128)(2,1)} %slave_ref.3), kind=kOutput, calls=%fused_computation.58 | convolution fusion | flops 3145728 | bytes 540672 | tf_op jit(solution)/shard_map/snq,sq->sn/dot_general | solution.py:152
  93.0 0.7 broadcast_in_dim.23
  93.7 4.4 %all-to-all-start.4 = ((f32[8,16,128]{2,1,0:T(8,128)}), f32[8,16,128]{2,1,0:T(8,128)S(1)}, u32[]{:S(2)}, u32[]{:S(2)}) async-start(f32[8,16,128]{2,1,0:T(8,128)} %broadcast_in_dim.23), calls=%async_computation.4 | async-start | bytes 131072 | tf_op jit(solution)/shard_map/all_to_all | solution.py:87
  98.1 0.0 copy-start.5
  98.1 0.0 all-gather.2.cloned.1.call-done.basis_hbm
  98.1 0.0 copy-done.2
  98.1 0.0 copy-done.1
  98.1 0.0 copy-done
  98.1 11.6 %shard_map.139.rest_0_ = bf16[512,128,128]{2,1,0:T(8,128)(2,1)} custom-call(s32[512]{0:T(512)S(1)} %copy-done.1, s32[512]{0:T(512)S(1)} %copy-done.2, s32[128]{0:T(128)S(1)} %get-tuple-element.14.mreq_ref, bf16[16,128,128]{2,1,0:T(8,128)(2,1)S(1)} %copy-done, bf16[512,128,128]{2,1,0:T(8,128)(2,1)} %all-gather.2.cloned.1.call-done.basis_hbm, ...), custom_call_target="tpu_custom_call" | custom-call | flops 1073741824 | bytes 12713984 | tf_op jit(solution)/shard_map/pallas_call | solution.py:72
  109.7 0.0 all-to-all-done.4
  109.7 0.0 copy-done.5
  109.8 0.0 copy-start.4
  109.8 0.5 fusion.34
  110.3 1.0 gather_fusion.5
  111.3 0.3 fusion.3
  111.7 1.0 fusion.9
  112.6 7.3 %all-to-all-start.5 = ((f32[128,4,128]{2,1,0:T(4,128)}), f32[128,4,128]{2,1,0:T(4,128)S(1)}, u32[]{:S(2)}, u32[]{:S(2)}) async-start(f32[128,4,128]{2,1,0:T(4,128)} %bitcast.40), calls=%async_computation.5 | async-start | bytes 524288 | tf_op jit(solution)/shard_map/all_to_all | solution.py:164
  120.0 0.0 copy-start.3
  120.0 11.6 %shard_map.140 = bf16[512,128,128]{2,1,0:T(8,128)(2,1)} custom-call(s32[512]{0:T(512)S(1)} %copy-done.1, s32[512]{0:T(512)S(1)} %copy-done.2, s32[128]{0:T(128)S(1)} %get-tuple-element.14.mreq_ref, bf16[16,128,128]{2,1,0:T(8,128)(2,1)S(1)} %copy-done, bf16[512,128,128]{2,1,0:T(8,128)(2,1)} %all-gather.2.cloned.1.call-done.basis_hbm, ...), custom_call_target="tpu_custom_call", output_to_operand_aliasing={{}: (6, {})} | custom-call | flops 1073741824 | bytes 12713984 | tf_op jit(solution)/shard_map/pallas_call | solution.py:72
  131.6 0.0 copy-done.4
  131.6 0.0 all-to-all-done.5
  131.6 0.1 reduce_sum.39
  131.7 0.0 copy-done.3
  131.7 0.3 fusion.35
  132.0 0.6 multiply_subtract_fusion
  (8 shorter events, 0.1 us)
Async XLA Ops:
  7.2 91.0 %copy-start.2 = (s32[512]{0:T(512)S(1)}, s32[512]{0:T(512)}, u32[]{:S(2)}) copy-start(s32[512]{0:T(512)} %nidx_ref.3) | copy-start | bytes 6148
  7.2 91.0 %copy-start.1 = (s32[512]{0:T(512)S(1)}, s32[512]{0:T(512)}, u32[]{:S(2)}) copy-start(s32[512]{0:T(512)} %sidx_ref.3) | copy-start | bytes 6148
  7.2 91.0 %copy-start = (bf16[16,128,128]{2,1,0:T(8,128)(2,1)S(1)}, bf16[16,128,128]{2,1,0:T(8,128)(2,1)}, u32[]{:S(2)}) copy-start(bf16[16,128,128]{2,1,0:T(8,128)(2,1)} %slave_ref.3) | copy-start | bytes 1572868
  7.2 90.9 %all-gather.2.cloned.1.call-start = ((), (), s32[]{:S(2)}) async-start(), calls=%async_computation.6 | async-start | bytes 16908288 | tf_op jit(solution)/shard_map/all_gather | solution.py:115
  9.8 22.5 %all-to-all-start = ((f32[128,4,128]{2,1,0:T(4,128)}), f32[128,4,128]{2,1,0:T(4,128)S(1)}, u32[]{:S(2)}, u32[]{:S(2)}) async-start(f32[128,4,128]{2,1,0:T(4,128)} %broadcast_in_dim.17), calls=%async_computation | async-start | bytes 524288 | tf_op jit(solution)/shard_map/all_to_all | solution.py:148
  37.6 9.3 %all-to-all-start.1 = ((f32[8,2,16,128]{3,2,1,0:T(8,128)}), f32[8,2,16,128]{3,2,1,0:T(8,128)S(1)}, u32[]{:S(2)}, u32[]{:S(2)}) async-start(f32[8,2,16,128]{3,2,1,0:T(8,128)} %broadcast_in_dim.20), calls=%async_computation.1 | async-start | bytes 262144 | tf_op jit(solution)/shard_map/all_to_all | solution.py:87
  93.7 16.0 %all-to-all-start.4 = ((f32[8,16,128]{2,1,0:T(8,128)}), f32[8,16,128]{2,1,0:T(8,128)S(1)}, u32[]{:S(2)}, u32[]{:S(2)}) async-start(f32[8,16,128]{2,1,0:T(8,128)} %broadcast_in_dim.23), calls=%async_computation.4 | async-start | bytes 131072 | tf_op jit(solution)/shard_map/all_to_all | solution.py:87
  98.1 11.7 %copy-start.5 = (f32[16,128]{1,0:T(8,128)S(1)}, f32[16,128]{1,0:T(8,128)}, u32[]{:S(2)}) copy-start(f32[16,128]{1,0:T(8,128)} %param.14) | copy-start | bytes 24580
  109.8 21.8 %copy-start.4 = (f32[16,128]{1,0:T(8,128)}, f32[16,128]{1,0:T(8,128)S(1)}, u32[]{:S(2)}) copy-start(f32[16,128]{1,0:T(8,128)S(1)} %subtract_select_fusion) | copy-start | bytes 24580
  112.6 19.0 %all-to-all-start.5 = ((f32[128,4,128]{2,1,0:T(4,128)}), f32[128,4,128]{2,1,0:T(4,128)S(1)}, u32[]{:S(2)}, u32[]{:S(2)}) async-start(f32[128,4,128]{2,1,0:T(4,128)} %bitcast.40), calls=%async_computation.5 | async-start | bytes 524288 | tf_op jit(solution)/shard_map/all_to_all | solution.py:164
  120.0 11.8 %copy-start.3 = (bf16[4,128,128]{2,1,0:T(8,128)(2,1)S(1)}, bf16[4,128,128]{2,1,0:T(8,128)(2,1)}, u32[]{:S(2)}) copy-start(bf16[4,128,128]{2,1,0:T(8,128)(2,1)} %param.13) | copy-start | bytes 393220
Sparse Core Ops, SparseCore 0:
  11.2 86.9 all-gather.1

commit v7 on v5

--- a/solution.py
+++ b/solution.py
@@ -122,7 +122,7 @@
     slave_float = slave_basis.astype(jnp.float32)
     master_float = master_basis.astype(jnp.float32)
     squares = jnp.square(slave_float)
-    lump_part = jnp.einsum("snq,sq->sn", squares, slave_weight, precision=high)
+    lump_part = jnp.sum(squares * slave_weight[:, None, :], axis=2)
 
     stored = build_tiles(slave_basis, every_basis, request, pair_slave, pair_need, weights)
     lam = pressure
@@ -130,13 +130,13 @@
     flags = active == 1
     root_lump = None
     for update in range(ITERS):
-        own_proj = jnp.einsum("mnq,mn->mq", master_float, disp, precision=high)
+        own_proj = jnp.sum(master_float * disp[:, :, None], axis=1)
         outgoing_proj = jnp.broadcast_to(own_proj[None], (peers,) + own_proj.shape)
         returned = lax.all_to_all(outgoing_proj, everyone, split_axis=0, concat_axis=0, tiled=True)
         need_proj = returned.reshape(mblocks, qpts)[request]
         pair_terms = weights * need_proj[pair_need]
         slave_terms = jnp.dot(slave_onehot, pair_terms, precision=high)
-        partial_coupled = jnp.einsum("snq,sq->sn", slave_float, slave_terms, precision=high)
+        partial_coupled = jnp.sum(slave_float * slave_terms[:, None, :], axis=2)
         if update == 0:
             both = master_sum(jnp.stack([lump_part, partial_coupled]))
             root_lump = jnp.sqrt(1.0 + both[0])
@@ -145,7 +145,7 @@
             coupled = master_sum(partial_coupled)
         gap = slave_gap - coupled / root_lump
         lam = jnp.where(flags, lam - 1.0 * gap, jnp.zeros_like(lam))
-        slave_proj = jnp.einsum("snq,sn->sq", slave_float, lam, precision=high)
+        slave_proj = jnp.sum(slave_float * lam[:, :, None], axis=1)
         need_load = jnp.dot(need_onehot, weights * slave_proj[pair_slave], precision=high)
         outbound = jnp.dot(block_onehot, need_load, precision=high)
         inbound = lax.all_to_all(
@@ -154,7 +154,7 @@
         if update == ITERS - 1:
             stored, inbound = lax.optimization_barrier((stored, inbound))
         own_load = jnp.sum(inbound, axis=0)
-        force = jnp.einsum("mnq,mq->mn", master_float, own_load, precision=high)
+        force = jnp.sum(master_float * own_load[:, None, :], axis=2)
         disp = disp - 0.05 * force
     return (lam, disp, stored)
 

time: 135 us -> 134 us (level)
  matrix products: 17.7 us -> 5.19 us
  other arithmetic: 6.24 us -> 15 us
  waiting for transfers between devices: 9.44 us -> 12.2 us
    dot_general x9 -> x0, matrix products: 12.5 us -> none  [the longest x2 3.89 us: on_device(): jnp.einsum('snq,sq->sn', slave_float, slave_terms, precision=high)]
    reduce_sum x0 -> x8, other arithmetic: none -> 8.08 us  [the longest x2 2.1 us: on_device(): own_proj = jnp.sum(master_float * disp[:, :, None], axis=1)]
    all_to_all x1, waiting for transfers between devices: 4.16 us -> 6.97 us  [on_device(): lax.all_to_all(outgoing_proj, everyone, split_axis=0, concat_axis=0, tile...]
  transfers between devices with their start and end apart: 4 -> 4, of which waited for: 2 -> 2; matrix products, arithmetic and copies ran while one was open for 22% -> 20% of each run, Pallas kernels for 13% -> 13%
where the time goes in v7:
time: 134 us; the launch traced here: 133 us
  blocking collectives  41.5 us (31%)
  starting transfers between devices  20 us (15%)
  Pallas kernels  17.9 us (13%)
  other arithmetic  15 us (11%)
  between operations  14.3 us (11%)
  waiting for transfers between devices  12.2 us (9%)
  local copies, waits for them, and re-layouts  6.92 us (5%)
  matrix products  5.19 us (4%)
    all_to_all x1, blocking collectives, on_device(): lax.all_to_all(outgoing_proj, everyone, split_axis=0, concat_axis=0, tile...  18.3 us
    pallas_call x1, Pallas kernels, build_tiles(): pl.pallas_call(functools.partial(tile_kernel, group), grid_spec=grid_spec...  17.9 us
    all_to_all x1, blocking collectives, on_device(): lax.all_to_all(outbound.reshape(peers, mb_dev, qpts), everyone, split_axi...  14.9 us
    all_to_all x1, starting transfers between devices, on_device(): lax.all_to_all(outgoing_proj, everyone, split_axis=0, concat_axis=0, tile...  11.5 us
    all_to_all x1, blocking collectives, master_sum(): lax.all_to_all(spread, 'master', split_axis=0, concat_axis=0, tiled=True)  8.35 us
    all_to_all x1, waiting for transfers between devices, on_device(): lax.all_to_all(outgoing_proj, everyone, split_axis=0, concat_axis=0, tile...  6.97 us
    all_to_all x1, waiting for transfers between devices, master_sum(): lax.all_to_all(spread, 'master', split_axis=0, concat_axis=0, tiled=True)  4.57 us
    all_to_all x1, starting transfers between devices, on_device(): lax.all_to_all(outbound.reshape(peers, mb_dev, qpts), everyone, split_axi...  4.44 us
  transfers between devices with their start and end apart: 4, of which 2 were waited for; matrix products, arithmetic and copies ran while one was open for 20% of the time, Pallas kernels for 13%

profile of v7, /device:TPU:1, one launch (start us, length us, event | category | flops | bytes accessed | tf_op | source)
XLA Modules:
  0.0 133.1 jit_solution(8813527733605722740)
XLA Ops:
  7.2 0.0 copy-start.2
  7.2 0.0 copy-start.1
  7.2 0.0 copy-start
  7.2 0.0 all-gather.2.cloned.1.call-start
  7.2 0.7 all-gather.2.cloned.1.call-update
  7.9 1.1 fusion.6
  9.0 0.7 broadcast_in_dim.17
  9.7 11.5 %all-to-all-start = ((f32[128,4,128]{2,1,0:T(4,128)}), f32[128,4,128]{2,1,0:T(4,128)S(1)}, u32[]{:S(2)}, u32[]{:S(2)}) async-start(f32[128,4,128]{2,1,0:T(4,128)} %broadcast_in_dim.17), calls=%async_computation | async-start | bytes 524288 | tf_op jit(solution)/shard_map/all_to_all | solution.py:135
  21.2 0.7 compare_select_fusion.1
  21.9 0.7 compare_select_fusion.2
  22.6 0.7 broadcast_multiply_fusion
  23.3 1.1 fusion.20.w_ref
  24.4 0.9 fusion.25
  25.3 7.0 %all-to-all-done = f32[128,4,128]{2,1,0:T(4,128)S(1)} async-done(((f32[128,4,128]{2,1,0:T(4,128)}), f32[128,4,128]{2,1,0:T(4,128)S(1)}, u32[]{:S(2)}, u32[]{:S(2)}) %all-to-all-start) | async-done | bytes 262176 | tf_op jit(solution)/shard_map/all_to_all | solution.py:135
  32.2 0.6 gather_fusion
  32.9 1.0 gather_fusion.1
  33.9 0.9 fusion.18
  34.8 1.7 %fusion.1 = (f32[16,128]{1,0:T(8,128)S(1)}, f32[16,128]{1,0:T(8,128)S(1)}) fusion(bf16[16,128,128]{2,1,0:T(8,128)(2,1)} %slave_ref.1, f32[16,128]{1,0:T(8,128)S(1)} %fusion.25, f32[16,128]{1,0:T(8,128)S(1)} %fusion.18), kind=kLoop, calls=%fused_computation.12 | loop fusion | flops 1568768 | bytes 557056 | tf_op jit(solution)/shard_map/reduce_sum | solution.py:125
  36.5 0.7 broadcast_in_dim.20
  37.2 4.0 %all-to-all-start.1 = ((f32[8,2,16,128]{3,2,1,0:T(8,128)}), f32[8,2,16,128]{3,2,1,0:T(8,128)S(1)}, u32[]{:S(2)}, u32[]{:S(2)}) async-start(f32[8,2,16,128]{3,2,1,0:T(8,128)} %broadcast_in_dim.20), calls=%async_computation.1 | async-start | bytes 262144 | tf_op jit(solution)/shard_map/all_to_all | solution.py:76
  41.2 0.7 compare_select_fusion
  41.9 4.6 %all-to-all-done.1 = f32[8,2,16,128]{3,2,1,0:T(8,128)S(1)} async-done(((f32[8,2,16,128]{3,2,1,0:T(8,128)}), f32[8,2,16,128]{3,2,1,0:T(8,128)S(1)}, u32[]{:S(2)}, u32[]{:S(2)}) %all-to-all-start.1) | async-done | bytes 131104 | tf_op jit(solution)/shard_map/all_to_all | solution.py:76
  46.5 0.7 fusion.34
  47.2 1.4 %fusion.3 = f32[16,128]{1,0:T(8,128)S(1)} fusion(bf16[16,128,128]{2,1,0:T(8,128)(2,1)} %slave_ref.1, f32[16,128]{1,0:T(8,128)S(1)} %get-tuple-element.9), kind=kLoop, calls=%fused_computation.14 | loop fusion | flops 784384 | bytes 540672 | tf_op jit(solution)/shard_map/reduce_sum | solution.py:148
  48.6 1.0 gather_fusion.2
  49.7 1.0 fusion.14
  50.7 0.3 fusion.17
  50.9 14.9 %all_to_all.30 = f32[128,4,128]{2,1,0:T(4,128)S(1)} all-to-all(f32[128,4,128]{2,1,0:T(4,128)S(1)} %bitcast.30), channel_id=1, replica_groups=mesh['slave'=16,'master'=8] {'slave','master'}, dimensions={0} | all-to-all | bytes 524288 | tf_op jit(solution)/shard_map/all_to_all | solution.py:151
  65.9 0.1 reduce_sum.122
  66.0 1.1 fusion.7
  67.1 0.7 multiply_subtract_fusion.1
  67.8 1.0 fusion.8
  68.9 18.3 %all_to_all.31 = f32[128,4,128]{2,1,0:T(4,128)S(1)} all-to-all(f32[128,4,128]{2,1,0:T(4,128)S(1)} %broadcast_in_dim.22), channel_id=1, replica_groups=mesh['slave'=16,'master'=8] {'slave','master'}, dimensions={0} | all-to-all | bytes 524288 | tf_op jit(solution)/shard_map/all_to_all | solution.py:135
  87.1 0.6 gather_fusion.3
  87.8 1.0 gather_fusion.4
  88.8 0.9 fusion.12
  89.7 1.4 %fusion.4 = f32[16,128]{1,0:T(8,128)S(1)} fusion(bf16[16,128,128]{2,1,0:T(8,128)(2,1)} %slave_ref.1, f32[16,128]{1,0:T(8,128)S(1)} %fusion.12), kind=kLoop, calls=%fused_computation.15 | loop fusion | flops 784384 | bytes 540672 | tf_op jit(solution)/shard_map/reduce_sum | solution.py:139
  91.1 8.4 %all_to_all.32 = f32[8,16,128]{2,1,0:T(8,128)S(1)} all-to-all(f32[8,16,128]{2,1,0:T(8,128)S(1)} %broadcast_in_dim.23), channel_id=1, replica_groups=mesh['slave'=16,'master'=8] {'master'}, dimensions={0} | all-to-all | bytes 131072 | tf_op jit(solution)/shard_map/all_to_all | solution.py:76
  99.5 0.7 subtract_select_fusion
  100.2 0.0 copy-done
  100.2 0.0 copy-start.4
  100.2 0.3 fusion.5
  100.6 1.0 gather_fusion.5
  101.6 0.0 copy-done.2
  101.6 0.3 fusion.10
  102.0 1.0 fusion.16
  102.9 4.4 %all-to-all-start.5 = ((f32[128,4,128]{2,1,0:T(4,128)}), f32[128,4,128]{2,1,0:T(4,128)S(1)}, u32[]{:S(2)}, u32[]{:S(2)}) async-start(f32[128,4,128]{2,1,0:T(4,128)} %bitcast.8), calls=%async_computation.5 | async-start | bytes 524288 | tf_op jit(solution)/shard_map/all_to_all | solution.py:151
  107.4 0.0 copy-start.3
  107.4 0.0 all-gather.2.cloned.1.call-done.basis_hbm
  107.4 0.0 copy-done.1
  107.4 17.9 %shard_map.139 = bf16[512,128,128]{2,1,0:T(8,128)(2,1)} custom-call(s32[512]{0:T(512)S(1)} %copy-done.1, s32[512]{0:T(512)S(1)} %copy-done.2, s32[128]{0:T(128)S(1)} %get-tuple-element.12.mreq_ref, bf16[16,128,128]{2,1,0:T(8,128)(2,1)S(1)} %copy-done, bf16[512,128,128]{2,1,0:T(8,128)(2,1)} %all-gather.2.cloned.1.call-done.basis_hbm, f32[512,128]{1,0:T(8,128)S(1)} %fusion.20.w_ref), custom_call_target="tpu_custom_call" | custom-call | flops 2147483648 | bytes 21233664 | tf_op jit(solution)/shard_map/pallas_call | solution.py:62
  125.4 0.0 copy-done.4
  125.4 0.0 all-to-all-done.5
  125.4 0.1 reduce_sum.128
  125.5 0.0 copy-done.3
  125.5 0.1 fusion.9
  125.7 0.6 multiply_subtract_fusion
  (8 shorter events, 0.1 us)
Async XLA Ops:
  7.2 94.5 %copy-start.2 = (s32[512]{0:T(512)S(1)}, s32[512]{0:T(512)}, u32[]{:S(2)}) copy-start(s32[512]{0:T(512)} %nidx_ref.1) | copy-start | bytes 6148
  7.2 100.2 %copy-start.1 = (s32[512]{0:T(512)S(1)}, s32[512]{0:T(512)}, u32[]{:S(2)}) copy-start(s32[512]{0:T(512)} %sidx_ref.1) | copy-start | bytes 6148
  7.2 93.0 %copy-start = (bf16[16,128,128]{2,1,0:T(8,128)(2,1)S(1)}, bf16[16,128,128]{2,1,0:T(8,128)(2,1)}, u32[]{:S(2)}) copy-start(bf16[16,128,128]{2,1,0:T(8,128)(2,1)} %slave_ref.1) | copy-start | bytes 1572868
  7.2 100.2 %all-gather.2.cloned.1.call-start = ((), (), s32[]{:S(2)}) async-start(), calls=%async_computation.6 | async-start | bytes 16908288 | tf_op jit(solution)/shard_map/all_gather | solution.py:102
  9.7 22.5 %all-to-all-start = ((f32[128,4,128]{2,1,0:T(4,128)}), f32[128,4,128]{2,1,0:T(4,128)S(1)}, u32[]{:S(2)}, u32[]{:S(2)}) async-start(f32[128,4,128]{2,1,0:T(4,128)} %broadcast_in_dim.17), calls=%async_computation | async-start | bytes 524288 | tf_op jit(solution)/shard_map/all_to_all | solution.py:135
  37.2 9.3 %all-to-all-start.1 = ((f32[8,2,16,128]{3,2,1,0:T(8,128)}), f32[8,2,16,128]{3,2,1,0:T(8,128)S(1)}, u32[]{:S(2)}, u32[]{:S(2)}) async-start(f32[8,2,16,128]{3,2,1,0:T(8,128)} %broadcast_in_dim.20), calls=%async_computation.1 | async-start | bytes 262144 | tf_op jit(solution)/shard_map/all_to_all | solution.py:76
  100.2 25.1 %copy-start.4 = (f32[16,128]{1,0:T(8,128)}, f32[16,128]{1,0:T(8,128)S(1)}, u32[]{:S(2)}) copy-start(f32[16,128]{1,0:T(8,128)S(1)} %subtract_select_fusion) | copy-start | bytes 24580
  102.9 22.5 %all-to-all-start.5 = ((f32[128,4,128]{2,1,0:T(4,128)}), f32[128,4,128]{2,1,0:T(4,128)S(1)}, u32[]{:S(2)}, u32[]{:S(2)}) async-start(f32[128,4,128]{2,1,0:T(4,128)} %bitcast.8), calls=%async_computation.5 | async-start | bytes 524288 | tf_op jit(solution)/shard_map/all_to_all | solution.py:151
  107.4 18.2 %copy-start.3 = (bf16[4,128,128]{2,1,0:T(8,128)(2,1)S(1)}, bf16[4,128,128]{2,1,0:T(8,128)(2,1)}, u32[]{:S(2)}) copy-start(bf16[4,128,128]{2,1,0:T(8,128)(2,1)} %param.13) | copy-start | bytes 393220
Sparse Core Ops, SparseCore 0:
  11.2 86.8 all-gather.1

commit v8 on v7

--- a/solution.py
+++ b/solution.py
@@ -95,7 +95,6 @@
     everyone = ("slave", "master")
     peers = lax.axis_size(everyone)
     mb_dev = master_basis.shape[0]
-    need_dev = need_slot.shape[0]
     qpts = slave_basis.shape[2]
     owner = need_owner[:, 0]
     request = owner * mb_dev + need_slot
@@ -111,13 +110,11 @@
     slave_onehot = (
         pair_slave[None, :] == jnp.arange(slave_count, dtype=jnp.int32)[:, None]
     ).astype(jnp.float32)
-    need_onehot = (pair_need[None, :] == jnp.arange(need_dev, dtype=jnp.int32)[:, None]).astype(
-        jnp.float32
-    )
     mblocks = peers * mb_dev
-    block_onehot = (request[None, :] == jnp.arange(mblocks, dtype=jnp.int32)[:, None]).astype(
-        jnp.float32
-    )
+    pair_block = request[pair_need]
+    block_onehot = (
+        pair_block[None, :] == jnp.arange(mblocks, dtype=jnp.int32)[:, None]
+    ).astype(jnp.float32)
     slave_weight = jnp.dot(slave_onehot, weights, precision=high)
     slave_float = slave_basis.astype(jnp.float32)
     master_float = master_basis.astype(jnp.float32)
@@ -133,8 +130,7 @@
         own_proj = jnp.sum(master_float * disp[:, :, None], axis=1)
         outgoing_proj = jnp.broadcast_to(own_proj[None], (peers,) + own_proj.shape)
         returned = lax.all_to_all(outgoing_proj, everyone, split_axis=0, concat_axis=0, tiled=True)
-        need_proj = returned.reshape(mblocks, qpts)[request]
-        pair_terms = weights * need_proj[pair_need]
+        pair_terms = weights * returned.reshape(mblocks, qpts)[pair_block]
         slave_terms = jnp.dot(slave_onehot, pair_terms, precision=high)
         partial_coupled = jnp.sum(slave_float * slave_terms[:, None, :], axis=2)
         if update == 0:
@@ -146,8 +142,7 @@
         gap = slave_gap - coupled / root_lump
         lam = jnp.where(flags, lam - 1.0 * gap, jnp.zeros_like(lam))
         slave_proj = jnp.sum(slave_float * lam[:, :, None], axis=1)
-        need_load = jnp.dot(need_onehot, weights * slave_proj[pair_slave], precision=high)
-        outbound = jnp.dot(block_onehot, need_load, precision=high)
+        outbound = jnp.dot(block_onehot, weights * slave_proj[pair_slave], precision=high)
         inbound = lax.all_to_all(
             outbound.reshape(peers, mb_dev, qpts), everyone, split_axis=0, concat_axis=0, tiled=True
         )

time: 134 us -> 133 us (level)
  waiting for transfers between devices: 12.2 us -> 8.9 us
  local copies, waits for them, and re-layouts: 6.92 us -> 8.97 us
  other arithmetic: 15 us -> 13.3 us
    all_to_all x1, waiting for transfers between devices: 6.97 us -> 3.62 us  [on_device(): lax.all_to_all(outgoing_proj, everyone, split_axis=0, concat_axis=0, tile...]
    gather x4 -> x3, local copies, waits for them, and re-layouts: 3.35 us -> 5.4 us  [the longest x1 3.34 us: on_device(): pair_block = request[pair_need]]
  transfers between devices with their start and end apart: 4 -> 4, of which waited for: 2 -> 2; matrix products, arithmetic and copies ran while one was open for 20% -> 20% of each run, Pallas kernels for 13% -> 14%
where the time goes in v8:
time: 133 us; the launch traced here: 132 us
  blocking collectives  42.7 us (32%)
  starting transfers between devices  20.6 us (15%)
  Pallas kernels  18.2 us (14%)
  between operations  14.3 us (11%)
  other arithmetic  13.3 us (10%)
  local copies, waits for them, and re-layouts  8.97 us (7%)
  waiting for transfers between devices  8.9 us (7%)
  matrix products  4.62 us (3%)
    all_to_all x1, blocking collectives, on_device(): lax.all_to_all(outgoing_proj, everyone, split_axis=0, concat_axis=0, tile...  18.3 us
    pallas_call x1, Pallas kernels, build_tiles(): pl.pallas_call(functools.partial(tile_kernel, group), grid_spec=grid_spec...  18.2 us
    all_to_all x1, blocking collectives, on_device(): lax.all_to_all(outbound.reshape(peers, mb_dev, qpts), everyone, split_axi...  16.1 us
    all_to_all x1, starting transfers between devices, on_device(): lax.all_to_all(outgoing_proj, everyone, split_axis=0, concat_axis=0, tile...  11.5 us
    all_to_all x1, blocking collectives, master_sum(): lax.all_to_all(spread, 'master', split_axis=0, concat_axis=0, tiled=True)  8.35 us
    all_to_all x1, starting transfers between devices, on_device(): lax.all_to_all(outbound.reshape(peers, mb_dev, qpts), everyone, split_axi...  5.1 us
    all_to_all x1, waiting for transfers between devices, master_sum(): lax.all_to_all(spread, 'master', split_axis=0, concat_axis=0, tiled=True)  4.57 us
    all_to_all x1, starting transfers between devices, master_sum(): lax.all_to_all(spread, 'master', split_axis=0, concat_axis=0, tiled=True)  4.02 us
  transfers between devices with their start and end apart: 4, of which 2 were waited for; matrix products, arithmetic and copies ran while one was open for 20% of the time, Pallas kernels for 14%

profile of v8, /device:TPU:1, one launch (start us, length us, event | category | flops | bytes accessed | tf_op | source)
XLA Modules:
  0.0 131.7 jit_solution(16325726102830785869)
XLA Ops:
  7.2 0.0 copy-start.2
  7.2 0.0 copy-start.1
  7.2 0.0 copy-start
  7.2 0.0 copy-start.5
  7.2 0.0 all-gather.2.cloned.1.call-start
  7.3 0.7 all-gather.2.cloned.1.call-update
  7.9 1.1 fusion.10
  9.0 0.7 broadcast_in_dim.15
  9.7 11.5 %all-to-all-start = ((f32[128,4,128]{2,1,0:T(4,128)}), f32[128,4,128]{2,1,0:T(4,128)S(1)}, u32[]{:S(2)}, u32[]{:S(2)}) async-start(f32[128,4,128]{2,1,0:T(4,128)} %broadcast_in_dim.15), calls=%async_computation | async-start | bytes 524288 | tf_op jit(solution)/shard_map/all_to_all | solution.py:132
  21.2 0.7 compare_select_fusion.2
  21.9 0.7 bitcast_add_fusion.mreq_ref
  22.6 3.3 %gather_fusion = s32[512]{0:T(512)S(1)} fusion(s32[128]{0:T(128)S(1)} %bitcast_add_fusion.mreq_ref, s32[1024]{0:T(1024)S(1)} %pad_clamp_fusion.2), kind=kCustom, calls=%fused_computation | custom fusion | bytes 6144 | tf_op jit(solution)/shard_map/gather | solution.py:114
  26.0 0.7 broadcast_multiply_fusion
  26.6 1.1 fusion.20.w_ref
  27.7 0.9 fusion.21
  28.6 3.6 %all-to-all-done = f32[128,4,128]{2,1,0:T(4,128)S(1)} async-done(((f32[128,4,128]{2,1,0:T(4,128)}), f32[128,4,128]{2,1,0:T(4,128)S(1)}, u32[]{:S(2)}, u32[]{:S(2)}) %all-to-all-start) | async-done | bytes 262176 | tf_op jit(solution)/shard_map/all_to_all | solution.py:132
  32.3 1.0 gather_fusion.1
  33.3 0.9 fusion.18
  34.2 1.7 %fusion.1 = (f32[16,128]{1,0:T(8,128)S(1)}, f32[16,128]{1,0:T(8,128)S(1)}) fusion(bf16[16,128,128]{2,1,0:T(8,128)(2,1)} %slave_ref.1, f32[16,128]{1,0:T(8,128)S(1)} %fusion.21, f32[16,128]{1,0:T(8,128)S(1)} %fusion.18), kind=kLoop, calls=%fused_computation.11 | loop fusion | flops 1568768 | bytes 557056 | tf_op jit(solution)/shard_map/reduce_sum | solution.py:122
  35.9 0.7 broadcast_in_dim.17
  36.5 4.0 %all-to-all-start.1 = ((f32[8,2,16,128]{3,2,1,0:T(8,128)}), f32[8,2,16,128]{3,2,1,0:T(8,128)S(1)}, u32[]{:S(2)}, u32[]{:S(2)}) async-start(f32[8,2,16,128]{3,2,1,0:T(8,128)} %broadcast_in_dim.17), calls=%async_computation.1 | async-start | bytes 262144 | tf_op jit(solution)/shard_map/all_to_all | solution.py:76
  40.6 0.7 compare_select_fusion.1
  41.3 4.6 %all-to-all-done.1 = f32[8,2,16,128]{3,2,1,0:T(8,128)S(1)} async-done(((f32[8,2,16,128]{3,2,1,0:T(8,128)}), f32[8,2,16,128]{3,2,1,0:T(8,128)S(1)}, u32[]{:S(2)}, u32[]{:S(2)}) %all-to-all-start.1) | async-done | bytes 131104 | tf_op jit(solution)/shard_map/all_to_all | solution.py:76
  45.8 0.7 fusion.30
  46.6 1.4 %fusion.3 = f32[16,128]{1,0:T(8,128)S(1)} fusion(bf16[16,128,128]{2,1,0:T(8,128)(2,1)} %slave_ref.1, f32[16,128]{1,0:T(8,128)S(1)} %get-tuple-element.9), kind=kLoop, calls=%fused_computation.13 | loop fusion | flops 784384 | bytes 540672 | tf_op jit(solution)/shard_map/reduce_sum | solution.py:144
  48.0 1.0 gather_fusion.2
  49.0 0.6 fusion.7
  49.7 16.1 %all_to_all.30 = f32[128,4,128]{2,1,0:T(4,128)S(1)} all-to-all(f32[128,4,128]{2,1,0:T(4,128)S(1)} %bitcast.29), channel_id=1, replica_groups=mesh['slave'=16,'master'=8] {'slave','master'}, dimensions={0} | all-to-all | bytes 524288 | tf_op jit(solution)/shard_map/all_to_all | solution.py:146
  65.8 0.1 reduce_sum.122
  65.9 1.0 fusion.11
  67.0 0.7 multiply_subtract_fusion.1
  67.7 1.0 fusion.12
  68.8 18.3 %all_to_all.31 = f32[128,4,128]{2,1,0:T(4,128)S(1)} all-to-all(f32[128,4,128]{2,1,0:T(4,128)S(1)} %broadcast_in_dim.19), channel_id=1, replica_groups=mesh['slave'=16,'master'=8] {'slave','master'}, dimensions={0} | all-to-all | bytes 524288 | tf_op jit(solution)/shard_map/all_to_all | solution.py:132
  87.0 1.0 gather_fusion.3
  88.1 0.9 fusion.15
  89.0 0.0 copy-done
  89.0 0.3 fusion.4
  89.4 8.4 %all_to_all.32 = f32[8,16,128]{2,1,0:T(8,128)S(1)} all-to-all(f32[8,16,128]{2,1,0:T(8,128)S(1)} %broadcast_in_dim.20), channel_id=1, replica_groups=mesh['slave'=16,'master'=8] {'master'}, dimensions={0} | all-to-all | bytes 131072 | tf_op jit(solution)/shard_map/all_to_all | solution.py:76
  97.7 0.0 copy-done.5
  97.8 0.0 copy-start.4
  97.8 0.3 fusion.5
  98.1 1.0 gather_fusion.4
  99.2 1.3 %fusion.6 = f32[512,128]{1,0:T(8,128)} fusion(s32[512]{0:T(512)S(1)} %gather_fusion, f32[512,128]{1,0:T(8,128)S(1)} %fusion.20.w_ref, f32[512,128]{1,0:T(8,128)S(1)} %gather_fusion.4), kind=kOutput, calls=%fused_computation.17 | convolution fusion | flops 402980864 | bytes 788480 | tf_op jit(solution)/shard_map/dot_general | solution.py:145
  100.5 5.1 %all-to-all-start.5 = ((f32[128,4,128]{2,1,0:T(4,128)}), f32[128,4,128]{2,1,0:T(4,128)S(1)}, u32[]{:S(2)}, u32[]{:S(2)}) async-start(f32[128,4,128]{2,1,0:T(4,128)} %bitcast.10), calls=%async_computation.5 | async-start | bytes 524288 | tf_op jit(solution)/shard_map/all_to_all | solution.py:146
  105.6 0.0 copy-start.3
  105.6 0.0 all-gather.2.cloned.1.call-done.basis_hbm
  105.7 0.0 copy-done.2
  105.7 0.0 copy-done.1
  105.7 18.2 %shard_map.139 = bf16[512,128,128]{2,1,0:T(8,128)(2,1)} custom-call(s32[512]{0:T(512)S(1)} %copy-done.1, s32[512]{0:T(512)S(1)} %copy-done.2, s32[128]{0:T(128)S(1)} %bitcast_add_fusion.mreq_ref, bf16[16,128,128]{2,1,0:T(8,128)(2,1)S(1)} %copy-done, bf16[512,128,128]{2,1,0:T(8,128)(2,1)} %all-gather.2.cloned.1.call-done.basis_hbm, f32[512,128]{1,0:T(8,128)S(1)} %fusion.20.w_ref), custom_call_target="tpu_custom_call" | custom-call | flops 2147483648 | bytes 21233664 | tf_op jit(solution)/shard_map/pallas_call | solution.py:62
  123.9 0.0 copy-done.4
  123.9 0.0 all-to-all-done.5
  123.9 0.1 reduce_sum.128
  124.1 0.0 copy-done.3
  124.1 0.1 fusion.13
  124.2 0.6 multiply_subtract_fusion
  (10 shorter events, 0.1 us)
Async XLA Ops:
  7.2 98.5 %copy-start.2 = (s32[512]{0:T(512)S(1)}, s32[512]{0:T(512)}, u32[]{:S(2)}) copy-start(s32[512]{0:T(512)} %nidx_ref.1) | copy-start | bytes 6148
  7.2 98.5 %copy-start.1 = (s32[512]{0:T(512)S(1)}, s32[512]{0:T(512)}, u32[]{:S(2)}) copy-start(s32[512]{0:T(512)} %sidx_ref.1) | copy-start | bytes 6148
  7.2 81.8 %copy-start = (bf16[16,128,128]{2,1,0:T(8,128)(2,1)S(1)}, bf16[16,128,128]{2,1,0:T(8,128)(2,1)}, u32[]{:S(2)}) copy-start(bf16[16,128,128]{2,1,0:T(8,128)(2,1)} %slave_ref.1) | copy-start | bytes 1572868
  7.2 90.5 %copy-start.5 = (f32[16,128]{1,0:T(8,128)S(1)}, f32[16,128]{1,0:T(8,128)}, u32[]{:S(2)}) copy-start(f32[16,128]{1,0:T(8,128)} %param.14) | copy-start | bytes 24580
  7.2 98.4 %all-gather.2.cloned.1.call-start = ((), (), s32[]{:S(2)}) async-start(), calls=%async_computation.6 | async-start | bytes 16908288 | tf_op jit(solution)/shard_map/all_gather | solution.py:101
  9.7 22.5 %all-to-all-start = ((f32[128,4,128]{2,1,0:T(4,128)}), f32[128,4,128]{2,1,0:T(4,128)S(1)}, u32[]{:S(2)}, u32[]{:S(2)}) async-start(f32[128,4,128]{2,1,0:T(4,128)} %broadcast_in_dim.15), calls=%async_computation | async-start | bytes 524288 | tf_op jit(solution)/shard_map/all_to_all | solution.py:132
  36.5 9.3 %all-to-all-start.1 = ((f32[8,2,16,128]{3,2,1,0:T(8,128)}), f32[8,2,16,128]{3,2,1,0:T(8,128)S(1)}, u32[]{:S(2)}, u32[]{:S(2)}) async-start(f32[8,2,16,128]{3,2,1,0:T(8,128)} %broadcast_in_dim.17), calls=%async_computation.1 | async-start | bytes 262144 | tf_op jit(solution)/shard_map/all_to_all | solution.py:76
  97.8 26.1 %copy-start.4 = (f32[16,128]{1,0:T(8,128)}, f32[16,128]{1,0:T(8,128)S(1)}, u32[]{:S(2)}) copy-start(f32[16,128]{1,0:T(8,128)S(1)} %subtract_select_fusion) | copy-start | bytes 24580
  100.5 23.4 %all-to-all-start.5 = ((f32[128,4,128]{2,1,0:T(4,128)}), f32[128,4,128]{2,1,0:T(4,128)S(1)}, u32[]{:S(2)}, u32[]{:S(2)}) async-start(f32[128,4,128]{2,1,0:T(4,128)} %bitcast.10), calls=%async_computation.5 | async-start | bytes 524288 | tf_op jit(solution)/shard_map/all_to_all | solution.py:146
  105.6 18.5 %copy-start.3 = (bf16[4,128,128]{2,1,0:T(8,128)(2,1)S(1)}, bf16[4,128,128]{2,1,0:T(8,128)(2,1)}, u32[]{:S(2)}) copy-start(bf16[4,128,128]{2,1,0:T(8,128)(2,1)} %param.13) | copy-start | bytes 393220
Sparse Core Ops, SparseCore 0:
  11.2 86.8 all-gather.1

commit v9 on v8

--- a/solution.py
+++ b/solution.py
@@ -70,13 +70,6 @@
     )(pair_slave, pair_need, request, slave_basis, every_basis, weights)
 
 
-def master_sum(x):
-    count = lax.axis_size("master")
-    spread = jnp.broadcast_to(x[None], (count,) + x.shape)
-    got = lax.all_to_all(spread, "master", split_axis=0, concat_axis=0, tiled=True)
-    return jnp.sum(got, axis=0)
-
-
 def on_device(
     slave_basis,
     master_basis,
@@ -115,7 +108,23 @@
     block_onehot = (
         pair_block[None, :] == jnp.arange(mblocks, dtype=jnp.int32)[:, None]
     ).astype(jnp.float32)
-    slave_weight = jnp.dot(slave_onehot, weights, precision=high)
+    group = lax.axis_size("master")
+    weights_group = lax.all_to_all(
+        jnp.broadcast_to(weights[None], (group,) + weights.shape), "master", 0, 0, tiled=True
+    ).reshape(-1, qpts)
+    index_group = lax.all_to_all(
+        jnp.broadcast_to(jnp.stack([pair_block, pair_slave])[None], (group, 2) + pair_block.shape),
+        "master",
+        0,
+        0,
+        tiled=True,
+    )
+    block_group = index_group[:, 0].reshape(-1)
+    slave_group = index_group[:, 1].reshape(-1)
+    group_onehot = (
+        slave_group[None, :] == jnp.arange(slave_count, dtype=jnp.int32)[:, None]
+    ).astype(jnp.float32)
+    slave_weight = jnp.dot(group_onehot, weights_group, precision=high)
     slave_float = slave_basis.astype(jnp.float32)
     master_float = master_basis.astype(jnp.float32)
     squares = jnp.square(slave_float)
@@ -130,15 +139,12 @@
         own_proj = jnp.sum(master_float * disp[:, :, None], axis=1)
         outgoing_proj = jnp.broadcast_to(own_proj[None], (peers,) + own_proj.shape)
         returned = lax.all_to_all(outgoing_proj, everyone, split_axis=0, concat_axis=0, tiled=True)
-        pair_terms = weights * returned.reshape(mblocks, qpts)[pair_block]
-        slave_terms = jnp.dot(slave_onehot, pair_terms, precision=high)
+        pair_terms = weights_group * returned.reshape(mblocks, qpts)[block_group]
+        slave_terms = jnp.dot(group_onehot, pair_terms, precision=high)
         partial_coupled = jnp.sum(slave_float * slave_terms[:, None, :], axis=2)
         if update == 0:
-            both = master_sum(jnp.stack([lump_part, partial_coupled]))
-            root_lump = jnp.sqrt(1.0 + both[0])
-            coupled = both[1]
-        else:
-            coupled = master_sum(partial_coupled)
+            root_lump = jnp.sqrt(1.0 + lump_part)
+        coupled = partial_coupled
         gap = slave_gap - coupled / root_lump
         lam = jnp.where(flags, lam - 1.0 * gap, jnp.zeros_like(lam))
         slave_proj = jnp.sum(slave_float * lam[:, :, None], axis=1)

time: 133 us -> 174 us (1.31)
  local copies, waits for them, and re-layouts: 8.97 us -> 37.8 us
  waiting for transfers between devices: 8.9 us -> 37.4 us
  blocking collectives: 42.7 us -> 31.7 us
  other arithmetic: 13.3 us -> 4.72 us
  starting transfers between devices: 20.6 us -> 23.6 us
    gather x2, local copies, waits for them, and re-layouts: 2.06 us -> 28.3 us  [on_device(): pair_terms = weights_group * returned.reshape(mblocks, qpts)[block_group]]
    all_to_all x1 -> x2, waiting for transfers between devices: 4.57 us -> 25.8 us  [the longest x1 21.3 us: on_device(): lax.all_to_all(jnp.broadcast_to(weights[None], (group,) + weights.shape),...]
    all_to_all x1 -> x0, blocking collectives: 8.35 us -> none  [master_sum(): lax.all_to_all(spread, 'master', split_axis=0, concat_axis=0, tiled=True)]
    all_to_all x1, waiting for transfers between devices: 3.62 us -> 10.8 us  [on_device(): lax.all_to_all(outgoing_proj, everyone, split_axis=0, concat_axis=0, tile...]
    all_to_all x1 -> x2, starting transfers between devices: 4.02 us -> 10 us  [the longest x1 5.79 us: on_device(): lax.all_to_all(jnp.broadcast_to(jnp.stack([pair_block, pair_slave])[None]...]
    all_to_all x1, starting transfers between devices: 11.5 us -> 8.87 us  [on_device(): lax.all_to_all(outgoing_proj, everyone, split_axis=0, concat_axis=0, tile...]
    all_to_all x1, blocking collectives: 18.3 us -> 15.7 us  [on_device(): lax.all_to_all(outgoing_proj, everyone, split_axis=0, concat_axis=0, tile...]
    reduce_sum x2, other arithmetic: 2.1 us -> 0.3 us  [on_device(): own_proj = jnp.sum(master_float * disp[:, :, None], axis=1)]
  transfers between devices with their start and end apart: 4 -> 5, of which waited for: 2 -> 3; matrix products, arithmetic and copies ran while one was open for 20% -> 27% of each run, Pallas kernels for 14% -> 10%
where the time goes in v9:
time: 174 us
  local copies, waits for them, and re-layouts  37.8 us (22%)
  waiting for transfers between devices  37.4 us (21%)
  blocking collectives  31.7 us (18%)
  starting transfers between devices  23.6 us (14%)
  Pallas kernels  17.9 us (10%)
  between operations  14.4 us (8%)
  matrix products  6.27 us (4%)
  other arithmetic  4.72 us (3%)
    gather x2, local copies, waits for them, and re-layouts, on_device(): pair_terms = weights_group * returned.reshape(mblocks, qpts)[block_group]  28.3 us
    all_to_all x1, waiting for transfers between devices, on_device(): lax.all_to_all(jnp.broadcast_to(weights[None], (group,) + weights.shape),...  21.3 us
    pallas_call x1, Pallas kernels, build_tiles(): pl.pallas_call(functools.partial(tile_kernel, group), grid_spec=grid_spec...  17.9 us
    all_to_all x1, blocking collectives, on_device(): lax.all_to_all(outbound.reshape(peers, mb_dev, qpts), everyone, split_axi...  16 us
    all_to_all x1, blocking collectives, on_device(): lax.all_to_all(outgoing_proj, everyone, split_axis=0, concat_axis=0, tile...  15.7 us
    all_to_all x1, waiting for transfers between devices, on_device(): lax.all_to_all(outgoing_proj, everyone, split_axis=0, concat_axis=0, tile...  10.8 us
    all_to_all x1, starting transfers between devices, on_device(): lax.all_to_all(outgoing_proj, everyone, split_axis=0, concat_axis=0, tile...  8.87 us
    all_to_all x1, starting transfers between devices, on_device(): lax.all_to_all(jnp.broadcast_to(jnp.stack([pair_block, pair_slave])[None]...  5.79 us
  transfers between devices with their start and end apart: 5, of which 3 were waited for; matrix products, arithmetic and copies ran while one was open for 27% of the time, Pallas kernels for 10%

profile of v9, /device:TPU:1, one launch (start us, length us, event | category | flops | bytes accessed | tf_op | source)
XLA Modules:
  0.0 173.7 jit_solution(5149819187396008006)
XLA Ops:
  7.2 0.0 copy-start.4
  7.2 0.0 copy-start.1
  7.2 0.0 copy-start.10
  7.2 0.0 copy-start.13
  7.2 0.0 copy-start.7
  7.2 0.0 all-gather.2.cloned.1.call-start
  7.3 0.7 all-gather.2.cloned.1.call-update
  8.0 0.7 compare_select_fusion.2
  8.6 0.7 bitcast_add_fusion.mreq_ref
  9.3 3.3 %gather_fusion = s32[512]{0:T(512)S(1)} fusion(s32[128]{0:T(128)S(1)} %bitcast_add_fusion.mreq_ref, s32[1024]{0:T(1024)S(1)} %pad_clamp_fusion.1), kind=kCustom, calls=%fused_computation | custom fusion | bytes 6144 | tf_op jit(solution)/shard_map/gather | solution.py:107
  12.7 0.0 copy-done.1
  12.7 0.6 broadcast_in_dim.15
  13.3 5.8 %all-to-all-start = ((s32[8,2,512]{2,1,0:T(2,128)}), s32[8,2,512]{2,1,0:T(2,128)S(1)}, u32[]{:S(2)}, u32[]{:S(2)}) async-start(s32[8,2,512]{2,1,0:T(2,128)} %broadcast_in_dim.15), calls=%async_computation | async-start | bytes 65536 | tf_op jit(solution)/shard_map/all_to_all | solution.py:115
  19.1 0.0 copy-done.4
  19.1 0.0 copy-done.10
  19.1 0.1 fusion.14
  19.3 4.6 %all-to-all-done = s32[8,2,512]{2,1,0:T(2,128)S(1)} async-done(((s32[8,2,512]{2,1,0:T(2,128)}), s32[8,2,512]{2,1,0:T(2,128)S(1)}, u32[]{:S(2)}, u32[]{:S(2)}) %all-to-all-start) | async-done | bytes 32800 | tf_op jit(solution)/shard_map/all_to_all | solution.py:115
  23.8 0.7 broadcast_in_dim.18
  24.6 8.9 %all-to-all-start.2 = ((f32[128,4,128]{2,1,0:T(4,128)}), f32[128,4,128]{2,1,0:T(4,128)S(1)}, u32[]{:S(2)}, u32[]{:S(2)}) async-start(f32[128,4,128]{2,1,0:T(4,128)} %broadcast_in_dim.18), calls=%async_computation.2 | async-start | bytes 524288 | tf_op jit(solution)/shard_map/all_to_all | solution.py:141
  33.4 0.0 copy-done.13
  33.5 0.0 copy-done.7
  33.5 0.1 fusion.21.w_ref
  33.6 10.8 %all-to-all-done.2 = f32[128,4,128]{2,1,0:T(4,128)S(1)} async-done(((f32[128,4,128]{2,1,0:T(4,128)}), f32[128,4,128]{2,1,0:T(4,128)S(1)}, u32[]{:S(2)}, u32[]{:S(2)}) %all-to-all-start.2) | async-done | bytes 262176 | tf_op jit(solution)/shard_map/all_to_all | solution.py:141
  44.5 1.5 broadcast_in_dim.17
  45.9 4.3 %all-to-all-start.1 = ((f32[8,512,128]{2,1,0:T(8,128)}), f32[8,512,128]{2,1,0:T(8,128)S(1)}, u32[]{:S(2)}, u32[]{:S(2)}) async-start(f32[8,512,128]{2,1,0:T(8,128)} %broadcast_in_dim.17), calls=%async_computation.1 | async-start | bytes 4194304 | tf_op jit(solution)/shard_map/all_to_all | solution.py:112
  50.2 0.0 copy-start.5
  50.3 14.1 %gather_fusion.1 = f32[4096,128]{1,0:T(8,128)} fusion(f32[512,128]{1,0:T(8,128)S(1)} %bitcast.14, s32[4096]{0:T(1024)S(1)} %broadcast_clamp_fusion), kind=kCustom, calls=%fused_computation.1 | custom fusion | bytes 4210688 | tf_op jit(solution)/shard_map/gather | solution.py:142
  64.4 21.3 %all-to-all-done.1 = f32[8,512,128]{2,1,0:T(8,128)S(1)} async-done(((f32[8,512,128]{2,1,0:T(8,128)}), f32[8,512,128]{2,1,0:T(8,128)S(1)}, u32[]{:S(2)}, u32[]{:S(2)}) %all-to-all-start.1) | async-done | bytes 2097184 | tf_op jit(solution)/shard_map/all_to_all | solution.py:112
  85.6 0.0 copy-start.3
  85.6 0.8 fusion.20
  86.5 0.0 copy-done.5
  86.5 1.0 copy-done.3
  87.5 0.9 fusion.2
  88.5 0.1 copy-done
  88.6 0.6 fusion.6
  89.2 0.0 copy-done.9
  89.2 0.0 copy-done.11
  89.2 0.0 copy-done.12
  89.2 0.3 fusion.7
  89.6 1.0 gather_fusion.2
  90.6 0.6 fusion.11
  91.3 16.0 %all_to_all.30 = f32[128,4,128]{2,1,0:T(4,128)S(1)} all-to-all(f32[128,4,128]{2,1,0:T(4,128)S(1)} %bitcast.19), channel_id=1, replica_groups=mesh['slave'=16,'master'=8] {'slave','master'}, dimensions={0} | all-to-all | bytes 524288 | tf_op jit(solution)/shard_map/all_to_all | solution.py:152
  107.3 0.1 reduce_sum.103
  107.4 0.1 fusion.15
  107.6 0.1 fusion.16
  107.8 15.7 %all_to_all.31 = f32[128,4,128]{2,1,0:T(4,128)S(1)} all-to-all(f32[128,4,128]{2,1,0:T(4,128)S(1)} %broadcast_in_dim.20), channel_id=1, replica_groups=mesh['slave'=16,'master'=8] {'slave','master'}, dimensions={0} | all-to-all | bytes 524288 | tf_op jit(solution)/shard_map/all_to_all | solution.py:141
  123.5 14.2 %gather_fusion.3 = f32[4096,128]{1,0:T(8,128)} fusion(f32[512,128]{1,0:T(8,128)S(1)} %bitcast.15, s32[4096]{0:T(1024)S(1)} %broadcast_clamp_fusion), kind=kCustom, calls=%fused_computation.3 | custom fusion | bytes 4210688 | tf_op jit(solution)/shard_map/gather | solution.py:142
  137.7 0.0 copy-done.6
  137.7 2.6 %fusion = f32[16,128]{1,0:T(8,128)S(1)} fusion(f32[4096,128]{1,0:T(8,128)S(1)} %bitcast.18, f32[4096,128]{1,0:T(8,128)} %gather_fusion.3, s32[4096]{0:T(1024)S(1)} %bitcast.22), kind=kOutput, calls=%fused_computation.5 | convolution fusion | flops 101253120 | bytes 4218880 | tf_op jit(solution)/shard_map/dot_general | solution.py:143
  140.3 0.4 fusion.8
  140.6 0.0 copy-start.8
  140.6 0.0 copy-start.2
  140.7 0.3 fusion.9
  141.0 1.0 gather_fusion.4
  142.1 1.3 fusion.10
  143.4 0.0 copy-done.8
  143.4 4.6 %all-to-all-start.5 = ((f32[128,4,128]{2,1,0:T(4,128)}), f32[128,4,128]{2,1,0:T(4,128)S(1)}, u32[]{:S(2)}, u32[]{:S(2)}) async-start(f32[128,4,128]{2,1,0:T(4,128)} %bitcast.10), calls=%async_computation.5 | async-start | bytes 524288 | tf_op jit(solution)/shard_map/all_to_all | solution.py:152
  148.0 0.0 all-gather.2.cloned.1.call-done.basis_hbm
  148.0 0.0 copy-done.2
  148.0 17.9 %shard_map.139 = bf16[512,128,128]{2,1,0:T(8,128)(2,1)} custom-call(s32[512]{0:T(512)S(1)} %copy-done.1, s32[512]{0:T(512)S(1)} %copy-done.2, s32[128]{0:T(128)S(1)} %bitcast_add_fusion.mreq_ref, bf16[16,128,128]{2,1,0:T(8,128)(2,1)S(1)} %copy-done, bf16[512,128,128]{2,1,0:T(8,128)(2,1)} %all-gather.2.cloned.1.call-done.basis_hbm, f32[512,128]{1,0:T(8,128)S(1)} %fusion.21.w_ref), custom_call_target="tpu_custom_call" | custom-call | flops 2147483648 | bytes 21233664 | tf_op jit(solution)/shard_map/pallas_call | solution.py:62
  166.0 0.0 all-to-all-done.5
  166.0 0.1 reduce_sum.108
  166.1 0.1 fusion.17
  166.3 0.6 multiply_subtract_fusion
  (17 shorter events, 0.2 us)
Async XLA Ops:
  7.2 11.9 %copy-start.4 = (bf16[4,128,128]{2,1,0:T(8,128)(2,1)S(1)}, bf16[4,128,128]{2,1,0:T(8,128)(2,1)}, u32[]{:S(2)}) copy-start(bf16[4,128,128]{2,1,0:T(8,128)(2,1)} %param.13) | copy-start | bytes 393220
  7.2 5.5 %copy-start.1 = (s32[512]{0:T(512)S(1)}, s32[512]{0:T(512)}, u32[]{:S(2)}) copy-start(s32[512]{0:T(512)} %sidx_ref.1) | copy-start | bytes 6148
  7.2 11.9 %copy-start.10 = (f32[4,128]{1,0:T(4,128)S(1)}, f32[4,128]{1,0:T(4,128)}, u32[]{:S(2)}) copy-start(f32[4,128]{1,0:T(4,128)} %param.15) | copy-start | bytes 6148
  7.2 26.2 %copy-start.13 = (s32[512]{0:T(512)S(1)}, s32[512]{0:T(512)}, u32[]{:S(2)}) copy-start(s32[512]{0:T(512)} %param.22) | copy-start | bytes 6148
  7.2 26.3 %copy-start.7 = (f32[512,128]{1,0:T(8,128)S(1)}, f32[512,128]{1,0:T(8,128)}, u32[]{:S(2)}) copy-start(f32[512,128]{1,0:T(8,128)} %param.23) | copy-start | bytes 786436
  7.2 140.8 %all-gather.2.cloned.1.call-start = ((), (), s32[]{:S(2)}) async-start(), calls=%async_computation.6 | async-start | bytes 16908288 | tf_op jit(solution)/shard_map/all_gather | solution.py:94
  13.3 10.5 %all-to-all-start = ((s32[8,2,512]{2,1,0:T(2,128)}), s32[8,2,512]{2,1,0:T(2,128)S(1)}, u32[]{:S(2)}, u32[]{:S(2)}) async-start(s32[8,2,512]{2,1,0:T(2,128)} %broadcast_in_dim.15), calls=%async_computation | async-start | bytes 65536 | tf_op jit(solution)/shard_map/all_to_all | solution.py:115
  24.6 19.9 %all-to-all-start.2 = ((f32[128,4,128]{2,1,0:T(4,128)}), f32[128,4,128]{2,1,0:T(4,128)S(1)}, u32[]{:S(2)}, u32[]{:S(2)}) async-start(f32[128,4,128]{2,1,0:T(4,128)} %broadcast_in_dim.18), calls=%async_computation.2 | async-start | bytes 524288 | tf_op jit(solution)/shard_map/all_to_all | solution.py:141
  45.9 39.7 %all-to-all-start.1 = ((f32[8,512,128]{2,1,0:T(8,128)}), f32[8,512,128]{2,1,0:T(8,128)S(1)}, u32[]{:S(2)}, u32[]{:S(2)}) async-start(f32[8,512,128]{2,1,0:T(8,128)} %broadcast_in_dim.17), calls=%async_computation.1 | async-start | bytes 4194304 | tf_op jit(solution)/shard_map/all_to_all | solution.py:112
  50.2 36.2 %copy-start.5 = (s32[8,1,512]{2,1,0:T(1,128)}, s32[8,1,512]{2,1,0:T(1,128)S(1)}, u32[]{:S(2)}) copy-start(s32[8,1,512]{2,1,0:T(1,128)S(1)} %get-tuple-element.12) | copy-start | bytes 49156
  85.6 1.9 %copy-start.3 = (f32[4096,128]{1,0:T(8,128)S(1)}, f32[4096,128]{1,0:T(8,128)}, u32[]{:S(2)}) copy-start(f32[4096,128]{1,0:T(8,128)} %gather_fusion.1) | copy-start | bytes 6291460
  87.5 1.0 copy-start
  87.5 1.7 copy-start.9
  87.5 1.7 copy-start.11
  87.5 1.7 copy-start.12
  123.5 14.2 %copy-start.6 = (s32[8,1,512]{2,1,0:T(1,128)S(1)}, s32[8,1,512]{2,1,0:T(1,128)}, u32[]{:S(2)}) copy-start(s32[8,1,512]{2,1,0:T(1,128)} %copy-done.5) | copy-start | bytes 49156
  140.6 2.8 %copy-start.8 = (f32[16,128]{1,0:T(8,128)}, f32[16,128]{1,0:T(8,128)S(1)}, u32[]{:S(2)}) copy-start(f32[16,128]{1,0:T(8,128)S(1)} %subtract_select_fusion) | copy-start | bytes 24580
  140.6 7.4 %copy-start.2 = (s32[512]{0:T(512)S(1)}, s32[512]{0:T(512)}, u32[]{:S(2)}) copy-start(s32[512]{0:T(512)} %nidx_ref.1) | copy-start | bytes 6148
  143.4 22.6 %all-to-all-start.5 = ((f32[128,4,128]{2,1,0:T(4,128)}), f32[128,4,128]{2,1,0:T(4,128)S(1)}, u32[]{:S(2)}, u32[]{:S(2)}) async-start(f32[128,4,128]{2,1,0:T(4,128)} %bitcast.10), calls=%async_computation.5 | async-start | bytes 524288 | tf_op jit(solution)/shard_map/all_to_all | solution.py:152
Sparse Core Ops, SparseCore 0:
  11.2 96.3 all-gather.1

commit v10 on v8

--- a/solution.py
+++ b/solution.py
@@ -12,20 +12,27 @@
 GROUP = 64
 
 
-def tile_kernel(group, sidx_ref, nidx_ref, mreq_ref, slave_ref, basis_hbm, w_ref, out_ref, recv, sems):
+def tile_kernel(
+    group, sidx_ref, nidx_ref, mreq_ref, slave_ref, basis_hbm, w_ref, out_ref, recv, sems, landed
+):
     need = recv.shape[0]
 
     @pl.when(pl.program_id(0) == 0)
     def _():
         for r in range(need):
+            landed[r] = 0
             pltpu.make_async_copy(basis_hbm.at[mreq_ref[r]], recv.at[r], sems.at[r]).start()
-        for r in range(need):
-            pltpu.make_async_copy(basis_hbm.at[0], recv.at[r], sems.at[r]).wait()
 
     base = pl.program_id(0) * group
     for g in range(group):
         s = sidx_ref[base + g]
         r = nidx_ref[base + g]
+
+        @pl.when(landed[r] == 0)
+        def _():
+            pltpu.make_async_copy(basis_hbm.at[0], recv.at[r], sems.at[r]).wait()
+            landed[r] = 1
+
         left = slave_ref[s]
         w = w_ref[pl.ds(g, 1), :]
         right = (recv[r].astype(jnp.float32) * w).astype(jnp.bfloat16)
@@ -33,6 +40,14 @@
             left, right, (((1,), (1,)), ((), ())), preferred_element_type=jnp.float32
         )
         out_ref[g] = tile.astype(out_ref.dtype)
+
+    @pl.when(pl.program_id(0) == pl.num_programs(0) - 1)
+    def _():
+        for r in range(need):
+
+            @pl.when(landed[r] == 0)
+            def _():
+                pltpu.make_async_copy(basis_hbm.at[0], recv.at[r], sems.at[r]).wait()
 
 
 def build_tiles(slave_basis, every_basis, request, pair_slave, pair_need, weights):
@@ -52,6 +67,7 @@
         scratch_shapes=[
             pltpu.VMEM((need, nodes, qpts), jnp.bfloat16),
             pltpu.SemaphoreType.DMA((need,)),
+            pltpu.SMEM((need,), jnp.int32),
         ],
     )
     cost = pl.CostEstimate(

time: 133 us -> 206 us (1.55)
  Pallas kernels: 18.2 us -> 91.3 us
    pallas_call x1, Pallas kernels: 18.2 us -> 91.3 us  [build_tiles(): pl.pallas_call(functools.partial(tile_kernel, group), grid_spec=grid_spec...]
  transfers between devices with their start and end apart: 4 -> 4, of which waited for: 2 -> 2; matrix products, arithmetic and copies ran while one was open for 20% -> 13% of each run, Pallas kernels for 14% -> 45%
where the time goes in v10:
time: 206 us; the launch traced here: 205 us
  Pallas kernels  91.3 us (44%)
  blocking collectives  42.7 us (21%)
  starting transfers between devices  20.7 us (10%)
  between operations  14.3 us (7%)
  other arithmetic  13.3 us (6%)
  local copies, waits for them, and re-layouts  8.97 us (4%)
  waiting for transfers between devices  8.9 us (4%)
  matrix products  4.62 us (2%)
    pallas_call x1, Pallas kernels, build_tiles(): pl.pallas_call(functools.partial(tile_kernel, group), grid_spec=grid_spec...  91.3 us
    all_to_all x1, blocking collectives, on_device(): lax.all_to_all(outgoing_proj, everyone, split_axis=0, concat_axis=0, tile...  18.3 us
    all_to_all x1, blocking collectives, on_device(): lax.all_to_all(outbound.reshape(peers, mb_dev, qpts), everyone, split_axi...  16.1 us
    all_to_all x1, starting transfers between devices, on_device(): lax.all_to_all(outgoing_proj, everyone, split_axis=0, concat_axis=0, tile...  11.5 us
    all_to_all x1, blocking collectives, master_sum(): lax.all_to_all(spread, 'master', split_axis=0, concat_axis=0, tiled=True)  8.35 us
    all_to_all x1, starting transfers between devices, on_device(): lax.all_to_all(outbound.reshape(peers, mb_dev, qpts), everyone, split_axi...  5.11 us
    all_to_all x1, waiting for transfers between devices, master_sum(): lax.all_to_all(spread, 'master', split_axis=0, concat_axis=0, tiled=True)  4.57 us
  transfers between devices with their start and end apart: 4, of which 2 were waited for; matrix products, arithmetic and copies ran while one was open for 13% of the time, Pallas kernels for 45%

profile of v10, /device:TPU:1, one launch (start us, length us, event | category | flops | bytes accessed | tf_op | source)
XLA Modules:
  0.0 204.8 jit_solution(9515726156553805489)
XLA Ops:
  7.2 0.0 copy-start.2
  7.2 0.0 copy-start.1
  7.2 0.0 copy-start
  7.2 0.0 copy-start.5
  7.2 0.0 all-gather.2.cloned.1.call-start
  7.3 0.7 all-gather.2.cloned.1.call-update
  7.9 1.1 fusion.10
  9.0 0.7 broadcast_in_dim.15
  9.7 11.5 %all-to-all-start = ((f32[128,4,128]{2,1,0:T(4,128)}), f32[128,4,128]{2,1,0:T(4,128)S(1)}, u32[]{:S(2)}, u32[]{:S(2)}) async-start(f32[128,4,128]{2,1,0:T(4,128)} %broadcast_in_dim.15), calls=%async_computation | async-start | bytes 524288 | tf_op jit(solution)/shard_map/all_to_all | solution.py:148
  21.2 0.7 compare_select_fusion.2
  21.9 0.7 bitcast_add_fusion.mreq_ref
  22.6 3.3 %gather_fusion = s32[512]{0:T(512)S(1)} fusion(s32[128]{0:T(128)S(1)} %bitcast_add_fusion.mreq_ref, s32[1024]{0:T(1024)S(1)} %pad_clamp_fusion.2), kind=kCustom, calls=%fused_computation | custom fusion | bytes 6144 | tf_op jit(solution)/shard_map/gather | solution.py:130
  26.0 0.7 broadcast_multiply_fusion
  26.6 1.1 fusion.20.w_ref
  27.7 0.9 fusion.21
  28.6 3.6 %all-to-all-done = f32[128,4,128]{2,1,0:T(4,128)S(1)} async-done(((f32[128,4,128]{2,1,0:T(4,128)}), f32[128,4,128]{2,1,0:T(4,128)S(1)}, u32[]{:S(2)}, u32[]{:S(2)}) %all-to-all-start) | async-done | bytes 262176 | tf_op jit(solution)/shard_map/all_to_all | solution.py:148
  32.3 1.0 gather_fusion.1
  33.3 0.9 fusion.18
  34.2 1.7 fusion.1
  35.9 0.7 broadcast_in_dim.17
  36.5 4.0 %all-to-all-start.1 = ((f32[8,2,16,128]{3,2,1,0:T(8,128)}), f32[8,2,16,128]{3,2,1,0:T(8,128)S(1)}, u32[]{:S(2)}, u32[]{:S(2)}) async-start(f32[8,2,16,128]{3,2,1,0:T(8,128)} %broadcast_in_dim.17), calls=%async_computation.1 | async-start | bytes 262144 | tf_op jit(solution)/shard_map/all_to_all | solution.py:92
  40.6 0.7 compare_select_fusion.1
  41.3 4.6 %all-to-all-done.1 = f32[8,2,16,128]{3,2,1,0:T(8,128)S(1)} async-done(((f32[8,2,16,128]{3,2,1,0:T(8,128)}), f32[8,2,16,128]{3,2,1,0:T(8,128)S(1)}, u32[]{:S(2)}, u32[]{:S(2)}) %all-to-all-start.1) | async-done | bytes 131104 | tf_op jit(solution)/shard_map/all_to_all | solution.py:92
  45.8 0.7 fusion.30
  46.6 1.4 fusion.3
  48.0 1.0 gather_fusion.2
  49.0 0.6 fusion.7
  49.7 16.1 %all_to_all.30 = f32[128,4,128]{2,1,0:T(4,128)S(1)} all-to-all(f32[128,4,128]{2,1,0:T(4,128)S(1)} %bitcast.29), channel_id=1, replica_groups=mesh['slave'=16,'master'=8] {'slave','master'}, dimensions={0} | all-to-all | bytes 524288 | tf_op jit(solution)/shard_map/all_to_all | solution.py:162
  65.8 0.1 reduce_sum.122
  65.9 1.0 fusion.11
  67.0 0.7 multiply_subtract_fusion.1
  67.7 1.0 fusion.12
  68.8 18.3 %all_to_all.31 = f32[128,4,128]{2,1,0:T(4,128)S(1)} all-to-all(f32[128,4,128]{2,1,0:T(4,128)S(1)} %broadcast_in_dim.19), channel_id=1, replica_groups=mesh['slave'=16,'master'=8] {'slave','master'}, dimensions={0} | all-to-all | bytes 524288 | tf_op jit(solution)/shard_map/all_to_all | solution.py:148
  87.0 1.0 gather_fusion.3
  88.1 0.9 fusion.15
  89.0 0.0 copy-done
  89.0 0.3 fusion.4
  89.4 8.4 %all_to_all.32 = f32[8,16,128]{2,1,0:T(8,128)S(1)} all-to-all(f32[8,16,128]{2,1,0:T(8,128)S(1)} %broadcast_in_dim.20), channel_id=1, replica_groups=mesh['slave'=16,'master'=8] {'master'}, dimensions={0} | all-to-all | bytes 131072 | tf_op jit(solution)/shard_map/all_to_all | solution.py:92
  97.7 0.0 copy-done.5
  97.8 0.0 copy-start.4
  97.8 0.3 fusion.5
  98.1 1.0 gather_fusion.4
  99.2 1.3 fusion.6
  100.5 5.1 %all-to-all-start.5 = ((f32[128,4,128]{2,1,0:T(4,128)}), f32[128,4,128]{2,1,0:T(4,128)S(1)}, u32[]{:S(2)}, u32[]{:S(2)}) async-start(f32[128,4,128]{2,1,0:T(4,128)} %bitcast.10), calls=%async_computation.5 | async-start | bytes 524288 | tf_op jit(solution)/shard_map/all_to_all | solution.py:162
  105.6 0.0 copy-start.3
  105.6 0.0 all-gather.2.cloned.1.call-done.basis_hbm
  105.7 0.0 copy-done.2
  105.7 0.0 copy-done.1
  105.7 91.3 %shard_map.139 = bf16[512,128,128]{2,1,0:T(8,128)(2,1)} custom-call(s32[512]{0:T(512)S(1)} %copy-done.1, s32[512]{0:T(512)S(1)} %copy-done.2, s32[128]{0:T(128)S(1)} %bitcast_add_fusion.mreq_ref, bf16[16,128,128]{2,1,0:T(8,128)(2,1)S(1)} %copy-done, bf16[512,128,128]{2,1,0:T(8,128)(2,1)} %all-gather.2.cloned.1.call-done.basis_hbm, f32[512,128]{1,0:T(8,128)S(1)} %fusion.20.w_ref), custom_call_target="tpu_custom_call" | custom-call | flops 2147483648 | bytes 21233664 | tf_op jit(solution)/shard_map/pallas_call | solution.py:78
  197.0 0.0 copy-done.4
  197.0 0.0 all-to-all-done.5
  197.1 0.1 reduce_sum.128
  197.2 0.0 copy-done.3
  197.2 0.1 fusion.13
  197.3 0.6 multiply_subtract_fusion
  (10 shorter events, 0.1 us)
Async XLA Ops:
  7.2 98.5 %copy-start.2 = (s32[512]{0:T(512)S(1)}, s32[512]{0:T(512)}, u32[]{:S(2)}) copy-start(s32[512]{0:T(512)} %nidx_ref.1) | copy-start | bytes 6148
  7.2 98.5 %copy-start.1 = (s32[512]{0:T(512)S(1)}, s32[512]{0:T(512)}, u32[]{:S(2)}) copy-start(s32[512]{0:T(512)} %sidx_ref.1) | copy-start | bytes 6148
  7.2 81.8 %copy-start = (bf16[16,128,128]{2,1,0:T(8,128)(2,1)S(1)}, bf16[16,128,128]{2,1,0:T(8,128)(2,1)}, u32[]{:S(2)}) copy-start(bf16[16,128,128]{2,1,0:T(8,128)(2,1)} %slave_ref.1) | copy-start | bytes 1572868
  7.2 90.5 %copy-start.5 = (f32[16,128]{1,0:T(8,128)S(1)}, f32[16,128]{1,0:T(8,128)}, u32[]{:S(2)}) copy-start(f32[16,128]{1,0:T(8,128)} %param.14) | copy-start | bytes 24580
  7.2 98.4 %all-gather.2.cloned.1.call-start = ((), (), s32[]{:S(2)}) async-start(), calls=%async_computation.6 | async-start | bytes 16908288 | tf_op jit(solution)/shard_map/all_gather | solution.py:117
  9.7 22.5 %all-to-all-start = ((f32[128,4,128]{2,1,0:T(4,128)}), f32[128,4,128]{2,1,0:T(4,128)S(1)}, u32[]{:S(2)}, u32[]{:S(2)}) async-start(f32[128,4,128]{2,1,0:T(4,128)} %broadcast_in_dim.15), calls=%async_computation | async-start | bytes 524288 | tf_op jit(solution)/shard_map/all_to_all | solution.py:148
  36.5 9.3 %all-to-all-start.1 = ((f32[8,2,16,128]{3,2,1,0:T(8,128)}), f32[8,2,16,128]{3,2,1,0:T(8,128)S(1)}, u32[]{:S(2)}, u32[]{:S(2)}) async-start(f32[8,2,16,128]{3,2,1,0:T(8,128)} %broadcast_in_dim.17), calls=%async_computation.1 | async-start | bytes 262144 | tf_op jit(solution)/shard_map/all_to_all | solution.py:92
  97.8 99.3 %copy-start.4 = (f32[16,128]{1,0:T(8,128)}, f32[16,128]{1,0:T(8,128)S(1)}, u32[]{:S(2)}) copy-start(f32[16,128]{1,0:T(8,128)S(1)} %subtract_select_fusion) | copy-start | bytes 24580
  100.5 96.5 %all-to-all-start.5 = ((f32[128,4,128]{2,1,0:T(4,128)}), f32[128,4,128]{2,1,0:T(4,128)S(1)}, u32[]{:S(2)}, u32[]{:S(2)}) async-start(f32[128,4,128]{2,1,0:T(4,128)} %bitcast.10), calls=%async_computation.5 | async-start | bytes 524288 | tf_op jit(solution)/shard_map/all_to_all | solution.py:162
  105.6 91.6 %copy-start.3 = (bf16[4,128,128]{2,1,0:T(8,128)(2,1)S(1)}, bf16[4,128,128]{2,1,0:T(8,128)(2,1)}, u32[]{:S(2)}) copy-start(bf16[4,128,128]{2,1,0:T(8,128)(2,1)} %param.13) | copy-start | bytes 393220
Sparse Core Ops, SparseCore 0:
  11.2 86.8 all-gather.1

commit v11 on v8

--- a/solution.py
+++ b/solution.py
@@ -120,14 +120,15 @@
     master_float = master_basis.astype(jnp.float32)
     squares = jnp.square(slave_float)
     lump_part = jnp.sum(squares * slave_weight[:, None, :], axis=2)
+    gram = jnp.einsum("mnq,mnr->mqr", master_float, master_float, precision=high)
 
     stored = build_tiles(slave_basis, every_basis, request, pair_slave, pair_need, weights)
     lam = pressure
     disp = master_disp
     flags = active == 1
     root_lump = None
+    own_proj = jnp.sum(master_float * disp[:, :, None], axis=1)
     for update in range(ITERS):
-        own_proj = jnp.sum(master_float * disp[:, :, None], axis=1)
         outgoing_proj = jnp.broadcast_to(own_proj[None], (peers,) + own_proj.shape)
         returned = lax.all_to_all(outgoing_proj, everyone, split_axis=0, concat_axis=0, tiled=True)
         pair_terms = weights * returned.reshape(mblocks, qpts)[pair_block]
@@ -151,6 +152,8 @@
         own_load = jnp.sum(inbound, axis=0)
         force = jnp.sum(master_float * own_load[:, None, :], axis=2)
         disp = disp - 0.05 * force
+        if update < ITERS - 1:
+            own_proj = own_proj - 0.05 * jnp.einsum("mq,mqr->mr", own_load, gram, precision=high)
     return (lam, disp, stored)
 
 

time: 133 us -> 131 us (0.985)
  blocking collectives: 42.7 us -> 26.8 us
  waiting for transfers between devices: 8.9 us -> 18.7 us
  starting transfers between devices: 20.6 us -> 25.8 us
  other arithmetic: 13.3 us -> 10.5 us
  matrix products: 4.62 us -> 6.85 us
    all_to_all x1 -> x0, blocking collectives: 16.1 us -> none  [on_device(): lax.all_to_all(outbound.reshape(peers, mb_dev, qpts), everyone, split_axi...]
    all_to_all x1 -> x2, waiting for transfers between devices: 0.01 us -> 9.8 us  [on_device(): lax.all_to_all(outbound.reshape(peers, mb_dev, qpts), everyone, split_axi...]
    all_to_all x1 -> x2, starting transfers between devices: 5.1 us -> 10.3 us  [on_device(): lax.all_to_all(outbound.reshape(peers, mb_dev, qpts), everyone, split_axi...]
    dot_general x0 -> x2, matrix products: none -> 1.53 us  [the longest x1 1.21 us: on_device(): jnp.einsum('mnq,mnr->mqr', master_float, master_float, precision=high)]
  transfers between devices with their start and end apart: 4 -> 5, of which waited for: 2 -> 3; matrix products, arithmetic and copies ran while one was open for 20% -> 19% of each run, Pallas kernels for 14% -> 14%
where the time goes in v11:
time: 131 us; the launch traced here: 130 us
  blocking collectives  26.8 us (20%)
  starting transfers between devices  25.8 us (20%)
  waiting for transfers between devices  18.7 us (14%)
  Pallas kernels  18.2 us (14%)
  between operations  14.3 us (11%)
  other arithmetic  10.5 us (8%)
  local copies, waits for them, and re-layouts  8.97 us (7%)
  matrix products  6.85 us (5%)
    pallas_call x1, Pallas kernels, build_tiles(): pl.pallas_call(functools.partial(tile_kernel, group), grid_spec=grid_spec...  18.2 us
    all_to_all x1, blocking collectives, on_device(): lax.all_to_all(outgoing_proj, everyone, split_axis=0, concat_axis=0, tile...  18.2 us
    all_to_all x1, starting transfers between devices, on_device(): lax.all_to_all(outgoing_proj, everyone, split_axis=0, concat_axis=0, tile...  11.5 us
    all_to_all x2, starting transfers between devices, on_device(): lax.all_to_all(outbound.reshape(peers, mb_dev, qpts), everyone, split_axi...  10.3 us
    all_to_all x2, waiting for transfers between devices, on_device(): lax.all_to_all(outbound.reshape(peers, mb_dev, qpts), everyone, split_axi...  9.8 us
    all_to_all x1, blocking collectives, master_sum(): lax.all_to_all(spread, 'master', split_axis=0, concat_axis=0, tiled=True)  8.61 us
    all_to_all x1, waiting for transfers between devices, master_sum(): lax.all_to_all(spread, 'master', split_axis=0, concat_axis=0, tiled=True)  4.57 us
    all_to_all x1, starting transfers between devices, master_sum(): lax.all_to_all(spread, 'master', split_axis=0, concat_axis=0, tiled=True)  4.02 us
  transfers between devices with their start and end apart: 5, of which 3 were waited for; matrix products, arithmetic and copies ran while one was open for 19% of the time, Pallas kernels for 14%

profile of v11, /device:TPU:1, one launch (start us, length us, event | category | flops | bytes accessed | tf_op | source)
XLA Modules:
  0.0 130.2 jit_solution(13354130817021953276)
XLA Ops:
  7.2 0.0 copy-start.2
  7.2 0.0 copy-start.1
  7.2 0.0 copy-start
  7.2 0.0 copy-start.5
  7.2 0.0 all-gather.2.cloned.1.call-start
  7.3 0.7 all-gather.2.cloned.1.call-update
  7.9 1.1 fusion.10
  9.0 0.7 broadcast_in_dim.15
  9.7 11.5 %all-to-all-start = ((f32[128,4,128]{2,1,0:T(4,128)}), f32[128,4,128]{2,1,0:T(4,128)S(1)}, u32[]{:S(2)}, u32[]{:S(2)}) async-start(f32[128,4,128]{2,1,0:T(4,128)} %broadcast_in_dim.15), calls=%async_computation | async-start | bytes 524288 | tf_op jit(solution)/shard_map/all_to_all | solution.py:133
  21.2 0.7 compare_select_fusion.2
  21.9 0.7 bitcast_add_fusion.mreq_ref
  22.6 3.3 %gather_fusion = s32[512]{0:T(512)S(1)} fusion(s32[128]{0:T(128)S(1)} %bitcast_add_fusion.mreq_ref, s32[1024]{0:T(1024)S(1)} %pad_clamp_fusion.2), kind=kCustom, calls=%fused_computation | custom fusion | bytes 6144 | tf_op jit(solution)/shard_map/gather | solution.py:114
  26.0 0.7 broadcast_multiply_fusion
  26.6 1.1 fusion.19.w_ref
  27.7 0.9 fusion.20
  28.6 3.6 %all-to-all-done = f32[128,4,128]{2,1,0:T(4,128)S(1)} async-done(((f32[128,4,128]{2,1,0:T(4,128)}), f32[128,4,128]{2,1,0:T(4,128)S(1)}, u32[]{:S(2)}, u32[]{:S(2)}) %all-to-all-start) | async-done | bytes 262176 | tf_op jit(solution)/shard_map/all_to_all | solution.py:133
  32.3 1.0 gather_fusion.1
  33.3 0.9 fusion.17
  34.2 1.7 %fusion.1 = (f32[16,128]{1,0:T(8,128)S(1)}, f32[16,128]{1,0:T(8,128)S(1)}) fusion(bf16[16,128,128]{2,1,0:T(8,128)(2,1)} %slave_ref.1, f32[16,128]{1,0:T(8,128)S(1)} %fusion.20, f32[16,128]{1,0:T(8,128)S(1)} %fusion.17), kind=kLoop, calls=%fused_computation.11 | loop fusion | flops 1568768 | bytes 557056 | tf_op jit(solution)/shard_map/reduce_sum | solution.py:122
  35.9 0.7 broadcast_in_dim.17
  36.5 4.0 %all-to-all-start.1 = ((f32[8,2,16,128]{3,2,1,0:T(8,128)}), f32[8,2,16,128]{3,2,1,0:T(8,128)S(1)}, u32[]{:S(2)}, u32[]{:S(2)}) async-start(f32[8,2,16,128]{3,2,1,0:T(8,128)} %broadcast_in_dim.17), calls=%async_computation.1 | async-start | bytes 262144 | tf_op jit(solution)/shard_map/all_to_all | solution.py:76
  40.6 0.7 compare_select_fusion.1
  41.3 4.6 %all-to-all-done.1 = f32[8,2,16,128]{3,2,1,0:T(8,128)S(1)} async-done(((f32[8,2,16,128]{3,2,1,0:T(8,128)}), f32[8,2,16,128]{3,2,1,0:T(8,128)S(1)}, u32[]{:S(2)}, u32[]{:S(2)}) %all-to-all-start.1) | async-done | bytes 131104 | tf_op jit(solution)/shard_map/all_to_all | solution.py:76
  45.8 0.7 fusion.29
  46.6 1.4 %fusion.3 = f32[16,128]{1,0:T(8,128)S(1)} fusion(bf16[16,128,128]{2,1,0:T(8,128)(2,1)} %slave_ref.1, f32[16,128]{1,0:T(8,128)S(1)} %get-tuple-element.11), kind=kLoop, calls=%fused_computation.13 | loop fusion | flops 784384 | bytes 540672 | tf_op jit(solution)/shard_map/reduce_sum | solution.py:145
  48.0 1.0 gather_fusion.2
  49.0 1.3 %fusion.7 = f32[512,128]{1,0:T(8,128)} fusion(s32[512]{0:T(512)S(1)} %gather_fusion, f32[512,128]{1,0:T(8,128)S(1)} %fusion.19.w_ref, f32[512,128]{1,0:T(8,128)S(1)} %gather_fusion.2), kind=kOutput, calls=%fused_computation.18 | convolution fusion | flops 402980864 | bytes 788480 | tf_op jit(solution)/shard_map/dot_general | solution.py:146
  50.4 5.4 %all-to-all-start.2 = ((f32[128,4,128]{2,1,0:T(4,128)}), f32[128,4,128]{2,1,0:T(4,128)S(1)}, u32[]{:S(2)}, u32[]{:S(2)}) async-start(f32[128,4,128]{2,1,0:T(4,128)} %bitcast.8), calls=%async_computation.2 | async-start | bytes 524288 | tf_op jit(solution)/shard_map/all_to_all | solution.py:147
  55.8 1.2 fusion.30
  57.0 9.8 %all-to-all-done.2 = f32[128,4,128]{2,1,0:T(4,128)S(1)} async-done(((f32[128,4,128]{2,1,0:T(4,128)}), f32[128,4,128]{2,1,0:T(4,128)S(1)}, u32[]{:S(2)}, u32[]{:S(2)}) %all-to-all-start.2) | async-done | bytes 262176 | tf_op jit(solution)/shard_map/all_to_all | solution.py:147
  66.8 0.1 reduce_sum.113
  67.0 0.3 fusion.31
  67.3 18.2 %all_to_all.30 = f32[128,4,128]{2,1,0:T(4,128)S(1)} all-to-all(f32[128,4,128]{2,1,0:T(4,128)S(1)} %broadcast_in_dim.19), channel_id=1, replica_groups=mesh['slave'=16,'master'=8] {'slave','master'}, dimensions={0} | all-to-all | bytes 524288 | tf_op jit(solution)/shard_map/all_to_all | solution.py:133
  85.5 1.0 gather_fusion.3
  86.5 0.9 fusion.14
  87.4 0.0 copy-done
  87.4 0.3 fusion.4
  87.8 8.6 %all_to_all.31 = f32[8,16,128]{2,1,0:T(8,128)S(1)} all-to-all(f32[8,16,128]{2,1,0:T(8,128)S(1)} %broadcast_in_dim.20), channel_id=1, replica_groups=mesh['slave'=16,'master'=8] {'master'}, dimensions={0} | all-to-all | bytes 131072 | tf_op jit(solution)/shard_map/all_to_all | solution.py:76
  96.4 0.0 copy-done.5
  96.5 0.0 copy-start.4
  96.5 0.3 fusion.5
  96.8 1.0 gather_fusion.4
  97.9 1.3 %fusion.6 = f32[512,128]{1,0:T(8,128)} fusion(s32[512]{0:T(512)S(1)} %gather_fusion, f32[512,128]{1,0:T(8,128)S(1)} %fusion.19.w_ref, f32[512,128]{1,0:T(8,128)S(1)} %gather_fusion.4), kind=kOutput, calls=%fused_computation.17 | convolution fusion | flops 402980864 | bytes 788480 | tf_op jit(solution)/shard_map/dot_general | solution.py:146
  99.2 4.8 %all-to-all-start.5 = ((f32[128,4,128]{2,1,0:T(4,128)}), f32[128,4,128]{2,1,0:T(4,128)S(1)}, u32[]{:S(2)}, u32[]{:S(2)}) async-start(f32[128,4,128]{2,1,0:T(4,128)} %bitcast.14), calls=%async_computation.5 | async-start | bytes 524288 | tf_op jit(solution)/shard_map/all_to_all | solution.py:147
  104.0 0.0 copy-start.3
  104.0 0.0 copy-start.6
  104.1 0.0 all-gather.2.cloned.1.call-done.basis_hbm
  104.1 0.0 copy-done.2
  104.1 0.0 copy-done.1
  104.1 18.2 %shard_map.139 = bf16[512,128,128]{2,1,0:T(8,128)(2,1)} custom-call(s32[512]{0:T(512)S(1)} %copy-done.1, s32[512]{0:T(512)S(1)} %copy-done.2, s32[128]{0:T(128)S(1)} %bitcast_add_fusion.mreq_ref, bf16[16,128,128]{2,1,0:T(8,128)(2,1)S(1)} %copy-done, bf16[512,128,128]{2,1,0:T(8,128)(2,1)} %all-gather.2.cloned.1.call-done.basis_hbm, f32[512,128]{1,0:T(8,128)S(1)} %fusion.19.w_ref), custom_call_target="tpu_custom_call" | custom-call | flops 2147483648 | bytes 21233664 | tf_op jit(solution)/shard_map/pallas_call | solution.py:62
  122.3 0.0 copy-done.4
  122.3 0.0 all-to-all-done.5
  122.4 0.1 reduce_sum.118
  122.5 0.0 copy-done.3
  122.5 0.2 fusion.11
  122.7 0.0 copy-done.6
  122.7 0.6 multiply_subtract_fusion
  (11 shorter events, 0.1 us)
Async XLA Ops:
  7.2 96.9 %copy-start.2 = (s32[512]{0:T(512)S(1)}, s32[512]{0:T(512)}, u32[]{:S(2)}) copy-start(s32[512]{0:T(512)} %nidx_ref.1) | copy-start | bytes 6148
  7.2 96.9 %copy-start.1 = (s32[512]{0:T(512)S(1)}, s32[512]{0:T(512)}, u32[]{:S(2)}) copy-start(s32[512]{0:T(512)} %sidx_ref.1) | copy-start | bytes 6148
  7.2 80.2 %copy-start = (bf16[16,128,128]{2,1,0:T(8,128)(2,1)S(1)}, bf16[16,128,128]{2,1,0:T(8,128)(2,1)}, u32[]{:S(2)}) copy-start(bf16[16,128,128]{2,1,0:T(8,128)(2,1)} %slave_ref.1) | copy-start | bytes 1572868
  7.2 89.2 %copy-start.5 = (f32[16,128]{1,0:T(8,128)S(1)}, f32[16,128]{1,0:T(8,128)}, u32[]{:S(2)}) copy-start(f32[16,128]{1,0:T(8,128)} %param.14) | copy-start | bytes 24580
  7.2 96.9 %all-gather.2.cloned.1.call-start = ((), (), s32[]{:S(2)}) async-start(), calls=%async_computation.6 | async-start | bytes 16908288 | tf_op jit(solution)/shard_map/all_gather | solution.py:101
  9.7 22.5 %all-to-all-start = ((f32[128,4,128]{2,1,0:T(4,128)}), f32[128,4,128]{2,1,0:T(4,128)S(1)}, u32[]{:S(2)}, u32[]{:S(2)}) async-start(f32[128,4,128]{2,1,0:T(4,128)} %broadcast_in_dim.15), calls=%async_computation | async-start | bytes 524288 | tf_op jit(solution)/shard_map/all_to_all | solution.py:133
  36.5 9.3 %all-to-all-start.1 = ((f32[8,2,16,128]{3,2,1,0:T(8,128)}), f32[8,2,16,128]{3,2,1,0:T(8,128)S(1)}, u32[]{:S(2)}, u32[]{:S(2)}) async-start(f32[8,2,16,128]{3,2,1,0:T(8,128)} %broadcast_in_dim.17), calls=%async_computation.1 | async-start | bytes 262144 | tf_op jit(solution)/shard_map/all_to_all | solution.py:76
  50.4 16.5 %all-to-all-start.2 = ((f32[128,4,128]{2,1,0:T(4,128)}), f32[128,4,128]{2,1,0:T(4,128)S(1)}, u32[]{:S(2)}, u32[]{:S(2)}) async-start(f32[128,4,128]{2,1,0:T(4,128)} %bitcast.8), calls=%async_computation.2 | async-start | bytes 524288 | tf_op jit(solution)/shard_map/all_to_all | solution.py:147
  96.5 25.9 %copy-start.4 = (f32[16,128]{1,0:T(8,128)}, f32[16,128]{1,0:T(8,128)S(1)}, u32[]{:S(2)}) copy-start(f32[16,128]{1,0:T(8,128)S(1)} %subtract_select_fusion) | copy-start | bytes 24580
  99.2 23.2 %all-to-all-start.5 = ((f32[128,4,128]{2,1,0:T(4,128)}), f32[128,4,128]{2,1,0:T(4,128)S(1)}, u32[]{:S(2)}, u32[]{:S(2)}) async-start(f32[128,4,128]{2,1,0:T(4,128)} %bitcast.14), calls=%async_computation.5 | async-start | bytes 524288 | tf_op jit(solution)/shard_map/all_to_all | solution.py:147
  104.0 18.5 %copy-start.3 = (bf16[4,128,128]{2,1,0:T(8,128)(2,1)S(1)}, bf16[4,128,128]{2,1,0:T(8,128)(2,1)}, u32[]{:S(2)}) copy-start(bf16[4,128,128]{2,1,0:T(8,128)(2,1)} %param.13) | copy-start | bytes 393220
  104.0 18.7 %copy-start.6 = (f32[4,128]{1,0:T(4,128)S(1)}, f32[4,128]{1,0:T(4,128)}, u32[]{:S(2)}) copy-start(f32[4,128]{1,0:T(4,128)} %param.15) | copy-start | bytes 6148
Sparse Core Ops, SparseCore 0:
  11.2 87.1 all-gather.1

commit v12 on v11

--- a/solution.py
+++ b/solution.py
@@ -132,7 +132,7 @@
         outgoing_proj = jnp.broadcast_to(own_proj[None], (peers,) + own_proj.shape)
         returned = lax.all_to_all(outgoing_proj, everyone, split_axis=0, concat_axis=0, tiled=True)
         pair_terms = weights * returned.reshape(mblocks, qpts)[pair_block]
-        slave_terms = jnp.dot(slave_onehot, pair_terms, precision=high)
+        slave_terms = jnp.dot(slave_onehot, pair_terms, precision=lax.Precision.HIGH)
         partial_coupled = jnp.sum(slave_float * slave_terms[:, None, :], axis=2)
         if update == 0:
             both = master_sum(jnp.stack([lump_part, partial_coupled]))
@@ -143,7 +143,9 @@
         gap = slave_gap - coupled / root_lump
         lam = jnp.where(flags, lam - 1.0 * gap, jnp.zeros_like(lam))
         slave_proj = jnp.sum(slave_float * lam[:, :, None], axis=1)
-        outbound = jnp.dot(block_onehot, weights * slave_proj[pair_slave], precision=high)
+        outbound = jnp.dot(
+            block_onehot, weights * slave_proj[pair_slave], precision=lax.Precision.HIGH
+        )
         inbound = lax.all_to_all(
             outbound.reshape(peers, mb_dev, qpts), everyone, split_axis=0, concat_axis=0, tiled=True
         )

time: 131 us -> 131 us (level)
  no operation moved by 1% of the time
where the time goes in v12:
time: 131 us; the launch traced here: 130 us
  blocking collectives  27 us (21%)
  starting transfers between devices  25.5 us (19%)
  waiting for transfers between devices  18.7 us (14%)
  Pallas kernels  18.2 us (14%)
  between operations  14.3 us (11%)
  other arithmetic  10.5 us (8%)
  local copies, waits for them, and re-layouts  8.97 us (7%)
  matrix products  6.42 us (5%)
    pallas_call x1, Pallas kernels, build_tiles(): pl.pallas_call(functools.partial(tile_kernel, group), grid_spec=grid_spec...  18.2 us
    all_to_all x1, blocking collectives, on_device(): lax.all_to_all(outgoing_proj, everyone, split_axis=0, concat_axis=0, tile...  18.1 us
    all_to_all x1, starting transfers between devices, on_device(): lax.all_to_all(outgoing_proj, everyone, split_axis=0, concat_axis=0, tile...  11.5 us
    all_to_all x2, starting transfers between devices, on_device(): lax.all_to_all(outbound.reshape(peers, mb_dev, qpts), everyone, split_axi...  9.99 us
    all_to_all x2, waiting for transfers between devices, on_device(): lax.all_to_all(outbound.reshape(peers, mb_dev, qpts), everyone, split_axi...  9.8 us
    all_to_all x1, blocking collectives, master_sum(): lax.all_to_all(spread, 'master', split_axis=0, concat_axis=0, tiled=True)  8.89 us
    all_to_all x1, waiting for transfers between devices, master_sum(): lax.all_to_all(spread, 'master', split_axis=0, concat_axis=0, tiled=True)  4.57 us
    all_to_all x1, starting transfers between devices, master_sum(): lax.all_to_all(spread, 'master', split_axis=0, concat_axis=0, tiled=True)  4.02 us
  transfers between devices with their start and end apart: 5, of which 3 were waited for; matrix products, arithmetic and copies ran while one was open for 19% of the time, Pallas kernels for 14%

profile of v12, /device:TPU:1, one launch (start us, length us, event | category | flops | bytes accessed | tf_op | source)
XLA Modules:
  0.0 129.7 jit_solution(18121895199427011032)
XLA Ops:
  7.2 0.0 copy-start.2
  7.2 0.0 copy-start.1
  7.2 0.0 copy-start
  7.2 0.0 copy-start.5
  7.2 0.0 all-gather.2.cloned.1.call-start
  7.3 0.7 all-gather.2.cloned.1.call-update
  7.9 1.1 fusion.10
  9.0 0.7 broadcast_in_dim.15
  9.7 11.5 %all-to-all-start = ((f32[128,4,128]{2,1,0:T(4,128)}), f32[128,4,128]{2,1,0:T(4,128)S(1)}, u32[]{:S(2)}, u32[]{:S(2)}) async-start(f32[128,4,128]{2,1,0:T(4,128)} %broadcast_in_dim.15), calls=%async_computation | async-start | bytes 524288 | tf_op jit(solution)/shard_map/all_to_all | solution.py:133
  21.2 0.7 compare_select_fusion.2
  21.9 0.7 bitcast_add_fusion.mreq_ref
  22.6 3.3 %gather_fusion = s32[512]{0:T(512)S(1)} fusion(s32[128]{0:T(128)S(1)} %bitcast_add_fusion.mreq_ref, s32[1024]{0:T(1024)S(1)} %pad_clamp_fusion.2), kind=kCustom, calls=%fused_computation | custom fusion | bytes 6144 | tf_op jit(solution)/shard_map/gather | solution.py:114
  26.0 0.7 broadcast_multiply_fusion
  26.6 1.1 fusion.19.w_ref
  27.7 0.9 fusion.20
  28.6 3.6 %all-to-all-done = f32[128,4,128]{2,1,0:T(4,128)S(1)} async-done(((f32[128,4,128]{2,1,0:T(4,128)}), f32[128,4,128]{2,1,0:T(4,128)S(1)}, u32[]{:S(2)}, u32[]{:S(2)}) %all-to-all-start) | async-done | bytes 262176 | tf_op jit(solution)/shard_map/all_to_all | solution.py:133
  32.3 1.0 gather_fusion.1
  33.3 0.9 fusion.17
  34.2 1.7 %fusion.1 = (f32[16,128]{1,0:T(8,128)S(1)}, f32[16,128]{1,0:T(8,128)S(1)}) fusion(bf16[16,128,128]{2,1,0:T(8,128)(2,1)} %slave_ref.1, f32[16,128]{1,0:T(8,128)S(1)} %fusion.20, f32[16,128]{1,0:T(8,128)S(1)} %fusion.17), kind=kLoop, calls=%fused_computation.11 | loop fusion | flops 1568768 | bytes 557056 | tf_op jit(solution)/shard_map/reduce_sum | solution.py:122
  35.8 0.7 broadcast_in_dim.17
  36.5 4.0 %all-to-all-start.1 = ((f32[8,2,16,128]{3,2,1,0:T(8,128)}), f32[8,2,16,128]{3,2,1,0:T(8,128)S(1)}, u32[]{:S(2)}, u32[]{:S(2)}) async-start(f32[8,2,16,128]{3,2,1,0:T(8,128)} %broadcast_in_dim.17), calls=%async_computation.1 | async-start | bytes 262144 | tf_op jit(solution)/shard_map/all_to_all | solution.py:76
  40.5 0.7 compare_select_fusion.1
  41.2 4.6 %all-to-all-done.1 = f32[8,2,16,128]{3,2,1,0:T(8,128)S(1)} async-done(((f32[8,2,16,128]{3,2,1,0:T(8,128)}), f32[8,2,16,128]{3,2,1,0:T(8,128)S(1)}, u32[]{:S(2)}, u32[]{:S(2)}) %all-to-all-start.1) | async-done | bytes 131104 | tf_op jit(solution)/shard_map/all_to_all | solution.py:76
  45.8 0.7 fusion.29
  46.6 1.4 %fusion.3 = f32[16,128]{1,0:T(8,128)S(1)} fusion(bf16[16,128,128]{2,1,0:T(8,128)(2,1)} %slave_ref.1, f32[16,128]{1,0:T(8,128)S(1)} %get-tuple-element.11), kind=kLoop, calls=%fused_computation.13 | loop fusion | flops 784384 | bytes 540672 | tf_op jit(solution)/shard_map/reduce_sum | solution.py:145
  48.0 1.0 gather_fusion.2
  49.0 1.1 fusion.7
  50.1 5.4 %all-to-all-start.2 = ((f32[128,4,128]{2,1,0:T(4,128)}), f32[128,4,128]{2,1,0:T(4,128)S(1)}, u32[]{:S(2)}, u32[]{:S(2)}) async-start(f32[128,4,128]{2,1,0:T(4,128)} %bitcast.8), calls=%async_computation.2 | async-start | bytes 524288 | tf_op jit(solution)/shard_map/all_to_all | solution.py:149
  55.6 1.2 fusion.30
  56.8 9.8 %all-to-all-done.2 = f32[128,4,128]{2,1,0:T(4,128)S(1)} async-done(((f32[128,4,128]{2,1,0:T(4,128)}), f32[128,4,128]{2,1,0:T(4,128)S(1)}, u32[]{:S(2)}, u32[]{:S(2)}) %all-to-all-start.2) | async-done | bytes 262176 | tf_op jit(solution)/shard_map/all_to_all | solution.py:149
  66.6 0.1 reduce_sum.113
  66.7 0.3 fusion.31
  67.1 18.1 %all_to_all.30 = f32[128,4,128]{2,1,0:T(4,128)S(1)} all-to-all(f32[128,4,128]{2,1,0:T(4,128)S(1)} %broadcast_in_dim.19), channel_id=1, replica_groups=mesh['slave'=16,'master'=8] {'slave','master'}, dimensions={0} | all-to-all | bytes 524288 | tf_op jit(solution)/shard_map/all_to_all | solution.py:133
  85.3 1.0 gather_fusion.3
  86.3 0.9 fusion.14
  87.2 0.0 copy-done
  87.2 0.3 fusion.4
  87.5 8.9 %all_to_all.31 = f32[8,16,128]{2,1,0:T(8,128)S(1)} all-to-all(f32[8,16,128]{2,1,0:T(8,128)S(1)} %broadcast_in_dim.20), channel_id=1, replica_groups=mesh['slave'=16,'master'=8] {'master'}, dimensions={0} | all-to-all | bytes 131072 | tf_op jit(solution)/shard_map/all_to_all | solution.py:76
  96.4 0.0 copy-done.5
  96.5 0.0 copy-start.4
  96.5 0.3 fusion.5
  96.8 1.0 gather_fusion.4
  97.9 1.1 fusion.6
  99.0 4.6 %all-to-all-start.5 = ((f32[128,4,128]{2,1,0:T(4,128)}), f32[128,4,128]{2,1,0:T(4,128)S(1)}, u32[]{:S(2)}, u32[]{:S(2)}) async-start(f32[128,4,128]{2,1,0:T(4,128)} %bitcast.14), calls=%async_computation.5 | async-start | bytes 524288 | tf_op jit(solution)/shard_map/all_to_all | solution.py:149
  103.6 0.0 copy-start.3
  103.6 0.0 copy-start.6
  103.6 0.0 all-gather.2.cloned.1.call-done.basis_hbm
  103.7 0.0 copy-done.2
  103.7 0.0 copy-done.1
  103.7 18.2 %shard_map.139 = bf16[512,128,128]{2,1,0:T(8,128)(2,1)} custom-call(s32[512]{0:T(512)S(1)} %copy-done.1, s32[512]{0:T(512)S(1)} %copy-done.2, s32[128]{0:T(128)S(1)} %bitcast_add_fusion.mreq_ref, bf16[16,128,128]{2,1,0:T(8,128)(2,1)S(1)} %copy-done, bf16[512,128,128]{2,1,0:T(8,128)(2,1)} %all-gather.2.cloned.1.call-done.basis_hbm, f32[512,128]{1,0:T(8,128)S(1)} %fusion.19.w_ref), custom_call_target="tpu_custom_call" | custom-call | flops 2147483648 | bytes 21233664 | tf_op jit(solution)/shard_map/pallas_call | solution.py:62
  121.9 0.0 copy-done.4
  121.9 0.0 all-to-all-done.5
  121.9 0.1 reduce_sum.118
  122.1 0.0 copy-done.3
  122.1 0.2 fusion.11
  122.3 0.0 copy-done.6
  122.3 0.6 multiply_subtract_fusion
  (11 shorter events, 0.1 us)
Async XLA Ops:
  7.2 96.5 %copy-start.2 = (s32[512]{0:T(512)S(1)}, s32[512]{0:T(512)}, u32[]{:S(2)}) copy-start(s32[512]{0:T(512)} %nidx_ref.1) | copy-start | bytes 6148
  7.2 96.5 %copy-start.1 = (s32[512]{0:T(512)S(1)}, s32[512]{0:T(512)}, u32[]{:S(2)}) copy-start(s32[512]{0:T(512)} %sidx_ref.1) | copy-start | bytes 6148
  7.2 80.0 %copy-start = (bf16[16,128,128]{2,1,0:T(8,128)(2,1)S(1)}, bf16[16,128,128]{2,1,0:T(8,128)(2,1)}, u32[]{:S(2)}) copy-start(bf16[16,128,128]{2,1,0:T(8,128)(2,1)} %slave_ref.1) | copy-start | bytes 1572868
  7.2 89.2 %copy-start.5 = (f32[16,128]{1,0:T(8,128)S(1)}, f32[16,128]{1,0:T(8,128)}, u32[]{:S(2)}) copy-start(f32[16,128]{1,0:T(8,128)} %param.14) | copy-start | bytes 24580
  7.2 96.4 %all-gather.2.cloned.1.call-start = ((), (), s32[]{:S(2)}) async-start(), calls=%async_computation.6 | async-start | bytes 16908288 | tf_op jit(solution)/shard_map/all_gather | solution.py:101
  9.7 22.5 %all-to-all-start = ((f32[128,4,128]{2,1,0:T(4,128)}), f32[128,4,128]{2,1,0:T(4,128)S(1)}, u32[]{:S(2)}, u32[]{:S(2)}) async-start(f32[128,4,128]{2,1,0:T(4,128)} %broadcast_in_dim.15), calls=%async_computation | async-start | bytes 524288 | tf_op jit(solution)/shard_map/all_to_all | solution.py:133
  36.5 9.3 %all-to-all-start.1 = ((f32[8,2,16,128]{3,2,1,0:T(8,128)}), f32[8,2,16,128]{3,2,1,0:T(8,128)S(1)}, u32[]{:S(2)}, u32[]{:S(2)}) async-start(f32[8,2,16,128]{3,2,1,0:T(8,128)} %broadcast_in_dim.17), calls=%async_computation.1 | async-start | bytes 262144 | tf_op jit(solution)/shard_map/all_to_all | solution.py:76
  50.1 16.5 %all-to-all-start.2 = ((f32[128,4,128]{2,1,0:T(4,128)}), f32[128,4,128]{2,1,0:T(4,128)S(1)}, u32[]{:S(2)}, u32[]{:S(2)}) async-start(f32[128,4,128]{2,1,0:T(4,128)} %bitcast.8), calls=%async_computation.2 | async-start | bytes 524288 | tf_op jit(solution)/shard_map/all_to_all | solution.py:149
  96.5 25.4 %copy-start.4 = (f32[16,128]{1,0:T(8,128)}, f32[16,128]{1,0:T(8,128)S(1)}, u32[]{:S(2)}) copy-start(f32[16,128]{1,0:T(8,128)S(1)} %subtract_select_fusion) | copy-start | bytes 24580
  99.0 22.9 %all-to-all-start.5 = ((f32[128,4,128]{2,1,0:T(4,128)}), f32[128,4,128]{2,1,0:T(4,128)S(1)}, u32[]{:S(2)}, u32[]{:S(2)}) async-start(f32[128,4,128]{2,1,0:T(4,128)} %bitcast.14), calls=%async_computation.5 | async-start | bytes 524288 | tf_op jit(solution)/shard_map/all_to_all | solution.py:149
  103.6 18.5 %copy-start.3 = (bf16[4,128,128]{2,1,0:T(8,128)(2,1)S(1)}, bf16[4,128,128]{2,1,0:T(8,128)(2,1)}, u32[]{:S(2)}) copy-start(bf16[4,128,128]{2,1,0:T(8,128)(2,1)} %param.13) | copy-start | bytes 393220
  103.6 18.7 %copy-start.6 = (f32[4,128]{1,0:T(4,128)S(1)}, f32[4,128]{1,0:T(4,128)}, u32[]{:S(2)}) copy-start(f32[4,128]{1,0:T(4,128)} %param.15) | copy-start | bytes 6148
Sparse Core Ops, SparseCore 0:
  11.2 87.2 all-gather.1

commit v13 on v11

--- a/solution.py
+++ b/solution.py
@@ -68,6 +68,40 @@
         ),
         cost_estimate=cost,
     )(pair_slave, pair_need, request, slave_basis, every_basis, weights)
+
+
+def couple_kernel(block_ref, proj_ref, w_ref, onehot_ref, basis_ref, out_ref, rows):
+    def gather(p, carry):
+        rows[pl.ds(p, 1), :] = proj_ref[pl.ds(block_ref[p], 1), :]
+        return carry
+
+    lax.fori_loop(0, rows.shape[0], gather, 0)
+    terms = rows[...] * w_ref[...]
+    summed = jnp.dot(
+        onehot_ref[...], terms, precision=lax.Precision.HIGHEST, preferred_element_type=jnp.float32
+    )
+    out_ref[...] = jnp.sum(basis_ref[...] * summed[:, None, :], axis=2)
+
+
+def couple(pair_block, proj, weights, onehot, basis):
+    grid_spec = pltpu.PrefetchScalarGridSpec(
+        num_scalar_prefetch=1,
+        grid=(1,),
+        in_specs=[
+            pl.BlockSpec(proj.shape, lambda i, b: (0, 0)),
+            pl.BlockSpec(weights.shape, lambda i, b: (0, 0)),
+            pl.BlockSpec(onehot.shape, lambda i, b: (0, 0)),
+            pl.BlockSpec(basis.shape, lambda i, b: (0, 0, 0)),
+        ],
+        out_specs=pl.BlockSpec(basis.shape[:2], lambda i, b: (0, 0)),
+        scratch_shapes=[pltpu.VMEM(weights.shape, jnp.float32)],
+    )
+    return pl.pallas_call(
+        couple_kernel,
+        grid_spec=grid_spec,
+        out_shape=jax.ShapeDtypeStruct(basis.shape[:2], jnp.float32),
+        compiler_params=pltpu.CompilerParams(vmem_limit_bytes=32 * 1024 * 1024),
+    )(pair_block, proj, weights, onehot, basis)
 
 
 def master_sum(x):
@@ -131,9 +165,9 @@
     for update in range(ITERS):
         outgoing_proj = jnp.broadcast_to(own_proj[None], (peers,) + own_proj.shape)
         returned = lax.all_to_all(outgoing_proj, everyone, split_axis=0, concat_axis=0, tiled=True)
-        pair_terms = weights * returned.reshape(mblocks, qpts)[pair_block]
-        slave_terms = jnp.dot(slave_onehot, pair_terms, precision=high)
-        partial_coupled = jnp.sum(slave_float * slave_terms[:, None, :], axis=2)
+        partial_coupled = couple(
+            pair_block, returned.reshape(mblocks, qpts), weights, slave_onehot, slave_float
+        )
         if update == 0:
             both = master_sum(jnp.stack([lump_part, partial_coupled]))
             root_lump = jnp.sqrt(1.0 + both[0])

time: 131 us -> 137 us (1.046)
  Pallas kernels: 18.2 us -> 26.5 us
  waiting for transfers between devices: 18.7 us -> 15.4 us
  other arithmetic: 10.5 us -> 13.5 us
  starting transfers between devices: 25.8 us -> 28.4 us
  local copies, waits for them, and re-layouts: 8.97 us -> 6.92 us
  matrix products: 6.85 us -> 5.07 us
    pallas_call x0 -> x2, Pallas kernels: none -> 8.23 us  [couple(): pl.pallas_call(couple_kernel, grid_spec=grid_spec, out_shape=jax.ShapeDty...]
    all_to_all x1, waiting for transfers between devices: 3.62 us -> 0.38 us  [on_device(): lax.all_to_all(outgoing_proj, everyone, split_axis=0, concat_axis=0, tile...]
    all_to_all x2, starting transfers between devices: 10.3 us -> 12.5 us  [on_device(): lax.all_to_all(outbound.reshape(peers, mb_dev, qpts), everyone, split_axi...]
    gather x2 -> x0, local copies, waits for them, and re-layouts: 2.06 us -> none  [on_device(): pair_terms = weights * returned.reshape(mblocks, qpts)[pair_block]]
    convert_element_type x0 -> x2, other arithmetic: none -> 1.83 us  [the longest x1 1.14 us: on_device(): slave_float = slave_basis.astype(jnp.float32)]
    dot_general x2 -> x0, matrix products: 1.79 us -> none  [on_device(): slave_terms = jnp.dot(slave_onehot, pair_terms, precision=high)]
  transfers between devices with their start and end apart: 5 -> 5, of which waited for: 3 -> 3; matrix products, arithmetic and copies ran while one was open for 19% -> 18% of each run, Pallas kernels for 14% -> 19%
where the time goes in v13:
time: 137 us
  starting transfers between devices  28.4 us (21%)
  Pallas kernels  26.5 us (19%)
  blocking collectives  26.5 us (19%)
  waiting for transfers between devices  15.4 us (11%)
  between operations  14.3 us (10%)
  other arithmetic  13.5 us (10%)
  local copies, waits for them, and re-layouts  6.92 us (5%)
  matrix products  5.07 us (4%)
    pallas_call x1, Pallas kernels, build_tiles(): pl.pallas_call(functools.partial(tile_kernel, group), grid_spec=grid_spec...  18.2 us
    all_to_all x1, blocking collectives, on_device(): lax.all_to_all(outgoing_proj, everyone, split_axis=0, concat_axis=0, tile...  18.1 us
    all_to_all x2, starting transfers between devices, on_device(): lax.all_to_all(outbound.reshape(peers, mb_dev, qpts), everyone, split_axi...  12.5 us
    all_to_all x1, starting transfers between devices, on_device(): lax.all_to_all(outgoing_proj, everyone, split_axis=0, concat_axis=0, tile...  11.5 us
    all_to_all x2, waiting for transfers between devices, on_device(): lax.all_to_all(outbound.reshape(peers, mb_dev, qpts), everyone, split_axi...  9.8 us
    all_to_all x1, blocking collectives, master_sum(): lax.all_to_all(spread, 'master', split_axis=0, concat_axis=0, tiled=True)  8.35 us
    pallas_call x2, Pallas kernels, couple(): pl.pallas_call(couple_kernel, grid_spec=grid_spec, out_shape=jax.ShapeDty...  8.23 us
    all_to_all x1, waiting for transfers between devices, master_sum(): lax.all_to_all(spread, 'master', split_axis=0, concat_axis=0, tiled=True)  4.55 us
  transfers between devices with their start and end apart: 5, of which 3 were waited for; matrix products, arithmetic and copies ran while one was open for 18% of the time, Pallas kernels for 19%

profile of v13, /device:TPU:1, one launch (start us, length us, event | category | flops | bytes accessed | tf_op | source)
XLA Modules:
  0.0 136.5 jit_solution(8998866514839616041)
XLA Ops:
  7.2 0.0 copy-start.1
  7.2 0.0 copy-start
  7.2 0.0 copy-start.2
  7.2 0.0 all-gather.2.cloned.1.call-start
  7.2 0.7 all-gather.2.cloned.1.call-update
  7.9 1.1 fusion.4
  9.0 0.7 broadcast_in_dim.16
  9.7 11.5 %all-to-all-start = ((f32[128,4,128]{2,1,0:T(4,128)}), f32[128,4,128]{2,1,0:T(4,128)S(1)}, u32[]{:S(2)}, u32[]{:S(2)}) async-start(f32[128,4,128]{2,1,0:T(4,128)} %broadcast_in_dim.16), calls=%async_computation | async-start | bytes 524288 | tf_op jit(solution)/shard_map/all_to_all | solution.py:167
  21.2 0.7 broadcast_multiply_fusion
  21.9 1.1 fusion.9.w_ref
  23.0 0.9 fusion.11
  23.9 1.4 %multiply_reduce_fusion.2 = f32[16,128]{1,0:T(8,128)S(1)} fusion(bf16[16,128,128]{2,1,0:T(8,128)(2,1)} %slave_ref.1, f32[16,128]{1,0:T(8,128)S(1)} %fusion.11), kind=kLoop, calls=%fused_computation.8 | loop fusion | flops 1046528 | bytes 540672 | tf_op jit(solution)/shard_map/reduce_sum | solution.py:156
  25.3 0.7 bitcast_add_fusion.mreq_ref
  26.0 0.7 compare_select_fusion.1
  26.7 1.1 convert_element_type.10.basis_ref
  27.8 3.3 %gather_fusion = s32[512]{0:T(512)S(1)} fusion(s32[128]{0:T(128)S(1)} %bitcast_add_fusion.mreq_ref, s32[1024]{0:T(1024)S(1)} %pad_clamp_fusion.1), kind=kCustom, calls=%fused_computation | custom fusion | bytes 6144 | tf_op jit(solution)/shard_map/gather | solution.py:148
  31.2 0.7 fusion.10.onehot_ref
  31.9 0.4 all-to-all-done
  32.2 4.1 %shard_map.139 = f32[16,128]{1,0:T(8,128)S(1)} custom-call(s32[512]{0:T(512)S(1)} %gather_fusion, f32[512,128]{1,0:T(8,128)S(1)} %bitcast.34, f32[512,128]{1,0:T(8,128)S(1)} %fusion.9.w_ref, f32[16,512]{1,0:T(8,128)S(1)} %fusion.10.onehot_ref, f32[16,128,128]{2,1,0:T(8,128)S(1)} %convert_element_type.10.basis_ref), custom_call_target="tpu_custom_call" | custom-call | tf_op jit(solution)/shard_map/pallas_call | solution.py:99
  36.4 0.7 broadcast_in_dim.17
  37.0 4.4 %all-to-all-start.1 = ((f32[8,2,16,128]{3,2,1,0:T(8,128)}), f32[8,2,16,128]{3,2,1,0:T(8,128)S(1)}, u32[]{:S(2)}, u32[]{:S(2)}) async-start(f32[8,2,16,128]{3,2,1,0:T(8,128)} %broadcast_in_dim.17), calls=%async_computation.1 | async-start | bytes 262144 | tf_op jit(solution)/shard_map/all_to_all | solution.py:110
  41.5 0.7 compare_select_fusion
  42.2 4.5 %all-to-all-done.1 = f32[8,2,16,128]{3,2,1,0:T(8,128)S(1)} async-done(((f32[8,2,16,128]{3,2,1,0:T(8,128)}), f32[8,2,16,128]{3,2,1,0:T(8,128)S(1)}, u32[]{:S(2)}, u32[]{:S(2)}) %all-to-all-start.1) | async-done | bytes 131104 | tf_op jit(solution)/shard_map/all_to_all | solution.py:110
  46.7 0.7 fusion.18
  47.5 1.4 %multiply_reduce_fusion.1 = f32[16,128]{1,0:T(8,128)S(1)} fusion(bf16[16,128,128]{2,1,0:T(8,128)(2,1)} %slave_ref.1, f32[16,128]{1,0:T(8,128)S(1)} %get-tuple-element.9), kind=kLoop, calls=%fused_computation.4 | loop fusion | flops 784384 | bytes 540672 | tf_op jit(solution)/shard_map/reduce_sum | solution.py:179
  48.9 1.0 gather_fusion.1
  49.9 1.3 fusion.1
  51.3 8.3 %all-to-all-start.2 = ((f32[128,4,128]{2,1,0:T(4,128)}), f32[128,4,128]{2,1,0:T(4,128)S(1)}, u32[]{:S(2)}, u32[]{:S(2)}) async-start(f32[128,4,128]{2,1,0:T(4,128)} %bitcast.6), calls=%async_computation.2 | async-start | bytes 524288 | tf_op jit(solution)/shard_map/all_to_all | solution.py:181
  59.5 1.2 fusion.19
  60.7 9.8 %all-to-all-done.2 = f32[128,4,128]{2,1,0:T(4,128)S(1)} async-done(((f32[128,4,128]{2,1,0:T(4,128)}), f32[128,4,128]{2,1,0:T(4,128)S(1)}, u32[]{:S(2)}, u32[]{:S(2)}) %all-to-all-start.2) | async-done | bytes 262176 | tf_op jit(solution)/shard_map/all_to_all | solution.py:181
  70.5 0.1 reduce_sum.94
  70.7 0.3 fusion.20
  71.1 18.1 %all_to_all.30 = f32[128,4,128]{2,1,0:T(4,128)S(1)} all-to-all(f32[128,4,128]{2,1,0:T(4,128)S(1)} %broadcast_in_dim.19), channel_id=1, replica_groups=mesh['slave'=16,'master'=8] {'slave','master'}, dimensions={0} | all-to-all | bytes 524288 | tf_op jit(solution)/shard_map/all_to_all | solution.py:167
  89.2 4.1 %shard_map.140 = f32[16,128]{1,0:T(8,128)S(1)} custom-call(s32[512]{0:T(512)S(1)} %gather_fusion, f32[512,128]{1,0:T(8,128)S(1)} %bitcast.35, f32[512,128]{1,0:T(8,128)S(1)} %fusion.9.w_ref, f32[16,512]{1,0:T(8,128)S(1)} %fusion.10.onehot_ref, f32[16,128,128]{2,1,0:T(8,128)S(1)} %convert_element_type.10.basis_ref), custom_call_target="tpu_custom_call" | custom-call | tf_op jit(solution)/shard_map/pallas_call | solution.py:99
  93.3 8.4 %all_to_all.31 = f32[8,16,128]{2,1,0:T(8,128)S(1)} all-to-all(f32[8,16,128]{2,1,0:T(8,128)S(1)} %broadcast_in_dim.20), channel_id=1, replica_groups=mesh['slave'=16,'master'=8] {'master'}, dimensions={0} | all-to-all | bytes 131072 | tf_op jit(solution)/shard_map/all_to_all | solution.py:110
  101.7 0.7 subtract_select_fusion
  102.4 0.0 copy-start.4
  102.4 1.4 %multiply_reduce_fusion = f32[16,128]{1,0:T(8,128)S(1)} fusion(bf16[16,128,128]{2,1,0:T(8,128)(2,1)} %slave_ref.1, f32[16,128]{1,0:T(8,128)S(1)} %subtract_select_fusion), kind=kLoop, calls=%fused_computation.3 | loop fusion | flops 784384 | bytes 540672 | tf_op jit(solution)/shard_map/reduce_sum | solution.py:179
  103.8 1.0 gather_fusion.2
  104.9 1.3 fusion
  106.2 4.2 %all-to-all-start.5 = ((f32[128,4,128]{2,1,0:T(4,128)}), f32[128,4,128]{2,1,0:T(4,128)S(1)}, u32[]{:S(2)}, u32[]{:S(2)}) async-start(f32[128,4,128]{2,1,0:T(4,128)} %bitcast.12), calls=%async_computation.5 | async-start | bytes 524288 | tf_op jit(solution)/shard_map/all_to_all | solution.py:181
  110.4 0.0 copy-start.3
  110.4 0.0 copy-start.5
  110.4 0.0 all-gather.2.cloned.1.call-done.basis_hbm
  110.5 0.0 copy-done.1
  110.5 0.0 copy-done
  110.5 0.0 copy-done.2
  110.5 18.2 %shard_map.141 = bf16[512,128,128]{2,1,0:T(8,128)(2,1)} custom-call(s32[512]{0:T(512)S(1)} %copy-done.1, s32[512]{0:T(512)S(1)} %copy-done.2, s32[128]{0:T(128)S(1)} %bitcast_add_fusion.mreq_ref, bf16[16,128,128]{2,1,0:T(8,128)(2,1)S(1)} %copy-done, bf16[512,128,128]{2,1,0:T(8,128)(2,1)} %all-gather.2.cloned.1.call-done.basis_hbm, f32[512,128]{1,0:T(8,128)S(1)} %fusion.9.w_ref), custom_call_target="tpu_custom_call" | custom-call | flops 2147483648 | bytes 21233664 | tf_op jit(solution)/shard_map/pallas_call | solution.py:62
  128.7 0.0 copy-done.4
  128.7 0.0 all-to-all-done.5
  128.7 0.1 reduce_sum.98
  128.9 0.0 copy-done.3
  128.9 0.2 fusion.5
  129.1 0.0 copy-done.5
  129.1 0.6 multiply_subtract_fusion
  (8 shorter events, 0.1 us)
Async XLA Ops:
  7.2 103.3 %copy-start.1 = (s32[512]{0:T(512)S(1)}, s32[512]{0:T(512)}, u32[]{:S(2)}) copy-start(s32[512]{0:T(512)} %sidx_ref.1) | copy-start | bytes 6148
  7.2 103.3 %copy-start = (bf16[16,128,128]{2,1,0:T(8,128)(2,1)S(1)}, bf16[16,128,128]{2,1,0:T(8,128)(2,1)}, u32[]{:S(2)}) copy-start(bf16[16,128,128]{2,1,0:T(8,128)(2,1)} %slave_ref.1) | copy-start | bytes 1572868
  7.2 103.3 %copy-start.2 = (s32[512]{0:T(512)S(1)}, s32[512]{0:T(512)}, u32[]{:S(2)}) copy-start(s32[512]{0:T(512)} %nidx_ref.1) | copy-start | bytes 6148
  7.2 103.2 %all-gather.2.cloned.1.call-start = ((), (), s32[]{:S(2)}) async-start(), calls=%async_computation.6 | async-start | bytes 16908288 | tf_op jit(solution)/shard_map/all_gather | solution.py:135
  9.7 22.5 %all-to-all-start = ((f32[128,4,128]{2,1,0:T(4,128)}), f32[128,4,128]{2,1,0:T(4,128)S(1)}, u32[]{:S(2)}, u32[]{:S(2)}) async-start(f32[128,4,128]{2,1,0:T(4,128)} %broadcast_in_dim.16), calls=%async_computation | async-start | bytes 524288 | tf_op jit(solution)/shard_map/all_to_all | solution.py:167
  37.0 9.7 %all-to-all-start.1 = ((f32[8,2,16,128]{3,2,1,0:T(8,128)}), f32[8,2,16,128]{3,2,1,0:T(8,128)S(1)}, u32[]{:S(2)}, u32[]{:S(2)}) async-start(f32[8,2,16,128]{3,2,1,0:T(8,128)} %broadcast_in_dim.17), calls=%async_computation.1 | async-start | bytes 262144 | tf_op jit(solution)/shard_map/all_to_all | solution.py:110
  51.3 19.3 %all-to-all-start.2 = ((f32[128,4,128]{2,1,0:T(4,128)}), f32[128,4,128]{2,1,0:T(4,128)S(1)}, u32[]{:S(2)}, u32[]{:S(2)}) async-start(f32[128,4,128]{2,1,0:T(4,128)} %bitcast.6), calls=%async_computation.2 | async-start | bytes 524288 | tf_op jit(solution)/shard_map/all_to_all | solution.py:181
  102.4 26.3 %copy-start.4 = (f32[16,128]{1,0:T(8,128)}, f32[16,128]{1,0:T(8,128)S(1)}, u32[]{:S(2)}) copy-start(f32[16,128]{1,0:T(8,128)S(1)} %subtract_select_fusion) | copy-start | bytes 24580
  106.2 22.5 %all-to-all-start.5 = ((f32[128,4,128]{2,1,0:T(4,128)}), f32[128,4,128]{2,1,0:T(4,128)S(1)}, u32[]{:S(2)}, u32[]{:S(2)}) async-start(f32[128,4,128]{2,1,0:T(4,128)} %bitcast.12), calls=%async_computation.5 | async-start | bytes 524288 | tf_op jit(solution)/shard_map/all_to_all | solution.py:181
  110.4 18.5 %copy-start.3 = (bf16[4,128,128]{2,1,0:T(8,128)(2,1)S(1)}, bf16[4,128,128]{2,1,0:T(8,128)(2,1)}, u32[]{:S(2)}) copy-start(bf16[4,128,128]{2,1,0:T(8,128)(2,1)} %param.13) | copy-start | bytes 393220
  110.4 18.7 %copy-start.5 = (f32[4,128]{1,0:T(4,128)S(1)}, f32[4,128]{1,0:T(4,128)}, u32[]{:S(2)}) copy-start(f32[4,128]{1,0:T(4,128)} %param.15) | copy-start | bytes 6148
Sparse Core Ops, SparseCore 0:
  11.2 86.5 all-gather.1
